TPU v7x, 32 devices: a whole 2x2x4 slice. The times are simulated.
32 devices in a mesh: seq: 8 (over y, x, core), head: 4 (over z).
Axes of the slice: x: 2, y: 2, z: 4, core: 2. Of those that a mesh axis runs over, the one named last changes fastest.
Arguments:
- queries: bfloat16 [4096, 4096], P('seq', 'head'), may hold values from -8 to 8
- keys: bfloat16 [4096, 4096], P('seq', 'head'), may hold values from -8 to 8
- values: bfloat16 [4096, 4096], P('seq', 'head'), may hold values from -6 to 6
- grad_normed: bfloat16 [4096, 4096], P('seq', 'head'), may hold values from -6 to 6
- docs: int32 [4096], P('seq'), may hold values from 0 to 3, as said below
Outputs:
- normed: bfloat16 [4096, 4096], P('seq', 'head')
- grad_queries: bfloat16 [4096, 4096], P('seq', 'head')
- grad_keys: bfloat16 [4096, 4096], P('seq', 'head')
- grad_values: bfloat16 [4096, 4096], P('seq', 'head')
Inputs may be any that keep to these rules, and one draw needn't show every extreme that they name: docs never falls along the sequence; each of the 4 documents is a run of 1 to 3072 tokens, one of exactly 3072.
All inputs are finite; a program needn't handle non-finite values.
Results may differ from a plain program's by a relative error of at most 0.01.
Values may be sent and summed in bfloat16 or wider, within the bound.
No kernel may reach another device: no remote copies, remote signals or barrier semaphores. Data moves between devices by JAX's collectives and lax.ppermute only.
A program may use at most 192 MiB of HBM per device.

v0:
```python
import functools
import math

import jax
import jax.numpy as jnp
from jax import lax
from jax.experimental import pallas as pl
from jax.experimental.pallas import tpu as pltpu
from jax.sharding import PartitionSpec as P

HEADS = 32
HEAD_DIM = 128


norm_eps = 1e-06

OFFSETS = (0, 1, 2, 4)
NEG = -1e30
F32 = jnp.float32
BF16 = jnp.bfloat16
VMEM_BYTES = 60 * 1024 * 1024


ORDER = (0, 1, 2, 4, 6, 3, 5, 7)
FIRST_USE = [max(t + off for off in OFFSETS if t + off < 8) for t in range(8)]


def find_bounds(ids, bounds):
    ids = ids[...].astype(F32)
    for d in range(3):
        count = jnp.sum(jnp.where(ids < d + 0.5, 1.0, 0.0))
        bounds[d] = count.astype(jnp.int32)


def doc_of(position, bounds):
    doc = jnp.int32(0)
    for d in range(3):
        doc = doc + (position >= bounds[d]).astype(jnp.int32)
    return doc


def reach(i, block, bounds):
    first, last = doc_of(i * block, bounds), doc_of(i * block + block - 1, bounds)

    def active(off):
        return (i >= off) & (first == doc_of((i - off + 1) * block - 1, bounds))

    def full(off):
        return doc_of((i - off) * block, bounds) == last

    near = 1 + active(1).astype(jnp.int32) + active(2).astype(jnp.int32)
    return near, active(4), full(2), full(4)


def pieces(i, near, far, block):
    found = []
    if far:
        found.append((0, (i - 4) * block, block, False))
    if near > 1:
        found.append(((4 - near) * block, (i - near + 1) * block, (near - 1) * block, False))
    found.append((3 * block, i * block, block, True))
    return [(row, pl.multiple_of(key, block), size, own) for row, key, size, own in found]


def slots_of(near, far):
    return ([0] if far else []) + list(range(4 - near, 4))


def for_each_reach(i, block, bounds, body, split_full):
    near, far, full2, full4 = reach(i, block, bounds)
    pl.when(near == 1)(functools.partial(body, 1, False, True))
    pl.when(near == 2)(functools.partial(body, 2, False, True))
    alone = (near == 3) & jnp.logical_not(far)
    if not split_full:
        pl.when(alone)(functools.partial(body, 3, False, True))
        pl.when(far)(functools.partial(body, 3, True, True))
        return
    pl.when(alone & full2)(functools.partial(body, 3, False, False))
    pl.when(alone & jnp.logical_not(full2))(functools.partial(body, 3, False, True))
    pl.when(far & full4)(functools.partial(body, 3, True, False))
    pl.when(far & jnp.logical_not(full4))(functools.partial(body, 3, True, True))


def each_slot(i, block, bounds, act):
    near, far, _, _ = reach(i, block, bounds)
    act(3)
    pl.when(near > 1)(lambda: act(2))
    pl.when(near > 2)(lambda: act(1))
    pl.when(far)(lambda: act(0))


def doc_starts(i, block, bounds):
    pos = i * block + lax.broadcasted_iota(jnp.int32, (1, block), 1)
    start = jnp.zeros((1, block), jnp.int32)
    for d in range(3):
        start = jnp.where(pos >= bounds[d], jnp.maximum(start, bounds[d]), start)
    return pos, start


def nt_dot(a, b):
    return lax.dot_general(a, b, (((1,), (1,)), ((), ())), preferred_element_type=F32)


def nn_dot(a, b):
    return lax.dot_general(a, b, (((1,), (0,)), ((), ())), preferred_element_type=F32)


def parts_in(ref, t, block, held, sems):
    return [
        pltpu.make_async_copy(
            ref.at[part * block : (part + 1) * block, :],
            held.at[part, pl.ds(pl.multiple_of(t * block, block), block), :],
            sems.at[part, t],
        )
        for part in range(3)
    ]


def forward_kernel(block, rank_ref, *refs):
    n = 8
    a_refs = refs[:n]
    prob_ref, out_t_ref, out_ref, inv_ref, square_ref, bounds = refs[n : n + 6]
    held, ids, val_t, prob, out_t_keep, out_keep = refs[n + 6 : n + 12]
    total, acc, sems, id_sems, prob_sems, out_sems = refs[n + 12 :]
    rank = rank_ref[0]

    def ids_in(m, ref):
        return pltpu.make_async_copy(ref.at[3 * block :, :], ids.at[rank ^ m], id_sems.at[m])

    for m, ref in zip(ORDER, a_refs):
        ids_in(m, ref).start()
    for m, ref in zip(ORDER, a_refs):
        for copy in parts_in(ref, rank ^ m, block, held, sems):
            copy.start()
    for m, ref in zip(ORDER, a_refs):
        ids_in(m, ref).wait()
    find_bounds(ids, bounds)

    gain = math.log2(math.e) / math.sqrt(HEAD_DIM)

    def prob_out(i, slot):
        rows = slice(slot * block, (slot + 1) * block)
        return pltpu.make_async_copy(
            prob.at[i, rows, :], prob_ref.at[i, rows, :], prob_sems.at[i, slot]
        )

    def rows_out(i):
        return (
            pltpu.make_async_copy(out_t_keep.at[i], out_t_ref.at[i], out_sems.at[0, i]),
            pltpu.make_async_copy(out_keep.at[i], out_ref.at[i], out_sems.at[1, i]),
        )

    def one_block(i, carry):
        own_rows = pl.ds(pl.multiple_of(i * block, block), block)
        for copy in parts_in(a_refs[0], i, block, held, sems):
            copy.wait()
        val_t[:, own_rows] = held[2, own_rows, :].T
        query = held[0, own_rows, :]
        q_pos, q_start = doc_starts(i, block, bounds)

        def body(near, far, masked):
            found = pieces(i, near, far, block)
            scores, top = [], None
            for row, key, size, own in found:
                s = nt_dot(held[1, pl.ds(key, size), :], query) * gain
                if masked or own:
                    k_pos = key + lax.broadcasted_iota(jnp.int32, (size, 1), 0)
                    if not masked:
                        keep = k_pos <= q_pos
                    elif own:
                        keep = (k_pos >= q_start) & (k_pos <= q_pos)
                    else:
                        keep = k_pos >= q_start
                    s = jnp.where(keep, s, NEG)
                scores.append(s)
                peak = jnp.max(s, axis=0, keepdims=True)
                top = peak if top is None else jnp.maximum(top, peak)
            for number, ((row, key, size, own), s) in enumerate(zip(found, scores)):
                p = jnp.exp2(s - top)
                line = jnp.sum(p, axis=0, keepdims=True)
                pb = p.astype(BF16)
                prob[i, row : row + size, :] = pb
                term = nn_dot(val_t[:, pl.ds(key, size)], pb)
                total[...] = line if number == 0 else total[...] + line
                acc[...] = term if number == 0 else acc[...] + term
            for slot in slots_of(near, far):
                prob_out(i, slot).start()

        for_each_reach(i, block, bounds, body, True)

        inv = 1.0 / total[...]
        out_t = acc[...] * inv
        out_t_keep[i] = out_t
        out_keep[i] = out_t.T.astype(BF16)
        inv_ref[i] = inv
        square_ref[i] = jnp.sum(out_t * out_t, axis=0, keepdims=True)
        for copy in rows_out(i):
            copy.start()
        return carry

    lax.fori_loop(0, n, one_block, 0)

    def finish(i, carry):
        each_slot(i, block, bounds, lambda slot: prob_out(i, slot).wait())
        for copy in rows_out(i):
            copy.wait()
        return carry

    lax.fori_loop(0, n, finish, 0)


def project_kernel(block, rank_ref, *refs):
    n = 8
    g_refs = refs[:n]
    out_ref, square_ref, stats_ref, held, sems = refs[n:]
    rank = rank_ref[0]
    copies = [
        pltpu.make_async_copy(ref, held.at[rank ^ m], sems.at[m]) for m, ref in zip(ORDER, g_refs)
    ]
    for copy in copies:
        copy.start()
    for copy in copies:
        copy.wait()
    ones = jnp.ones((16, HEAD_DIM), BF16)
    for t in range(n):
        x = held[t].astype(F32) * out_ref[t].astype(F32)
        high = x.astype(BF16)
        low = (x - high.astype(F32)).astype(BF16)
        cols = slice(t * block, (t + 1) * block)
        stats_ref[0:1, cols] = square_ref[t]
        stats_ref[1:2, cols] = (nt_dot(ones, high) + nt_dot(ones, low))[0:1]


def backward_kernel(block, rank_ref, bounds, *refs):
    n = 8
    a_refs, g_refs = refs[:n], refs[n : 2 * n]
    prob_ref, out_t_ref, inv_ref, stats_ref = refs[2 * n : 2 * n + 4]
    d_refs = refs[2 * n + 4 : 3 * n + 4]
    held, cot, key_t, prob, out_t_keep, stage, grad_k, grad_v, acc = refs[3 * n + 4 : 3 * n + 13]
    sems, g_sems, prob_sems, out_sems, d_sems = refs[3 * n + 13 :]
    rank = rank_ref[0]
    scale = 1.0 / math.sqrt(HEAD_DIM)
    width = HEADS * HEAD_DIM

    def cot_in(ref, t):
        return pltpu.make_async_copy(ref, cot.at[t], g_sems.at[t])

    def out_in(i):
        return pltpu.make_async_copy(out_t_ref.at[i], out_t_keep.at[i], out_sems.at[i])

    def prob_in(i, slot):
        rows = slice(slot * block, (slot + 1) * block)
        return pltpu.make_async_copy(
            prob_ref.at[i, rows, :], prob.at[i, rows, :], prob_sems.at[i, slot]
        )

    for m, ref in zip(ORDER, g_refs):
        cot_in(ref, rank ^ m).start()
    for m, ref in zip(ORDER, a_refs):
        for copy in parts_in(ref, rank ^ m, block, held, sems):
            copy.start()

    def fetch(step, carry):
        i = n - 1 - step
        out_in(i).start()
        each_slot(i, block, bounds, lambda slot: prob_in(i, slot).start())
        return carry

    lax.fori_loop(0, n, fetch, 0)
    grad_k[...] = jnp.zeros_like(grad_k)
    grad_v[...] = jnp.zeros_like(grad_v)

    def one_block(step, carry):
        i = n - 1 - step
        cot_in(g_refs[0], i).wait()
        out_in(i).wait()
        inv_rms = lax.rsqrt(stats_ref[i, 0:1, :] / width + norm_eps)
        coef = inv_rms * inv_rms * inv_rms * stats_ref[i, 1:2, :] / width
        out_t = out_t_keep[i]
        dattn_t = (inv_rms * cot[i].astype(F32).T - out_t * coef) * inv_ref[i]
        dattn_tb = dattn_t.astype(BF16)
        dattn_f = dattn_tb.astype(F32)
        delta = jnp.sum(dattn_f * out_t, axis=0, keepdims=True)
        dattn = dattn_f.T.astype(BF16)
        for first in sorted(set(FIRST_USE)):

            @pl.when(i == first)
            def _():
                for t in range(n):
                    if FIRST_USE[t] == first:
                        for copy in parts_in(a_refs[0], t, block, held, sems):
                            copy.wait()
                        cols = slice(t * block, (t + 1) * block)
                        key_t[:, cols] = held[1, cols, :].T

        own_rows = pl.ds(pl.multiple_of(i * block, block), block)
        query = held[0, own_rows, :]

        def body(near, far, masked):
            for slot in slots_of(near, far):
                prob_in(i, slot).wait()
            for number, (row, key, size, own) in enumerate(pieces(i, near, far, block)):
                rows = pl.ds(key, size)
                pb = prob[i, row : row + size, :]
                dprob = nn_dot(held[2, rows, :], dattn_tb)
                ds = (pb.astype(F32) * (dprob - delta)).astype(BF16)
                term = nn_dot(key_t[:, rows], ds)
                acc[...] = term if number == 0 else acc[...] + term
                grad_k[rows, :] += nn_dot(ds, query)
                grad_v[rows, :] += nn_dot(pb, dattn)

        for_each_reach(i, block, bounds, body, False)

        stage[i, 0:block, :] = (acc[...] * scale).T.astype(BF16)
        stage[i, block : 2 * block, :] = (grad_k[own_rows, :] * scale).astype(BF16)
        stage[i, 2 * block :, :] = grad_v[own_rows, :].astype(BF16)
        for m, ref in zip(ORDER, d_refs):

            @pl.when((rank ^ m) == i)
            def _():
                pltpu.make_async_copy(stage.at[i], ref, d_sems.at[m]).start()

        return carry

    lax.fori_loop(0, n, one_block, 0)
    for m, ref in zip(ORDER, d_refs):
        pltpu.make_async_copy(stage.at[0], ref, d_sems.at[m]).wait()


def pack_kernel(block, rank_ref, q_ref, k_ref, v_ref, g_ref, doc_ref, *refs):
    n = 8
    a_refs, g_refs, sems = refs[:n], refs[n : 2 * n], refs[2 * n]
    copies = []
    for index, m in enumerate(ORDER):
        cols = pl.ds(pl.multiple_of((rank_ref[0] ^ m) * HEAD_DIM, HEAD_DIM), HEAD_DIM)
        parts = [
            (q_ref.at[:, cols], a_refs[index].at[0:block, :]),
            (k_ref.at[:, cols], a_refs[index].at[block : 2 * block, :]),
            (v_ref.at[:, cols], a_refs[index].at[2 * block : 3 * block, :]),
            (g_ref.at[:, cols], g_refs[index]),
        ]
        for source, target in parts:
            copies.append(pltpu.make_async_copy(source, target, sems.at[len(copies)]))
    for copy in copies:
        copy.start()
    row = lax.broadcasted_iota(jnp.int32, (16, HEAD_DIM), 0)
    ids = jnp.full((16, HEAD_DIM), 4.0, F32)
    for k in range(block // HEAD_DIM):
        part = doc_ref[0:1, k * HEAD_DIM : (k + 1) * HEAD_DIM].astype(F32)
        ids = jnp.where(row == k, part, ids)
    for ref in a_refs:
        ref[3 * block :, :] = ids.astype(BF16)
    for copy in copies:
        copy.wait()


def unpack_kernel(block, rank_ref, *refs):
    n = 8
    d_refs, outs, sems = refs[:n], refs[n : n + 3], refs[n + 3]
    copies = []
    for m, ref in zip(ORDER, d_refs):
        cols = pl.ds(pl.multiple_of((rank_ref[0] ^ m) * HEAD_DIM, HEAD_DIM), HEAD_DIM)
        for part, out in enumerate(outs):
            rows = slice(part * block, (part + 1) * block)
            copies.append(
                pltpu.make_async_copy(ref.at[rows, :], out.at[:, cols], sems.at[len(copies)])
            )
    for copy in copies:
        copy.start()
    for copy in copies:
        copy.wait()


def normed_kernel(block, rank_ref, stats_ref, *refs):
    n = 8
    o_refs, out_ref = refs[:n], refs[n]
    inv_rms = lax.rsqrt(stats_ref[0, 0:1, :] / (HEADS * HEAD_DIM) + norm_eps)
    spread = jnp.broadcast_to(inv_rms, (HEAD_DIM, block)).T
    for m, ref in zip(ORDER, o_refs):
        cols = pl.ds(pl.multiple_of((rank_ref[0] ^ m) * HEAD_DIM, HEAD_DIM), HEAD_DIM)
        out_ref[:, cols] = (ref[...].astype(F32) * spread).astype(BF16)


SMEM_SPEC = pl.BlockSpec(memory_space=pltpu.SMEM)
ANY_SPEC = pl.BlockSpec(memory_space=pl.ANY)
VMEM_SPEC = pl.BlockSpec(memory_space=pltpu.VMEM)


def shape_of(shape, dtype):
    return jax.ShapeDtypeStruct(shape, dtype)


def swap(value, m):
    if m == 0:
        return value
    n = lax.axis_size("seq")
    return lax.ppermute(value, "seq", [(s, s ^ m) for s in range(n)])


def swap_all(parts):
    return [swap(part, m) for m, part in zip(ORDER, parts)]


def sum_everywhere(stats):
    stats = stats + swap(stats, 1)
    stats = stats + swap(stats, 2) + swap(stats, 4) + swap(stats, 6)
    heads = lax.axis_size("head")
    parts = [
        lax.ppermute(stats, "head", [(s, (s + d) % heads) for s in range(heads)])
        for d in range(1, heads)
    ]
    return functools.reduce(jnp.add, parts, stats)


def run_forward(rank, a, block):
    n = len(a)
    return pl.pallas_call(
        functools.partial(forward_kernel, block),
        out_shape=[
            shape_of((n, 4 * block, block), BF16),
            shape_of((n, HEAD_DIM, block), F32),
            shape_of((n, block, HEAD_DIM), BF16),
            shape_of((n, 1, block), F32),
            shape_of((n, 1, block), F32),
            shape_of((3,), jnp.int32),
        ],
        in_specs=[SMEM_SPEC] + [ANY_SPEC] * n,
        out_specs=[ANY_SPEC] * 3 + [VMEM_SPEC] * 2 + [SMEM_SPEC],
        scratch_shapes=[
            pltpu.VMEM((3, n * block, HEAD_DIM), BF16),
            pltpu.VMEM((n, 16, HEAD_DIM), BF16),
            pltpu.VMEM((HEAD_DIM, n * block), BF16),
            pltpu.VMEM((n, 4 * block, block), BF16),
            pltpu.VMEM((n, HEAD_DIM, block), F32),
            pltpu.VMEM((n, block, HEAD_DIM), BF16),
            pltpu.VMEM((1, block), F32),
            pltpu.VMEM((HEAD_DIM, block), F32),
            pltpu.SemaphoreType.DMA((3, n)),
            pltpu.SemaphoreType.DMA((n,)),
            pltpu.SemaphoreType.DMA((n, len(OFFSETS))),
            pltpu.SemaphoreType.DMA((2, n)),
        ],
        compiler_params=pltpu.CompilerParams(vmem_limit_bytes=VMEM_BYTES),
        name="forward",
    )(rank, *a)


def run_project(rank, g, out, square, block):
    n = len(g)
    return pl.pallas_call(
        functools.partial(project_kernel, block),
        out_shape=shape_of((2, n * block), F32),
        in_specs=[SMEM_SPEC] + [ANY_SPEC] * n + [VMEM_SPEC] * 2,
        out_specs=VMEM_SPEC,
        scratch_shapes=[
            pltpu.VMEM((n, block, HEAD_DIM), BF16),
            pltpu.SemaphoreType.DMA((n,)),
        ],
        compiler_params=pltpu.CompilerParams(vmem_limit_bytes=VMEM_BYTES),
        name="project",
    )(rank, *g, out, square)


def run_backward(rank, bounds, a, g, probs, out_t, inv_total, stats_by_block, block):
    n = len(a)
    return pl.pallas_call(
        functools.partial(backward_kernel, block),
        out_shape=[shape_of((3 * block, HEAD_DIM), BF16)] * n,
        in_specs=[SMEM_SPEC] * 2 + [ANY_SPEC] * (2 * n + 2) + [VMEM_SPEC] * 2,
        out_specs=[ANY_SPEC] * n,
        scratch_shapes=[
            pltpu.VMEM((3, n * block, HEAD_DIM), BF16),
            pltpu.VMEM((n, block, HEAD_DIM), BF16),
            pltpu.VMEM((HEAD_DIM, n * block), BF16),
            pltpu.VMEM((n, 4 * block, block), BF16),
            pltpu.VMEM((n, HEAD_DIM, block), F32),
            pltpu.VMEM((n, 3 * block, HEAD_DIM), BF16),
            pltpu.VMEM((n * block, HEAD_DIM), F32),
            pltpu.VMEM((n * block, HEAD_DIM), F32),
            pltpu.VMEM((HEAD_DIM, block), F32),
            pltpu.SemaphoreType.DMA((3, n)),
            pltpu.SemaphoreType.DMA((n,)),
            pltpu.SemaphoreType.DMA((n, len(OFFSETS))),
            pltpu.SemaphoreType.DMA((n,)),
            pltpu.SemaphoreType.DMA((n,)),
        ],
        compiler_params=pltpu.CompilerParams(vmem_limit_bytes=VMEM_BYTES),
        name="backward",
    )(rank, bounds, *a, *g, probs, out_t, inv_total, stats_by_block)


def core_test(rank, a, g, stats):
    block, n = 512, 8
    a = [a[m] for m in ORDER]
    g = [g[m] for m in ORDER]
    probs, out_t, out, inv_total, square, bounds = run_forward(rank, a, block)
    s = run_project(rank, g, out, square, block)
    by = stats.reshape(2, n, block).transpose(1, 0, 2)
    grads = run_backward(rank, bounds, a, g, probs, out_t, inv_total, by, block)
    grads = [grads[ORDER.index(m)] for m in range(n)]
    return [out, s, *grads]


def by_head(queries, keys, values, grad_normed, docs):
    block, width_dev = queries.shape
    n = width_dev // HEAD_DIM
    rank = lax.axis_index("seq").reshape(1).astype(jnp.int32)
    rows = 3 * block + 16
    params = pltpu.CompilerParams(vmem_limit_bytes=VMEM_BYTES)
    packed = pl.pallas_call(
        functools.partial(pack_kernel, block),
        out_shape=[shape_of((rows, HEAD_DIM), BF16)] * n + [shape_of((block, HEAD_DIM), BF16)] * n,
        in_specs=[SMEM_SPEC] + [ANY_SPEC] * 4 + [VMEM_SPEC],
        out_specs=[VMEM_SPEC] * (2 * n),
        scratch_shapes=[pltpu.SemaphoreType.DMA((4 * n,))],
        compiler_params=params,
        name="pack",
    )(rank, queries, keys, values, grad_normed, docs.reshape(1, block))
    a = swap_all(packed[:n])
    first, packed_g = lax.optimization_barrier((a[2], list(packed[n:])))
    a[2] = first
    g = swap_all(packed_g)

    probs, out_t, out, inv_total, square, bounds = run_forward(rank, a, block)
    stats = run_project(rank, g, out, square, block)
    stats = sum_everywhere(stats)

    home = swap_all(
        [lax.dynamic_index_in_dim(out, rank[0] ^ m, 0, keepdims=False) for m in ORDER]
    )
    home, stats = lax.optimization_barrier((home, stats))
    stats_by_block = stats.reshape(2, n, block).transpose(1, 0, 2)
    own_stats = lax.dynamic_slice_in_dim(stats_by_block, rank[0], 1, axis=0)
    normed = pl.pallas_call(
        functools.partial(normed_kernel, block),
        out_shape=shape_of((block, width_dev), BF16),
        in_specs=[SMEM_SPEC] + [VMEM_SPEC] * (n + 1),
        out_specs=VMEM_SPEC,
        compiler_params=params,
        name="normed",
    )(rank, own_stats, *home)

    grads = run_backward(rank, bounds, a, g, probs, out_t, inv_total, stats_by_block, block)
    back = swap_all(grads)
    grad_outs = pl.pallas_call(
        functools.partial(unpack_kernel, block),
        out_shape=[shape_of((block, width_dev), BF16)] * 3,
        in_specs=[SMEM_SPEC] + [ANY_SPEC] * n,
        out_specs=[VMEM_SPEC] * 3,
        scratch_shapes=[pltpu.SemaphoreType.DMA((3 * n,))],
        compiler_params=params,
        name="unpack",
    )(rank, *back)
    return (normed, *grad_outs)


def from_behind(value, axis, steps):
    count = lax.axis_size(axis)
    initial, last = (max(0, -steps), min(count, count - steps))
    return lax.ppermute(value, axis, [(source, source + steps) for source in range(initial, last)])


def allowed_pairs(all_docs, own_docs, query_pos, seq_rank, offset, block_len):
    key_start = (seq_rank - offset) * block_len
    key_pos = key_start + jnp.arange(block_len, dtype=jnp.int32)
    key_docs = lax.dynamic_slice_in_dim(all_docs, jnp.maximum(key_start, 0), block_len)
    return (
        (key_pos[None, :] >= 0)
        & (key_pos[None, :] <= query_pos[:, None])
        & (key_docs[None, :] == own_docs[:, None])
    )


def masked_scores(query_heads, source, allowed, score_scale):
    key_heads = source[0].reshape(query_heads.shape)
    scores = (
        jnp.einsum("qhd,khd->hqk", query_heads, key_heads, preferred_element_type=jnp.float32)
        * score_scale
    )
    return jnp.where(allowed[None], scores, -jnp.inf)


def by_block(queries, keys, values, grad_normed, docs):
    block_len, width_dev = queries.shape
    heads_dev = width_dev // HEAD_DIM
    width = HEADS * HEAD_DIM
    score_scale = 1.0 / math.sqrt(HEAD_DIM)
    seq_rank = lax.axis_index("seq")
    levels = lax.axis_size("seq").bit_length() - 1
    distances = [2**exponent for exponent in range(levels)]
    all_docs = lax.all_gather(docs, "seq", axis=0, tiled=True)
    query_pos = seq_rank * block_len + jnp.arange(block_len, dtype=jnp.int32)
    query_heads = queries.reshape(block_len, heads_dev, HEAD_DIM)
    key_value = jnp.stack([keys, values])
    fetched = [from_behind(key_value, "seq", offset) for offset in distances]
    offsets = [0] + distances
    sources = [key_value] + fetched
    masks = [
        allowed_pairs(all_docs, docs, query_pos, seq_rank, offset, block_len) for offset in offsets
    ]
    shape_heads = (block_len, heads_dev, HEAD_DIM)
    row_max = jnp.full((heads_dev, block_len), -jnp.inf, jnp.float32)
    row_sum = jnp.zeros((heads_dev, block_len), jnp.float32)
    for source, allowed in zip(sources, masks):

        def update_stats(state, source_kv, allowed_now):
            old_max, old_sum = state
            scores = masked_scores(query_heads, source_kv, allowed_now, score_scale)
            new_max = jnp.maximum(old_max, jnp.max(scores, axis=-1))
            new_sum = old_sum * jnp.exp(old_max - new_max) + jnp.sum(
                jnp.exp(scores - new_max[..., None]), axis=-1
            )
            return (new_max, new_sum)

        def keep_stats(state, source_kv, allowed_now):
            return state

        row_max, row_sum = lax.cond(
            jnp.any(allowed), update_stats, keep_stats, (row_max, row_sum), source, allowed
        )
    log_total = row_max + jnp.log(row_sum)
    attn = jnp.zeros(shape_heads, jnp.float32)
    for source, allowed in zip(sources, masks):

        def forward_term(source_kv, allowed_now):
            scores = masked_scores(query_heads, source_kv, allowed_now, score_scale)
            prob_round = jnp.exp(scores - log_total[..., None]).astype(jnp.bfloat16)
            value_heads = source_kv[1].reshape(shape_heads)
            return jnp.einsum(
                "hqk,khd->qhd", prob_round, value_heads, preferred_element_type=jnp.float32
            )

        def empty_term(source_kv, allowed_now):
            return jnp.zeros(shape_heads, jnp.float32)

        attn = attn + lax.cond(jnp.any(allowed), forward_term, empty_term, source, allowed)
    attn_flat = attn.reshape(block_len, width_dev)
    cotangent = grad_normed.astype(jnp.float32)
    square_local = jnp.sum(attn_flat * attn_flat, axis=-1)
    square_total = lax.psum(square_local, "head")
    inv_rms = lax.rsqrt(square_total / width + norm_eps)
    normed = (attn_flat * inv_rms[:, None]).astype(jnp.bfloat16)
    projection = lax.psum(jnp.sum(cotangent * attn_flat, axis=-1), "head")
    dattn = (
        inv_rms[:, None] * cotangent - attn_flat * (inv_rms**3 * projection / width)[:, None]
    ).astype(jnp.bfloat16)
    dattn_heads = dattn.reshape(shape_heads)
    row_delta = jnp.sum(dattn_heads.astype(jnp.float32) * attn, axis=-1).T
    grad_query = jnp.zeros(shape_heads, jnp.float32)
    partials = []
    for source, allowed in zip(sources, masks):

        def backward_term(source_kv, allowed_now):
            scores = masked_scores(query_heads, source_kv, allowed_now, score_scale)
            prob_exact = jnp.exp(scores - log_total[..., None])
            prob_round = prob_exact.astype(jnp.bfloat16)
            key_heads = source_kv[0].reshape(shape_heads)
            value_heads = source_kv[1].reshape(shape_heads)
            dprob = jnp.einsum(
                "qhd,khd->hqk", dattn_heads, value_heads, preferred_element_type=jnp.float32
            )
            dscore = (prob_exact * (dprob - row_delta[..., None]) * score_scale).astype(
                jnp.bfloat16
            )
            query_term = jnp.einsum(
                "hqk,khd->qhd", dscore, key_heads, preferred_element_type=jnp.float32
            )
            key_term = jnp.einsum(
                "hqk,qhd->khd", dscore, query_heads, preferred_element_type=jnp.float32
            )
            value_term = jnp.einsum(
                "hqk,qhd->khd", prob_round, dattn_heads, preferred_element_type=jnp.float32
            )
            return (
                query_term,
                jnp.stack(
                    [
                        key_term.reshape(block_len, width_dev),
                        value_term.reshape(block_len, width_dev),
                    ]
                ),
            )

        def empty_pair(source_kv, allowed_now):
            return (
                jnp.zeros(shape_heads, jnp.float32),
                jnp.zeros((2, block_len, width_dev), jnp.float32),
            )

        query_term, pair_term = lax.cond(
            jnp.any(allowed), backward_term, empty_pair, source, allowed
        )
        grad_query = grad_query + query_term
        partials.append(pair_term)
    local_term = partials[0]
    far_terms = partials[1:]
    summed = local_term
    for offset, addend in zip(distances, far_terms):
        summed = summed + from_behind(addend.astype(jnp.bfloat16), "seq", -offset).astype(
            addend.dtype
        )
    grad_queries = grad_query.reshape(block_len, width_dev).astype(jnp.bfloat16)
    return (normed, grad_queries, summed[0].astype(jnp.bfloat16), summed[1].astype(jnp.bfloat16))


def body(queries, *others):
    block_len, width_dev = queries.shape
    if lax.axis_size("seq") == 8 and width_dev == 8 * HEAD_DIM and block_len == 512:
        return by_head(queries, *others)
    return by_block(queries, *others)


def solution(mesh):
    placed = (P("seq", "head"), P("seq", "head"), P("seq", "head"), P("seq", "head"), P("seq"))
    return jax.shard_map(
        body,
        mesh=mesh,
        in_specs=placed,
        out_specs=(P("seq", "head"), P("seq", "head"), P("seq", "head"), P("seq", "head")),
        check_vma=False,
    )
```

profile of v0, /device:TPU:0, one launch (start us, length us, event | category | flops | bytes accessed | tf_op | source)
XLA Modules:
  0.0 163.2 jit_solution(13566135886823996064)
XLA Ops:
  0.6 5.3 %pack.1 = (bf16[1552,128]{1,0:T(8,128)(2,1)}, bf16[1552,128]{1,0:T(8,128)(2,1)}, bf16[1552,128]{1,0:T(8,128)(2,1)}, bf16[1552,128]{1,0:T(8,128)(2,1)}, bf16[1552...) custom-call(s32[1]{0:T(128)} %bitcast.rank_ref, ...), custom_call_target="tpu_custom_call" | custom-call | tf_op jit(solution)/shard_map/pack/pallas_call | solution.py:510
  6.0 0.5 collective-permute-start
  6.5 2.6 %collective-permute-start.1 = (bf16[1552,128]{1,0:T(8,128)(2,1)}, bf16[1552,128]{1,0:T(8,128)(2,1)S(1)}, u32[]{:S(2)}, u32[]{:S(2)}) collective-permute-start(bf16[1552,128]{1,0:T(8,128)(2,1)} %get-tuple-element.57), channel_id=1, source_target_pairs={{0,8},{4,12},{8,0},{12,4},{16,24},{20,28},{24,16},{28,20},{1,9},{5... | collective-permute-start | bytes 1191944 | tf_op jit(solution)/shard_map/ppermute | solution.py:397
  9.1 1.5 collective-permute-start.2
  10.6 1.1 collective-permute-start.4
  11.8 2.0 %collective-permute-start.5 = (bf16[1552,128]{1,0:T(8,128)(2,1)}, bf16[1552,128]{1,0:T(8,128)(2,1)S(1)}, u32[]{:S(2)}, u32[]{:S(2)}) collective-permute-start(bf16[1552,128]{1,0:T(8,128)(2,1)} %get-tuple-element.70), channel_id=1, source_target_pairs={{0,20},{4,16},{8,28},{12,24},{16,4},{20,0},{24,12},{28,8},{1,21},{... | collective-permute-start | bytes 1191944 | tf_op jit(solution)/shard_map/ppermute | solution.py:397
  13.8 5.5 %collective-permute-done.1.refs_2_ = bf16[1552,128]{1,0:T(8,128)(2,1)S(1)} collective-permute-done((bf16[1552,128]{1,0:T(8,128)(2,1)}, bf16[1552,128]{1,0:T(8,128)(2,1)S(1)}, u32[]{:S(2)}, u32[]{:S(2)}) %collective-permute-start.1) | collective-permute-done | bytes 397344 | tf_op jit(solution)/shard_map/ppermute | solution.py:397
  19.3 1.7 %collective-permute-start.6 = (bf16[1552,128]{1,0:T(8,128)(2,1)}, bf16[1552,128]{1,0:T(8,128)(2,1)S(1)}, u32[]{:S(2)}, u32[]{:S(2)}) collective-permute-start(bf16[1552,128]{1,0:T(8,128)(2,1)} %get-tuple-element.71), channel_id=1, source_target_pairs={{0,28},{4,24},{8,20},{12,16},{16,12},{20,8},{24,4},{28,0},{1,29},{... | collective-permute-start | bytes 1191944 | tf_op jit(solution)/shard_map/ppermute | solution.py:397
  21.1 8.8 %collective-permute-done.2.refs_3_ = bf16[1552,128]{1,0:T(8,128)(2,1)S(1)} collective-permute-done((bf16[1552,128]{1,0:T(8,128)(2,1)}, bf16[1552,128]{1,0:T(8,128)(2,1)S(1)}, u32[]{:S(2)}, u32[]{:S(2)}) %collective-permute-start.2) | collective-permute-done | bytes 397344 | tf_op jit(solution)/shard_map/ppermute | solution.py:397
  29.9 0.9 collective-permute-start.15
  30.8 5.2 %collective-permute-done.4.refs_5_ = bf16[1552,128]{1,0:T(8,128)(2,1)S(1)} collective-permute-done((bf16[1552,128]{1,0:T(8,128)(2,1)}, bf16[1552,128]{1,0:T(8,128)(2,1)S(1)}, u32[]{:S(2)}, u32[]{:S(2)}) %collective-permute-start.4) | collective-permute-done | bytes 397344 | tf_op jit(solution)/shard_map/ppermute | solution.py:397
  36.0 1.5 collective-permute-start.16
  37.5 8.5 %collective-permute-done.5.refs_6_ = bf16[1552,128]{1,0:T(8,128)(2,1)S(1)} collective-permute-done((bf16[1552,128]{1,0:T(8,128)(2,1)}, bf16[1552,128]{1,0:T(8,128)(2,1)S(1)}, u32[]{:S(2)}, u32[]{:S(2)}) %collective-permute-start.5) | collective-permute-done | bytes 397344 | tf_op jit(solution)/shard_map/ppermute | solution.py:397
  46.0 3.3 %collective-permute-start.18 = (bf16[512,128]{1,0:T(8,128)(2,1)}, bf16[512,128]{1,0:T(8,128)(2,1)S(1)}, u32[]{:S(2)}, u32[]{:S(2)}) collective-permute-start(bf16[512,128]{1,0:T(8,128)(2,1)} %get-tuple-element.78), channel_id=1, source_target_pairs={{0,12},{4,8},{8,4},{12,0},{16,28},{20,24},{24,20},{28,16},{1,13},{... | collective-permute-start | bytes 393224 | tf_op jit(solution)/shard_map/ppermute | solution.py:397
  49.3 0.6 collective-permute-start.20
  50.0 17.4 %forward.1 = (bf16[8,2048,512]{2,1,0:T(8,128)(2,1)}, f32[8,128,512]{2,1,0:T(8,128)}, bf16[8,512,128]{2,1,0:T(8,128)(2,1)}, f32[8,1,512]{2,1,0:T(1,128)}, f32[8,1,512]{2,1,0:T(1,128)}, /*index=5*/s32[3]{0:T(128)}) custom-call(s32[1]{0:T(128)} %bitcast.rank_ref, bf16[1552,128]{1,0:T(8,128)(2,1)} %get-tuple-element.55.refs_0_, bf16[1552,128]{1,0:T(8,128)(2,1)} %copy-done, ...), custom_call_target="tpu_custom_call" | custom-call | tf_op jit(solution)/shard_map/forward/pallas_call | solution.py:417
  67.5 0.6 copy-done.9
  68.3 3.9 %project.1 = f32[2,4096]{1,0:T(2,128)} custom-call(s32[1]{0:T(128)} %bitcast.rank_ref, bf16[512,128]{1,0:T(8,128)(2,1)} %get-tuple-element.73.refs_0_.refs_8_, bf16[512,128]{1,0:T(8,128)(2,1)} %copy-done.7, bf16[512,128]{1,0:T(8,128)(2,1)} %copy-done.8, bf16[512,128]{1,0:T(8,128)(2,1)} %copy-done.9, bf16[512,128]{1,0:T(8,128)(2,1)} %copy-done.10, ...), custom_call_target="tpu_custom_call" | custom-call | tf_op jit(solution)/shard_map/project/pallas_call | solution.py:450
  72.1 1.1 collective-permute-start.21
  73.2 1.1 collective-permute-done.21
  74.3 0.8 add.55
  75.1 1.6 collective-permute-start.24
  76.7 1.8 %collective-permute-start.23 = (f32[2,4096]{1,0:T(2,128)S(1)}, f32[2,4096]{1,0:T(2,128)S(1)}, u32[]{:S(2)}, u32[]{:S(2)}) collective-permute-start(f32[2,4096]{1,0:T(2,128)S(1)} %add.55), channel_id=1, source_target_pairs={{0,16},{4,20},{8,24},{12,28},{16,0},{20,4},{24,8},{28,12},{1,17},{... | collective-permute-start | bytes 98312 | tf_op jit(solution)/shard_map/ppermute | solution.py:397
  78.6 2.0 %dynamic-slice_bitcast_fusion = (bf16[512,128]{1,0:T(8,128)(2,1)S(1)}, bf16[512,128]{1,0:T(8,128)(2,1)S(1)}, bf16[512,128]{1,0:T(8,128)(2,1)S(1)}, bf16[512,128]...) fusion(bf16[8,512,128]{2,1,0:T(8,128)(2,1)} %get-tuple-element., ...), kind=kLoop, calls=%fused_computation | loop fusion | bytes 2097184 | tf_op jit(solution)/shard_map/jit(dynamic_index_in_dim)/squeeze | solution.py:529
  80.7 1.9 %collective-permute-start.8 = (bf16[512,128]{1,0:T(8,128)(2,1)S(1)}, bf16[512,128]{1,0:T(8,128)(2,1)S(1)}, u32[]{:S(2)}, u32[]{:S(2)}) collective-permute-start(bf16[512,128]{1,0:T(8,128)(2,1)S(1)} %get-tuple-element.111), channel_id=1, source_target_pairs={{0,8},{4,12},{8,0},{12,4},{16,24},{20,28},{24,16},{28,20},{1,9},{5... | collective-permute-start | bytes 393224 | tf_op jit(solution)/shard_map/ppermute | solution.py:397
  82.6 3.8 %collective-permute-start.27 = (f32[2,4096]{1,0:T(2,128)S(1)}, f32[2,4096]{1,0:T(2,128)S(1)}, u32[]{:S(2)}, u32[]{:S(2)}) collective-permute-start(f32[2,4096]{1,0:T(2,128)S(1)} %add_add_fusion.1), channel_id=1, source_target_pairs={{0,3},{1,0},{2,1},{3,2},{4,7},{5,4},{6,5},{7,6},{8,11},{9,8},{10,9... | collective-permute-start | bytes 98312 | tf_op jit(solution)/shard_map/ppermute | solution.py:409
  86.4 1.0 collective-permute-start.25
  87.7 1.4 collective-permute-start.10
  89.1 0.3 collective-permute-start.11
  89.4 2.1 %collective-permute-done.26 = f32[2,4096]{1,0:T(2,128)S(1)} collective-permute-done((f32[2,4096]{1,0:T(2,128)S(1)}, f32[2,4096]{1,0:T(2,128)S(1)}, u32[]{:S(2)}, u32[]{:S(2)}) %collective-permute-start.26) | collective-permute-done | bytes 32800 | tf_op jit(solution)/shard_map/ppermute | solution.py:409
  91.5 0.7 collective-permute-done.25
  92.2 0.8 collective-permute-start.13
  93.0 0.6 add_add_fusion
  93.6 1.9 %collective-permute-done.9.refs_3_ = bf16[512,128]{1,0:T(8,128)(2,1)S(1)} collective-permute-done((bf16[512,128]{1,0:T(8,128)(2,1)S(1)}, bf16[512,128]{1,0:T(8,128)(2,1)S(1)}, u32[]{:S(2)}, u32[]{:S(2)}) %collective-permute-start.9) | collective-permute-done | bytes 131104 | tf_op jit(solution)/shard_map/ppermute | solution.py:397
  95.5 4.8 %collective-permute-done.12.refs_6_ = bf16[512,128]{1,0:T(8,128)(2,1)S(1)} collective-permute-done((bf16[512,128]{1,0:T(8,128)(2,1)S(1)}, bf16[512,128]{1,0:T(8,128)(2,1)S(1)}, u32[]{:S(2)}, u32[]{:S(2)}) %collective-permute-start.12) | collective-permute-done | bytes 131104 | tf_op jit(solution)/shard_map/ppermute | solution.py:397
  100.3 21.2 %backward.1 = (bf16[1536,128]{1,0:T(8,128)(2,1)}, bf16[1536,128]{1,0:T(8,128)(2,1)}, bf16[1536,128]{1,0:T(8,128)(2,1)}, bf16[1536,128]{1,0:T(8,128)(2,1)}, bf16[...) custom-call(s32[1]{0:T(128)} %bitcast.rank_ref, ...), custom_call_target="tpu_custom_call" | custom-call | tf_op jit(solution)/shard_map/backward/pallas_call | solution.py:466
  121.8 0.4 collective-permute-start.29
  122.2 0.7 collective-permute-start.30
  122.9 2.4 %collective-permute-start.31 = (bf16[1536,128]{1,0:T(8,128)(2,1)}, bf16[1536,128]{1,0:T(8,128)(2,1)S(1)}, u32[]{:S(2)}, u32[]{:S(2)}) collective-permute-start(bf16[1536,128]{1,0:T(8,128)(2,1)} %get-tuple-element.99), channel_id=1, source_target_pairs={{0,24},{4,28},{8,16},{12,20},{16,8},{20,12},{24,0},{28,4},{1,25},{... | collective-permute-start | bytes 1179656 | tf_op jit(solution)/shard_map/ppermute | solution.py:397
  125.3 0.8 collective-permute-start.33
  126.1 7.8 %collective-permute-done.29.refs_2_ = bf16[1536,128]{1,0:T(8,128)(2,1)S(1)} collective-permute-done((bf16[1536,128]{1,0:T(8,128)(2,1)}, bf16[1536,128]{1,0:T(8,128)(2,1)S(1)}, u32[]{:S(2)}, u32[]{:S(2)}) %collective-permute-start.29) | collective-permute-done | bytes 393248 | tf_op jit(solution)/shard_map/ppermute | solution.py:397
  133.9 1.3 dynamic-slice_bitcast_fusion.8.stats_ref
  135.2 2.7 %normed.1 = bf16[512,1024]{1,0:T(8,128)(2,1)} custom-call(s32[1]{0:T(128)} %bitcast.rank_ref, f32[1,2,512]{2,1,0:T(2,128)} %dynamic-slice_bitcast_fusion.8.stats_ref, bf16[512,128]{1,0:T(8,128)(2,1)} %get-tuple-element.83.refs_0_, bf16[512,128]{1,0:T(8,128)(2,1)} %copy-done.21, bf16[512,128]{1,0:T(8,128)(2,1)} %copy-done.22, bf16[512,128]{1,0:T(8,128)(2,1)} %copy-done.23, ...), custom_call_target="tpu_custom_call" | custom-call | tf_op jit(solution)/shard_map/normed/pallas_call | solution.py:534
  138.0 4.8 %collective-permute-done.30.refs_3_ = bf16[1536,128]{1,0:T(8,128)(2,1)S(1)} collective-permute-done((bf16[1536,128]{1,0:T(8,128)(2,1)}, bf16[1536,128]{1,0:T(8,128)(2,1)S(1)}, u32[]{:S(2)}, u32[]{:S(2)}) %collective-permute-start.30) | collective-permute-done | bytes 393248 | tf_op jit(solution)/shard_map/ppermute | solution.py:397
  142.8 6.8 %collective-permute-done.32.refs_5_ = bf16[1536,128]{1,0:T(8,128)(2,1)S(1)} collective-permute-done((bf16[1536,128]{1,0:T(8,128)(2,1)}, bf16[1536,128]{1,0:T(8,128)(2,1)S(1)}, u32[]{:S(2)}, u32[]{:S(2)}) %collective-permute-start.32) | collective-permute-done | bytes 393248 | tf_op jit(solution)/shard_map/ppermute | solution.py:397
  149.6 8.9 %collective-permute-done.34.refs_7_ = bf16[1536,128]{1,0:T(8,128)(2,1)S(1)} collective-permute-done((bf16[1536,128]{1,0:T(8,128)(2,1)}, bf16[1536,128]{1,0:T(8,128)(2,1)S(1)}, u32[]{:S(2)}, u32[]{:S(2)}) %collective-permute-start.34) | collective-permute-done | bytes 393248 | tf_op jit(solution)/shard_map/ppermute | solution.py:397
  158.6 0.7 copy-done.20
  159.3 3.8 %unpack.1 = (bf16[512,1024]{1,0:T(8,128)(2,1)}, bf16[512,1024]{1,0:T(8,128)(2,1)}, bf16[512,1024]{1,0:T(8,128)(2,1)}) custom-call(s32[1]{0:T(128)} %bitcast.rank_ref, bf16[1536,128]{1,0:T(8,128)(2,1)} %get-tuple-element.95.refs_0_, bf16[1536,128]{1,0:T(8,128)(2,1)} %copy-done.14, bf16[1536,128]{1,0:T(8,128)(2,1)} %copy-done.15, ...), custom_call_target="tpu_custom_call" | custom-call | tf_op jit(solution)/shard_map/unpack/pallas_call | solution.py:545
  (89 shorter events, 1.0 us)
Async XLA Ops:
  6.0 5.8 %collective-permute-start = (bf16[1552,128]{1,0:T(8,128)(2,1)}, bf16[1552,128]{1,0:T(8,128)(2,1)S(1)}, u32[]{:S(2)}, u32[]{:S(2)}) collective-permute-start(bf16[1552,128]{1,0:T(8,128)(2,1)} %get-tuple-element.56), channel_id=1, source_target_pairs={{0,4},{4,0},{8,12},{12,8},{16,20},{20,16},{24,28},{28,24},{1,5},{5... | collective-permute-start | bytes 1191944 | tf_op jit(solution)/shard_map/ppermute | solution.py:397
  6.5 12.8 %collective-permute-start.1 = (bf16[1552,128]{1,0:T(8,128)(2,1)}, bf16[1552,128]{1,0:T(8,128)(2,1)S(1)}, u32[]{:S(2)}, u32[]{:S(2)}) collective-permute-start(bf16[1552,128]{1,0:T(8,128)(2,1)} %get-tuple-element.57), channel_id=1, source_target_pairs={{0,8},{4,12},{8,0},{12,4},{16,24},{20,28},{24,16},{28,20},{1,9},{5... | collective-permute-start | bytes 1191944 | tf_op jit(solution)/shard_map/ppermute | solution.py:397
  9.1 20.8 %collective-permute-start.2 = (bf16[1552,128]{1,0:T(8,128)(2,1)}, bf16[1552,128]{1,0:T(8,128)(2,1)S(1)}, u32[]{:S(2)}, u32[]{:S(2)}) collective-permute-start(bf16[1552,128]{1,0:T(8,128)(2,1)} %get-tuple-element.67), channel_id=1, source_target_pairs={{0,16},{4,20},{8,24},{12,28},{16,0},{20,4},{24,8},{28,12},{1,17},{... | collective-permute-start | bytes 1191944 | tf_op jit(solution)/shard_map/ppermute | solution.py:397
  10.6 19.3 %collective-permute-start.3 = (bf16[1552,128]{1,0:T(8,128)(2,1)}, bf16[1552,128]{1,0:T(8,128)(2,1)S(1)}, u32[]{:S(2)}, u32[]{:S(2)}) collective-permute-start(bf16[1552,128]{1,0:T(8,128)(2,1)} %get-tuple-element.68), channel_id=1, source_target_pairs={{0,24},{4,28},{8,16},{12,20},{16,8},{20,12},{24,0},{28,4},{1,25},{... | collective-permute-start | bytes 1191944 | tf_op jit(solution)/shard_map/ppermute | solution.py:397
  10.6 25.4 %collective-permute-start.4 = (bf16[1552,128]{1,0:T(8,128)(2,1)}, bf16[1552,128]{1,0:T(8,128)(2,1)S(1)}, u32[]{:S(2)}, u32[]{:S(2)}) collective-permute-start(bf16[1552,128]{1,0:T(8,128)(2,1)} %get-tuple-element.69), channel_id=1, source_target_pairs={{0,12},{4,8},{8,4},{12,0},{16,28},{20,24},{24,20},{28,16},{1,13},{... | collective-permute-start | bytes 1191944 | tf_op jit(solution)/shard_map/ppermute | solution.py:397
  11.8 38.2 %copy-start = (bf16[1552,128]{1,0:T(8,128)(2,1)}, bf16[1552,128]{1,0:T(8,128)(2,1)S(1)}, u32[]{:S(2)}) copy-start(bf16[1552,128]{1,0:T(8,128)(2,1)S(1)} %collective-permute-done.refs_1_) | copy-start | bytes 1191940
  11.8 34.2 %collective-permute-start.5 = (bf16[1552,128]{1,0:T(8,128)(2,1)}, bf16[1552,128]{1,0:T(8,128)(2,1)S(1)}, u32[]{:S(2)}, u32[]{:S(2)}) collective-permute-start(bf16[1552,128]{1,0:T(8,128)(2,1)} %get-tuple-element.70), channel_id=1, source_target_pairs={{0,20},{4,16},{8,28},{12,24},{16,4},{20,0},{24,12},{28,8},{1,21},{... | collective-permute-start | bytes 1191944 | tf_op jit(solution)/shard_map/ppermute | solution.py:397
  19.3 30.6 %copy-start.1 = (bf16[1552,128]{1,0:T(8,128)(2,1)}, bf16[1552,128]{1,0:T(8,128)(2,1)S(1)}, u32[]{:S(2)}) copy-start(bf16[1552,128]{1,0:T(8,128)(2,1)S(1)} %collective-permute-done.1.refs_2_) | copy-start | bytes 1191940
  19.3 26.7 %collective-permute-start.6 = (bf16[1552,128]{1,0:T(8,128)(2,1)}, bf16[1552,128]{1,0:T(8,128)(2,1)S(1)}, u32[]{:S(2)}, u32[]{:S(2)}) collective-permute-start(bf16[1552,128]{1,0:T(8,128)(2,1)} %get-tuple-element.71), channel_id=1, source_target_pairs={{0,28},{4,24},{8,20},{12,16},{16,12},{20,8},{24,4},{28,0},{1,29},{... | collective-permute-start | bytes 1191944 | tf_op jit(solution)/shard_map/ppermute | solution.py:397
  29.8 20.1 %copy-start.2 = (bf16[1552,128]{1,0:T(8,128)(2,1)}, bf16[1552,128]{1,0:T(8,128)(2,1)S(1)}, u32[]{:S(2)}) copy-start(bf16[1552,128]{1,0:T(8,128)(2,1)S(1)} %collective-permute-done.2.refs_3_) | copy-start | bytes 1191940
  29.8 19.5 %collective-permute-start.14 = (bf16[512,128]{1,0:T(8,128)(2,1)}, bf16[512,128]{1,0:T(8,128)(2,1)S(1)}, u32[]{:S(2)}, u32[]{:S(2)}) collective-permute-start(bf16[512,128]{1,0:T(8,128)(2,1)} %get-tuple-element.74), channel_id=1, source_target_pairs={{0,4},{4,0},{8,12},{12,8},{16,20},{20,16},{24,28},{28,24},{1,5},{5... | collective-permute-start | bytes 393224 | tf_op jit(solution)/shard_map/ppermute | solution.py:397
  29.9 20.1 %copy-start.3 = (bf16[1552,128]{1,0:T(8,128)(2,1)}, bf16[1552,128]{1,0:T(8,128)(2,1)S(1)}, u32[]{:S(2)}) copy-start(bf16[1552,128]{1,0:T(8,128)(2,1)S(1)} %collective-permute-done.3.refs_4_) | copy-start | bytes 1191940
  29.9 19.5 %collective-permute-start.15 = (bf16[512,128]{1,0:T(8,128)(2,1)}, bf16[512,128]{1,0:T(8,128)(2,1)S(1)}, u32[]{:S(2)}, u32[]{:S(2)}) collective-permute-start(bf16[512,128]{1,0:T(8,128)(2,1)} %get-tuple-element.75), channel_id=1, source_target_pairs={{0,8},{4,12},{8,0},{12,4},{16,24},{20,28},{24,16},{28,20},{1,9},{5... | collective-permute-start | bytes 393224 | tf_op jit(solution)/shard_map/ppermute | solution.py:397
  36.0 31.4 %collective-permute-start.16 = (bf16[512,128]{1,0:T(8,128)(2,1)}, bf16[512,128]{1,0:T(8,128)(2,1)S(1)}, u32[]{:S(2)}, u32[]{:S(2)}) collective-permute-start(bf16[512,128]{1,0:T(8,128)(2,1)} %get-tuple-element.76), channel_id=1, source_target_pairs={{0,16},{4,20},{8,24},{12,28},{16,0},{20,4},{24,8},{28,12},{1,17},{... | collective-permute-start | bytes 393224 | tf_op jit(solution)/shard_map/ppermute | solution.py:397
  46.0 21.4 %collective-permute-start.17 = (bf16[512,128]{1,0:T(8,128)(2,1)}, bf16[512,128]{1,0:T(8,128)(2,1)S(1)}, u32[]{:S(2)}, u32[]{:S(2)}) collective-permute-start(bf16[512,128]{1,0:T(8,128)(2,1)} %get-tuple-element.77), channel_id=1, source_target_pairs={{0,24},{4,28},{8,16},{12,20},{16,8},{20,12},{24,0},{28,4},{1,25},{... | collective-permute-start | bytes 393224 | tf_op jit(solution)/shard_map/ppermute | solution.py:397
  46.0 21.4 %collective-permute-start.18 = (bf16[512,128]{1,0:T(8,128)(2,1)}, bf16[512,128]{1,0:T(8,128)(2,1)S(1)}, u32[]{:S(2)}, u32[]{:S(2)}) collective-permute-start(bf16[512,128]{1,0:T(8,128)(2,1)} %get-tuple-element.78), channel_id=1, source_target_pairs={{0,12},{4,8},{8,4},{12,0},{16,28},{20,24},{24,20},{28,16},{1,13},{... | collective-permute-start | bytes 393224 | tf_op jit(solution)/shard_map/ppermute | solution.py:397
  49.3 18.1 %collective-permute-start.19 = (bf16[512,128]{1,0:T(8,128)(2,1)}, bf16[512,128]{1,0:T(8,128)(2,1)S(1)}, u32[]{:S(2)}, u32[]{:S(2)}) collective-permute-start(bf16[512,128]{1,0:T(8,128)(2,1)} %get-tuple-element.79), channel_id=1, source_target_pairs={{0,20},{4,16},{8,28},{12,24},{16,4},{20,0},{24,12},{28,8},{1,21},{... | collective-permute-start | bytes 393224 | tf_op jit(solution)/shard_map/ppermute | solution.py:397
  49.3 18.1 %collective-permute-start.20 = (bf16[512,128]{1,0:T(8,128)(2,1)}, bf16[512,128]{1,0:T(8,128)(2,1)S(1)}, u32[]{:S(2)}, u32[]{:S(2)}) collective-permute-start(bf16[512,128]{1,0:T(8,128)(2,1)} %get-tuple-element.80), channel_id=1, source_target_pairs={{0,28},{4,24},{8,20},{12,16},{16,12},{20,8},{24,4},{28,0},{1,29},{... | collective-permute-start | bytes 393224 | tf_op jit(solution)/shard_map/ppermute | solution.py:397
  72.1 2.2 %collective-permute-start.21 = (f32[2,4096]{1,0:T(2,128)}, f32[2,4096]{1,0:T(2,128)S(1)}, u32[]{:S(2)}, u32[]{:S(2)}) collective-permute-start(f32[2,4096]{1,0:T(2,128)} %project.1), channel_id=1, source_target_pairs={{0,4},{4,0},{8,12},{12,8},{16,20},{20,16},{24,28},{28,24},{1,5},{5... | collective-permute-start | bytes 98312 | tf_op jit(solution)/shard_map/ppermute | solution.py:397
  75.1 7.5 %collective-permute-start.24 = (f32[2,4096]{1,0:T(2,128)S(1)}, f32[2,4096]{1,0:T(2,128)S(1)}, u32[]{:S(2)}, u32[]{:S(2)}) collective-permute-start(f32[2,4096]{1,0:T(2,128)S(1)} %add.55), channel_id=1, source_target_pairs={{0,24},{4,28},{8,16},{12,20},{16,8},{20,12},{24,0},{28,4},{1,25},{... | collective-permute-start | bytes 98312 | tf_op jit(solution)/shard_map/ppermute | solution.py:397
  76.7 5.9 %collective-permute-start.23 = (f32[2,4096]{1,0:T(2,128)S(1)}, f32[2,4096]{1,0:T(2,128)S(1)}, u32[]{:S(2)}, u32[]{:S(2)}) collective-permute-start(f32[2,4096]{1,0:T(2,128)S(1)} %add.55), channel_id=1, source_target_pairs={{0,16},{4,20},{8,24},{12,28},{16,0},{20,4},{24,8},{28,12},{1,17},{... | collective-permute-start | bytes 98312 | tf_op jit(solution)/shard_map/ppermute | solution.py:397
  78.5 4.0 %collective-permute-start.22 = (f32[2,4096]{1,0:T(2,128)S(1)}, f32[2,4096]{1,0:T(2,128)S(1)}, u32[]{:S(2)}, u32[]{:S(2)}) collective-permute-start(f32[2,4096]{1,0:T(2,128)S(1)} %add.55), channel_id=1, source_target_pairs={{0,8},{4,12},{8,0},{12,4},{16,24},{20,28},{24,16},{28,20},{1,9},{5... | collective-permute-start | bytes 98312 | tf_op jit(solution)/shard_map/ppermute | solution.py:397
  80.7 6.8 %collective-permute-start.7 = (bf16[512,128]{1,0:T(8,128)(2,1)S(1)}, bf16[512,128]{1,0:T(8,128)(2,1)S(1)}, u32[]{:S(2)}, u32[]{:S(2)}) collective-permute-start(bf16[512,128]{1,0:T(8,128)(2,1)S(1)} %get-tuple-element.112), channel_id=1, source_target_pairs={{0,4},{4,0},{8,12},{12,8},{16,20},{20,16},{24,28},{28,24},{1,5},{5... | collective-permute-start | bytes 393224 | tf_op jit(solution)/shard_map/ppermute | solution.py:397
  80.7 7.0 %collective-permute-start.8 = (bf16[512,128]{1,0:T(8,128)(2,1)S(1)}, bf16[512,128]{1,0:T(8,128)(2,1)S(1)}, u32[]{:S(2)}, u32[]{:S(2)}) collective-permute-start(bf16[512,128]{1,0:T(8,128)(2,1)S(1)} %get-tuple-element.111), channel_id=1, source_target_pairs={{0,8},{4,12},{8,0},{12,4},{16,24},{20,28},{24,16},{28,20},{1,9},{5... | collective-permute-start | bytes 393224 | tf_op jit(solution)/shard_map/ppermute | solution.py:397
  82.6 6.5 %collective-permute-start.27 = (f32[2,4096]{1,0:T(2,128)S(1)}, f32[2,4096]{1,0:T(2,128)S(1)}, u32[]{:S(2)}, u32[]{:S(2)}) collective-permute-start(f32[2,4096]{1,0:T(2,128)S(1)} %add_add_fusion.1), channel_id=1, source_target_pairs={{0,3},{1,0},{2,1},{3,2},{4,7},{5,4},{6,5},{7,6},{8,11},{9,8},{10,9... | collective-permute-start | bytes 98312 | tf_op jit(solution)/shard_map/ppermute | solution.py:409
  86.4 5.0 %collective-permute-start.26 = (f32[2,4096]{1,0:T(2,128)S(1)}, f32[2,4096]{1,0:T(2,128)S(1)}, u32[]{:S(2)}, u32[]{:S(2)}) collective-permute-start(f32[2,4096]{1,0:T(2,128)S(1)} %add_add_fusion.1), channel_id=1, source_target_pairs={{0,2},{1,3},{2,0},{3,1},{4,6},{5,7},{6,4},{7,5},{8,10},{9,11},{10,... | collective-permute-start | bytes 98312 | tf_op jit(solution)/shard_map/ppermute | solution.py:409
  86.4 5.7 %collective-permute-start.25 = (f32[2,4096]{1,0:T(2,128)S(1)}, f32[2,4096]{1,0:T(2,128)S(1)}, u32[]{:S(2)}, u32[]{:S(2)}) collective-permute-start(f32[2,4096]{1,0:T(2,128)S(1)} %add_add_fusion.1), channel_id=1, source_target_pairs={{0,1},{1,2},{2,3},{3,0},{4,5},{5,6},{6,7},{7,4},{8,9},{9,10},{10,1... | collective-permute-start | bytes 98312 | tf_op jit(solution)/shard_map/ppermute | solution.py:409
  87.5 47.7 %copy-start.21 = (bf16[512,128]{1,0:T(8,128)(2,1)}, bf16[512,128]{1,0:T(8,128)(2,1)S(1)}, u32[]{:S(2)}) copy-start(bf16[512,128]{1,0:T(8,128)(2,1)S(1)} %collective-permute-done.7.refs_1_) | copy-start | bytes 393220
  87.5 8.0 %collective-permute-start.9 = (bf16[512,128]{1,0:T(8,128)(2,1)S(1)}, bf16[512,128]{1,0:T(8,128)(2,1)S(1)}, u32[]{:S(2)}, u32[]{:S(2)}) collective-permute-start(bf16[512,128]{1,0:T(8,128)(2,1)S(1)} %get-tuple-element.110), channel_id=1, source_target_pairs={{0,16},{4,20},{8,24},{12,28},{16,0},{20,4},{24,8},{28,12},{1,17},{... | collective-permute-start | bytes 393224 | tf_op jit(solution)/shard_map/ppermute | solution.py:397
  87.7 47.5 %copy-start.22 = (bf16[512,128]{1,0:T(8,128)(2,1)}, bf16[512,128]{1,0:T(8,128)(2,1)S(1)}, u32[]{:S(2)}) copy-start(bf16[512,128]{1,0:T(8,128)(2,1)S(1)} %collective-permute-done.8.refs_2_) | copy-start | bytes 393220
  87.7 7.8 %collective-permute-start.10 = (bf16[512,128]{1,0:T(8,128)(2,1)S(1)}, bf16[512,128]{1,0:T(8,128)(2,1)S(1)}, u32[]{:S(2)}, u32[]{:S(2)}) collective-permute-start(bf16[512,128]{1,0:T(8,128)(2,1)S(1)} %get-tuple-element.109), channel_id=1, source_target_pairs={{0,24},{4,28},{8,16},{12,20},{16,8},{20,12},{24,0},{28,4},{1,25},{... | collective-permute-start | bytes 393224 | tf_op jit(solution)/shard_map/ppermute | solution.py:397
  89.1 6.4 %collective-permute-start.11 = (bf16[512,128]{1,0:T(8,128)(2,1)S(1)}, bf16[512,128]{1,0:T(8,128)(2,1)S(1)}, u32[]{:S(2)}, u32[]{:S(2)}) collective-permute-start(bf16[512,128]{1,0:T(8,128)(2,1)S(1)} %get-tuple-element.108), channel_id=1, source_target_pairs={{0,12},{4,8},{8,4},{12,0},{16,28},{20,24},{24,20},{28,16},{1,13},{... | collective-permute-start | bytes 393224 | tf_op jit(solution)/shard_map/ppermute | solution.py:397
  91.5 8.8 %collective-permute-start.12 = (bf16[512,128]{1,0:T(8,128)(2,1)S(1)}, bf16[512,128]{1,0:T(8,128)(2,1)S(1)}, u32[]{:S(2)}, u32[]{:S(2)}) collective-permute-start(bf16[512,128]{1,0:T(8,128)(2,1)S(1)} %get-tuple-element.107), channel_id=1, source_target_pairs={{0,20},{4,16},{8,28},{12,24},{16,4},{20,0},{24,12},{28,8},{1,21},{... | collective-permute-start | bytes 393224 | tf_op jit(solution)/shard_map/ppermute | solution.py:397
  92.2 8.1 %collective-permute-start.13 = (bf16[512,128]{1,0:T(8,128)(2,1)S(1)}, bf16[512,128]{1,0:T(8,128)(2,1)S(1)}, u32[]{:S(2)}, u32[]{:S(2)}) collective-permute-start(bf16[512,128]{1,0:T(8,128)(2,1)S(1)} %get-tuple-element.106), channel_id=1, source_target_pairs={{0,28},{4,24},{8,20},{12,16},{16,12},{20,8},{24,4},{28,0},{1,29},{... | collective-permute-start | bytes 393224 | tf_op jit(solution)/shard_map/ppermute | solution.py:397
  95.5 39.7 %copy-start.23 = (bf16[512,128]{1,0:T(8,128)(2,1)}, bf16[512,128]{1,0:T(8,128)(2,1)S(1)}, u32[]{:S(2)}) copy-start(bf16[512,128]{1,0:T(8,128)(2,1)S(1)} %collective-permute-done.9.refs_3_) | copy-start | bytes 393220
  95.5 39.7 %copy-start.24 = (bf16[512,128]{1,0:T(8,128)(2,1)}, bf16[512,128]{1,0:T(8,128)(2,1)S(1)}, u32[]{:S(2)}) copy-start(bf16[512,128]{1,0:T(8,128)(2,1)S(1)} %collective-permute-done.10.refs_4_) | copy-start | bytes 393220
  95.5 39.7 %copy-start.25 = (bf16[512,128]{1,0:T(8,128)(2,1)}, bf16[512,128]{1,0:T(8,128)(2,1)S(1)}, u32[]{:S(2)}) copy-start(bf16[512,128]{1,0:T(8,128)(2,1)S(1)} %collective-permute-done.11.refs_5_) | copy-start | bytes 393220
  100.3 34.9 %copy-start.26 = (bf16[512,128]{1,0:T(8,128)(2,1)}, bf16[512,128]{1,0:T(8,128)(2,1)S(1)}, u32[]{:S(2)}) copy-start(bf16[512,128]{1,0:T(8,128)(2,1)S(1)} %collective-permute-done.12.refs_6_) | copy-start | bytes 393220
  100.3 34.9 %copy-start.27 = (bf16[512,128]{1,0:T(8,128)(2,1)}, bf16[512,128]{1,0:T(8,128)(2,1)S(1)}, u32[]{:S(2)}) copy-start(bf16[512,128]{1,0:T(8,128)(2,1)S(1)} %collective-permute-done.13.refs_7_) | copy-start | bytes 393220
  121.5 3.8 %collective-permute-start.28 = (bf16[1536,128]{1,0:T(8,128)(2,1)}, bf16[1536,128]{1,0:T(8,128)(2,1)S(1)}, u32[]{:S(2)}, u32[]{:S(2)}) collective-permute-start(bf16[1536,128]{1,0:T(8,128)(2,1)} %get-tuple-element.96), channel_id=1, source_target_pairs={{0,4},{4,0},{8,12},{12,8},{16,20},{20,16},{24,28},{28,24},{1,5},{5... | collective-permute-start | bytes 1179656 | tf_op jit(solution)/shard_map/ppermute | solution.py:397
  121.8 12.1 %collective-permute-start.29 = (bf16[1536,128]{1,0:T(8,128)(2,1)}, bf16[1536,128]{1,0:T(8,128)(2,1)S(1)}, u32[]{:S(2)}, u32[]{:S(2)}) collective-permute-start(bf16[1536,128]{1,0:T(8,128)(2,1)} %get-tuple-element.97), channel_id=1, source_target_pairs={{0,8},{4,12},{8,0},{12,4},{16,24},{20,28},{24,16},{28,20},{1,9},{5... | collective-permute-start | bytes 1179656 | tf_op jit(solution)/shard_map/ppermute | solution.py:397
  122.2 20.6 %collective-permute-start.30 = (bf16[1536,128]{1,0:T(8,128)(2,1)}, bf16[1536,128]{1,0:T(8,128)(2,1)S(1)}, u32[]{:S(2)}, u32[]{:S(2)}) collective-permute-start(bf16[1536,128]{1,0:T(8,128)(2,1)} %get-tuple-element.98), channel_id=1, source_target_pairs={{0,16},{4,20},{8,24},{12,28},{16,0},{20,4},{24,8},{28,12},{1,17},{... | collective-permute-start | bytes 1179656 | tf_op jit(solution)/shard_map/ppermute | solution.py:397
  122.9 19.9 %collective-permute-start.31 = (bf16[1536,128]{1,0:T(8,128)(2,1)}, bf16[1536,128]{1,0:T(8,128)(2,1)S(1)}, u32[]{:S(2)}, u32[]{:S(2)}) collective-permute-start(bf16[1536,128]{1,0:T(8,128)(2,1)} %get-tuple-element.99), channel_id=1, source_target_pairs={{0,24},{4,28},{8,16},{12,20},{16,8},{20,12},{24,0},{28,4},{1,25},{... | collective-permute-start | bytes 1179656 | tf_op jit(solution)/shard_map/ppermute | solution.py:397
  125.2 24.4 %collective-permute-start.32 = (bf16[1536,128]{1,0:T(8,128)(2,1)}, bf16[1536,128]{1,0:T(8,128)(2,1)S(1)}, u32[]{:S(2)}, u32[]{:S(2)}) collective-permute-start(bf16[1536,128]{1,0:T(8,128)(2,1)} %get-tuple-element.100), channel_id=1, source_target_pairs={{0,12},{4,8},{8,4},{12,0},{16,28},{20,24},{24,20},{28,16},{1,13},{... | collective-permute-start | bytes 1179656 | tf_op jit(solution)/shard_map/ppermute | solution.py:397
  125.2 33.3 %copy-start.14 = (bf16[1536,128]{1,0:T(8,128)(2,1)}, bf16[1536,128]{1,0:T(8,128)(2,1)S(1)}, u32[]{:S(2)}) copy-start(bf16[1536,128]{1,0:T(8,128)(2,1)S(1)} %collective-permute-done.28.refs_1_) | copy-start | bytes 1179652
  125.3 24.4 %collective-permute-start.33 = (bf16[1536,128]{1,0:T(8,128)(2,1)}, bf16[1536,128]{1,0:T(8,128)(2,1)S(1)}, u32[]{:S(2)}, u32[]{:S(2)}) collective-permute-start(bf16[1536,128]{1,0:T(8,128)(2,1)} %get-tuple-element.101), channel_id=1, source_target_pairs={{0,20},{4,16},{8,28},{12,24},{16,4},{20,0},{24,12},{28,8},{1,21},{... | collective-permute-start | bytes 1179656 | tf_op jit(solution)/shard_map/ppermute | solution.py:397
  133.9 24.6 %copy-start.15 = (bf16[1536,128]{1,0:T(8,128)(2,1)}, bf16[1536,128]{1,0:T(8,128)(2,1)S(1)}, u32[]{:S(2)}) copy-start(bf16[1536,128]{1,0:T(8,128)(2,1)S(1)} %collective-permute-done.29.refs_2_) | copy-start | bytes 1179652
  133.9 24.6 %collective-permute-start.34 = (bf16[1536,128]{1,0:T(8,128)(2,1)}, bf16[1536,128]{1,0:T(8,128)(2,1)S(1)}, u32[]{:S(2)}, u32[]{:S(2)}) collective-permute-start(bf16[1536,128]{1,0:T(8,128)(2,1)} %get-tuple-element.102), channel_id=1, source_target_pairs={{0,28},{4,24},{8,20},{12,16},{16,12},{20,8},{24,4},{28,0},{1,29},{... | collective-permute-start | bytes 1179656 | tf_op jit(solution)/shard_map/ppermute | solution.py:397
  (15 other events, 111.9 us)
where the time goes:
time: 164 us; the launch traced here: 163 us
  waiting for transfers between devices  66.9 us (41%)
  Pallas kernels  54.3 us (33%)
  starting transfers between devices  34.6 us (21%)
  local copies, waits for them, and re-layouts  4.85 us (3%)
    ppermute x32, waiting for transfers between devices, swap(): return lax.ppermute(value, 'seq', [(s, s ^ m) for s in range(n)])  64.1 us
    ppermute x32, starting transfers between devices, swap(): return lax.ppermute(value, 'seq', [(s, s ^ m) for s in range(n)])  29.7 us
    pallas_call x1, Pallas kernels, run_backward(): pl.pallas_call(functools.partial(backward_kernel, block), out_shape=[shap...  21.2 us
    pallas_call x1, Pallas kernels, run_forward(): pl.pallas_call(functools.partial(forward_kernel, block), out_shape=[shape...  17.4 us
    pallas_call x1, Pallas kernels, by_head(): pl.pallas_call(functools.partial(pack_kernel, block), out_shape=[shape_of...  5.34 us
    ppermute x3, starting transfers between devices, sum_everywhere(): lax.ppermute(stats, 'head', [(s, (s + d) % heads) for s in range(heads)])  4.83 us
    pallas_call x1, Pallas kernels, run_project(): pl.pallas_call(functools.partial(project_kernel, block), out_shape=shape_...  3.87 us
    pallas_call x1, Pallas kernels, by_head(): pl.pallas_call(functools.partial(unpack_kernel, block), out_shape=[shape_...  3.78 us
  transfers between devices with their start and end apart: 35, of which 13 were waited for; matrix products, arithmetic and copies ran while one was open for 2% of the time, Pallas kernels for 12%

commit v1 on v0

--- a/solution.py
+++ b/solution.py
@@ -22,6 +22,7 @@
 
 
 ORDER = (0, 1, 2, 4, 6, 3, 5, 7)
+TIE = 3
 FIRST_USE = [max(t + off for off in OFFSETS if t + off < 8) for t in range(8)]
 
 
@@ -112,20 +113,19 @@
             held.at[part, pl.ds(pl.multiple_of(t * block, block), block), :],
             sems.at[part, t],
         )
-        for part in range(3)
+        for part in range(2)
     ]
 
 
-def forward_kernel(block, rank_ref, *refs):
+def score_kernel(block, rank_ref, *refs):
     n = 8
     a_refs = refs[:n]
-    prob_ref, out_t_ref, out_ref, inv_ref, square_ref, bounds = refs[n : n + 6]
-    held, ids, val_t, prob, out_t_keep, out_keep = refs[n + 6 : n + 12]
-    total, acc, sems, id_sems, prob_sems, out_sems = refs[n + 12 :]
+    prob_ref, inv_ref, bounds = refs[n : n + 3]
+    held, ids, prob, sems, id_sems, prob_sems = refs[n + 3 :]
     rank = rank_ref[0]
 
     def ids_in(m, ref):
-        return pltpu.make_async_copy(ref.at[3 * block :, :], ids.at[rank ^ m], id_sems.at[m])
+        return pltpu.make_async_copy(ref.at[2 * block :, :], ids.at[rank ^ m], id_sems.at[m])
 
     for m, ref in zip(ORDER, a_refs):
         ids_in(m, ref).start()
@@ -144,17 +144,10 @@
             prob.at[i, rows, :], prob_ref.at[i, rows, :], prob_sems.at[i, slot]
         )
 
-    def rows_out(i):
-        return (
-            pltpu.make_async_copy(out_t_keep.at[i], out_t_ref.at[i], out_sems.at[0, i]),
-            pltpu.make_async_copy(out_keep.at[i], out_ref.at[i], out_sems.at[1, i]),
-        )
-
     def one_block(i, carry):
         own_rows = pl.ds(pl.multiple_of(i * block, block), block)
         for copy in parts_in(a_refs[0], i, block, held, sems):
             copy.wait()
-        val_t[:, own_rows] = held[2, own_rows, :].T
         query = held[0, own_rows, :]
         q_pos, q_start = doc_starts(i, block, bounds)
 
@@ -175,33 +168,102 @@
                 scores.append(s)
                 peak = jnp.max(s, axis=0, keepdims=True)
                 top = peak if top is None else jnp.maximum(top, peak)
-            for number, ((row, key, size, own), s) in enumerate(zip(found, scores)):
+            total = None
+            for (row, key, size, own), s in zip(found, scores):
                 p = jnp.exp2(s - top)
                 line = jnp.sum(p, axis=0, keepdims=True)
-                pb = p.astype(BF16)
-                prob[i, row : row + size, :] = pb
-                term = nn_dot(val_t[:, pl.ds(key, size)], pb)
-                total[...] = line if number == 0 else total[...] + line
-                acc[...] = term if number == 0 else acc[...] + term
+                prob[i, row : row + size, :] = p.astype(BF16)
+                total = line if total is None else total + line
+            inv_ref[i] = 1.0 / total
             for slot in slots_of(near, far):
                 prob_out(i, slot).start()
 
         for_each_reach(i, block, bounds, body, True)
-
-        inv = 1.0 / total[...]
-        out_t = acc[...] * inv
+        return carry
+
+    lax.fori_loop(0, n, one_block, 0)
+
+    def finish(i, carry):
+        each_slot(i, block, bounds, lambda slot: prob_out(i, slot).wait())
+        return carry
+
+    lax.fori_loop(0, n, finish, 0)
+
+
+def value_in(vg_ref, t, block, values, sems):
+    return pltpu.make_async_copy(
+        vg_ref.at[0:block, :],
+        values.at[pl.ds(pl.multiple_of(t * block, block), block), :],
+        sems.at[0, t],
+    )
+
+
+def cot_in(vg_ref, t, block, cot, sems):
+    return pltpu.make_async_copy(vg_ref.at[block:, :], cot.at[t], sems.at[1, t])
+
+
+def fetch_probs(n, block, bounds, prob_ref, prob, sems):
+    def prob_in(i, slot):
+        rows = slice(slot * block, (slot + 1) * block)
+        return pltpu.make_async_copy(prob_ref.at[i, rows, :], prob.at[i, rows, :], sems.at[i, slot])
+
+    return prob_in
+
+
+def attend_kernel(block, rank_ref, bounds, *refs):
+    n = 8
+    vg_refs = refs[:n]
+    prob_ref, inv_ref, out_t_ref, out_ref, stats_ref = refs[n : n + 5]
+    values, cot, val_t, prob, out_t_keep, out_keep, acc, vg_sems, prob_sems, out_sems = refs[n + 5 :]
+    vg_ref = vg_refs[0]
+    prob_in = fetch_probs(n, block, bounds, prob_ref, prob, prob_sems)
+
+    def rows_out(i):
+        return (
+            pltpu.make_async_copy(out_t_keep.at[i], out_t_ref.at[i], out_sems.at[0, i]),
+            pltpu.make_async_copy(out_keep.at[i], out_ref.at[i], out_sems.at[1, i]),
+        )
+
+    for m, ref in zip(ORDER, vg_refs):
+        value_in(ref, rank_ref[0] ^ m, block, values, vg_sems).start()
+        cot_in(ref, rank_ref[0] ^ m, block, cot, vg_sems).start()
+    for t in range(n):
+        each_slot(t, block, bounds, lambda slot: prob_in(t, slot).start())
+    ones = jnp.ones((16, HEAD_DIM), BF16)
+
+    def one_block(i, carry):
+        own_rows = pl.ds(pl.multiple_of(i * block, block), block)
+        value_in(vg_ref, i, block, values, vg_sems).wait()
+        val_t[:, own_rows] = values[own_rows, :].T
+
+        def body(near, far, masked):
+            for slot in slots_of(near, far):
+                prob_in(i, slot).wait()
+            out = None
+            for row, key, size, own in pieces(i, near, far, block):
+                term = nn_dot(val_t[:, pl.ds(key, size)], prob[i, row : row + size, :])
+                out = term if out is None else out + term
+            acc[...] = out
+
+        for_each_reach(i, block, bounds, body, False)
+
+        out_t = acc[...] * inv_ref[i]
         out_t_keep[i] = out_t
-        out_keep[i] = out_t.T.astype(BF16)
-        inv_ref[i] = inv
-        square_ref[i] = jnp.sum(out_t * out_t, axis=0, keepdims=True)
+        out = out_t.T
+        out_keep[i] = out.astype(BF16)
         for copy in rows_out(i):
             copy.start()
+        stats_ref[0, i] = jnp.sum(out_t * out_t, axis=0, keepdims=True)
+        cot_in(vg_ref, i, block, cot, vg_sems).wait()
+        x = cot[i].astype(F32) * out
+        high = x.astype(BF16)
+        low = (x - high.astype(F32)).astype(BF16)
+        stats_ref[1, i] = (nt_dot(ones, high) + nt_dot(ones, low))[0:1]
         return carry
 
     lax.fori_loop(0, n, one_block, 0)
 
     def finish(i, carry):
-        each_slot(i, block, bounds, lambda slot: prob_out(i, slot).wait())
         for copy in rows_out(i):
             copy.wait()
         return carry
@@ -209,53 +271,28 @@
     lax.fori_loop(0, n, finish, 0)
 
 
-def project_kernel(block, rank_ref, *refs):
-    n = 8
-    g_refs = refs[:n]
-    out_ref, square_ref, stats_ref, held, sems = refs[n:]
-    rank = rank_ref[0]
-    copies = [
-        pltpu.make_async_copy(ref, held.at[rank ^ m], sems.at[m]) for m, ref in zip(ORDER, g_refs)
-    ]
-    for copy in copies:
-        copy.start()
-    for copy in copies:
-        copy.wait()
-    ones = jnp.ones((16, HEAD_DIM), BF16)
-    for t in range(n):
-        x = held[t].astype(F32) * out_ref[t].astype(F32)
-        high = x.astype(BF16)
-        low = (x - high.astype(F32)).astype(BF16)
-        cols = slice(t * block, (t + 1) * block)
-        stats_ref[0:1, cols] = square_ref[t]
-        stats_ref[1:2, cols] = (nt_dot(ones, high) + nt_dot(ones, low))[0:1]
-
-
 def backward_kernel(block, rank_ref, bounds, *refs):
     n = 8
-    a_refs, g_refs = refs[:n], refs[n : 2 * n]
-    prob_ref, out_t_ref, inv_ref, stats_ref = refs[2 * n : 2 * n + 4]
-    d_refs = refs[2 * n + 4 : 3 * n + 4]
-    held, cot, key_t, prob, out_t_keep, stage, grad_k, grad_v, acc = refs[3 * n + 4 : 3 * n + 13]
-    sems, g_sems, prob_sems, out_sems, d_sems = refs[3 * n + 13 :]
+    a_refs, vg_refs = refs[:n], refs[n : 2 * n]
+    vg_ref = vg_refs[0]
+    refs = refs[n - 1 :]
+    prob_ref, out_t_ref, inv_ref, stats_ref = refs[n + 1 : n + 5]
+    d_refs = refs[n + 5 : 2 * n + 5]
+    held, values, cot, key_t, prob, out_t_keep, stage, grad_k, grad_v, acc = refs[
+        2 * n + 5 : 2 * n + 15
+    ]
+    sems, vg_sems, prob_sems, out_sems, d_sems = refs[2 * n + 15 :]
     rank = rank_ref[0]
     scale = 1.0 / math.sqrt(HEAD_DIM)
     width = HEADS * HEAD_DIM
 
-    def cot_in(ref, t):
-        return pltpu.make_async_copy(ref, cot.at[t], g_sems.at[t])
-
     def out_in(i):
         return pltpu.make_async_copy(out_t_ref.at[i], out_t_keep.at[i], out_sems.at[i])
 
-    def prob_in(i, slot):
-        rows = slice(slot * block, (slot + 1) * block)
-        return pltpu.make_async_copy(
-            prob_ref.at[i, rows, :], prob.at[i, rows, :], prob_sems.at[i, slot]
-        )
-
-    for m, ref in zip(ORDER, g_refs):
-        cot_in(ref, rank ^ m).start()
+    prob_in = fetch_probs(n, block, bounds, prob_ref, prob, prob_sems)
+    for m, ref in zip(ORDER, vg_refs):
+        cot_in(ref, rank ^ m, block, cot, vg_sems).start()
+        value_in(ref, rank ^ m, block, values, vg_sems).start()
     for m, ref in zip(ORDER, a_refs):
         for copy in parts_in(ref, rank ^ m, block, held, sems):
             copy.start()
@@ -272,10 +309,10 @@
 
     def one_block(step, carry):
         i = n - 1 - step
-        cot_in(g_refs[0], i).wait()
+        cot_in(vg_ref, i, block, cot, vg_sems).wait()
         out_in(i).wait()
-        inv_rms = lax.rsqrt(stats_ref[i, 0:1, :] / width + norm_eps)
-        coef = inv_rms * inv_rms * inv_rms * stats_ref[i, 1:2, :] / width
+        inv_rms = lax.rsqrt(stats_ref[0, i] / width + norm_eps)
+        coef = inv_rms * inv_rms * inv_rms * stats_ref[1, i] / width
         out_t = out_t_keep[i]
         dattn_t = (inv_rms * cot[i].astype(F32).T - out_t * coef) * inv_ref[i]
         dattn_tb = dattn_t.astype(BF16)
@@ -290,6 +327,7 @@
                     if FIRST_USE[t] == first:
                         for copy in parts_in(a_refs[0], t, block, held, sems):
                             copy.wait()
+                        value_in(vg_ref, t, block, values, vg_sems).wait()
                         cols = slice(t * block, (t + 1) * block)
                         key_t[:, cols] = held[1, cols, :].T
 
@@ -302,7 +340,7 @@
             for number, (row, key, size, own) in enumerate(pieces(i, near, far, block)):
                 rows = pl.ds(key, size)
                 pb = prob[i, row : row + size, :]
-                dprob = nn_dot(held[2, rows, :], dattn_tb)
+                dprob = nn_dot(values[rows, :], dattn_tb)
                 ds = (pb.astype(F32) * (dprob - delta)).astype(BF16)
                 term = nn_dot(key_t[:, rows], ds)
                 acc[...] = term if number == 0 else acc[...] + term
@@ -329,18 +367,18 @@
 
 def pack_kernel(block, rank_ref, q_ref, k_ref, v_ref, g_ref, doc_ref, *refs):
     n = 8
-    a_refs, g_refs, sems = refs[:n], refs[n : 2 * n], refs[2 * n]
-    copies = []
-    for index, m in enumerate(ORDER):
+    a_refs, vg_refs, sems = refs[:n], refs[n : 2 * n], refs[2 * n]
+    parts = []
+    for m, ref, other in zip(ORDER, a_refs, vg_refs):
         cols = pl.ds(pl.multiple_of((rank_ref[0] ^ m) * HEAD_DIM, HEAD_DIM), HEAD_DIM)
-        parts = [
-            (q_ref.at[:, cols], a_refs[index].at[0:block, :]),
-            (k_ref.at[:, cols], a_refs[index].at[block : 2 * block, :]),
-            (v_ref.at[:, cols], a_refs[index].at[2 * block : 3 * block, :]),
-            (g_ref.at[:, cols], g_refs[index]),
-        ]
-        for source, target in parts:
-            copies.append(pltpu.make_async_copy(source, target, sems.at[len(copies)]))
+        parts.append((q_ref.at[:, cols], ref.at[0:block, :]))
+        parts.append((k_ref.at[:, cols], ref.at[block : 2 * block, :]))
+        parts.append((v_ref.at[:, cols], other.at[0:block, :]))
+        parts.append((g_ref.at[:, cols], other.at[block:, :]))
+    copies = [
+        pltpu.make_async_copy(source, target, sems.at[number])
+        for number, (source, target) in enumerate(parts)
+    ]
     for copy in copies:
         copy.start()
     row = lax.broadcasted_iota(jnp.int32, (16, HEAD_DIM), 0)
@@ -349,7 +387,7 @@
         part = doc_ref[0:1, k * HEAD_DIM : (k + 1) * HEAD_DIM].astype(F32)
         ids = jnp.where(row == k, part, ids)
     for ref in a_refs:
-        ref[3 * block :, :] = ids.astype(BF16)
+        ref[2 * block :, :] = ids.astype(BF16)
     for copy in copies:
         copy.wait()
 
@@ -371,14 +409,12 @@
         copy.wait()
 
 
-def normed_kernel(block, rank_ref, stats_ref, *refs):
-    n = 8
-    o_refs, out_ref = refs[:n], refs[n]
-    inv_rms = lax.rsqrt(stats_ref[0, 0:1, :] / (HEADS * HEAD_DIM) + norm_eps)
+def normed_kernel(block, stats_ref, home_ref, out_ref):
+    inv_rms = lax.rsqrt(stats_ref[...] / (HEADS * HEAD_DIM) + norm_eps)
     spread = jnp.broadcast_to(inv_rms, (HEAD_DIM, block)).T
-    for m, ref in zip(ORDER, o_refs):
-        cols = pl.ds(pl.multiple_of((rank_ref[0] ^ m) * HEAD_DIM, HEAD_DIM), HEAD_DIM)
-        out_ref[:, cols] = (ref[...].astype(F32) * spread).astype(BF16)
+    for h in range(home_ref.shape[0]):
+        cols = slice(h * HEAD_DIM, (h + 1) * HEAD_DIM)
+        out_ref[:, cols] = (home_ref[h].astype(F32) * spread).astype(BF16)
 
 
 SMEM_SPEC = pl.BlockSpec(memory_space=pltpu.SMEM)
@@ -399,6 +435,10 @@
 
 def swap_all(parts):
     return [swap(part, m) for m, part in zip(ORDER, parts)]
+
+
+def all_to_all(value):
+    return lax.all_to_all(value, "seq", split_axis=0, concat_axis=0, tiled=True)
 
 
 def sum_everywhere(stats):
@@ -412,56 +452,63 @@
     return functools.reduce(jnp.add, parts, stats)
 
 
-def run_forward(rank, a, block):
+def params():
+    return pltpu.CompilerParams(vmem_limit_bytes=VMEM_BYTES)
+
+
+def run_score(rank, a, block):
     n = len(a)
     return pl.pallas_call(
-        functools.partial(forward_kernel, block),
+        functools.partial(score_kernel, block),
         out_shape=[
             shape_of((n, 4 * block, block), BF16),
-            shape_of((n, HEAD_DIM, block), F32),
-            shape_of((n, block, HEAD_DIM), BF16),
-            shape_of((n, 1, block), F32),
             shape_of((n, 1, block), F32),
             shape_of((3,), jnp.int32),
         ],
         in_specs=[SMEM_SPEC] + [ANY_SPEC] * n,
-        out_specs=[ANY_SPEC] * 3 + [VMEM_SPEC] * 2 + [SMEM_SPEC],
+        out_specs=[ANY_SPEC, VMEM_SPEC, SMEM_SPEC],
         scratch_shapes=[
-            pltpu.VMEM((3, n * block, HEAD_DIM), BF16),
+            pltpu.VMEM((2, n * block, HEAD_DIM), BF16),
             pltpu.VMEM((n, 16, HEAD_DIM), BF16),
+            pltpu.VMEM((n, 4 * block, block), BF16),
+            pltpu.SemaphoreType.DMA((2, n)),
+            pltpu.SemaphoreType.DMA((n,)),
+            pltpu.SemaphoreType.DMA((n, 4)),
+        ],
+        compiler_params=params(),
+        name="score",
+    )(rank, *a)
+
+
+def run_attend(rank, bounds, vg, probs, inv_total, block):
+    n = len(vg)
+    return pl.pallas_call(
+        functools.partial(attend_kernel, block),
+        out_shape=[
+            shape_of((n, HEAD_DIM, block), F32),
+            shape_of((n, block, HEAD_DIM), BF16),
+            shape_of((2, n, 1, block), F32),
+        ],
+        in_specs=[SMEM_SPEC] * 2 + [ANY_SPEC] * (n + 1) + [VMEM_SPEC],
+        out_specs=[ANY_SPEC] * 2 + [VMEM_SPEC],
+        scratch_shapes=[
+            pltpu.VMEM((n * block, HEAD_DIM), BF16),
+            pltpu.VMEM((n, block, HEAD_DIM), BF16),
             pltpu.VMEM((HEAD_DIM, n * block), BF16),
             pltpu.VMEM((n, 4 * block, block), BF16),
             pltpu.VMEM((n, HEAD_DIM, block), F32),
             pltpu.VMEM((n, block, HEAD_DIM), BF16),
-            pltpu.VMEM((1, block), F32),
             pltpu.VMEM((HEAD_DIM, block), F32),
-            pltpu.SemaphoreType.DMA((3, n)),
-            pltpu.SemaphoreType.DMA((n,)),
-            pltpu.SemaphoreType.DMA((n, len(OFFSETS))),
+            pltpu.SemaphoreType.DMA((2, n)),
+            pltpu.SemaphoreType.DMA((n, 4)),
             pltpu.SemaphoreType.DMA((2, n)),
         ],
-        compiler_params=pltpu.CompilerParams(vmem_limit_bytes=VMEM_BYTES),
-        name="forward",
-    )(rank, *a)
-
-
-def run_project(rank, g, out, square, block):
-    n = len(g)
-    return pl.pallas_call(
-        functools.partial(project_kernel, block),
-        out_shape=shape_of((2, n * block), F32),
-        in_specs=[SMEM_SPEC] + [ANY_SPEC] * n + [VMEM_SPEC] * 2,
-        out_specs=VMEM_SPEC,
-        scratch_shapes=[
-            pltpu.VMEM((n, block, HEAD_DIM), BF16),
-            pltpu.SemaphoreType.DMA((n,)),
-        ],
-        compiler_params=pltpu.CompilerParams(vmem_limit_bytes=VMEM_BYTES),
-        name="project",
-    )(rank, *g, out, square)
-
-
-def run_backward(rank, bounds, a, g, probs, out_t, inv_total, stats_by_block, block):
+        compiler_params=params(),
+        name="attend",
+    )(rank, bounds, *vg, probs, inv_total)
+
+
+def run_backward(rank, bounds, a, vg, probs, out_t, inv_total, stats, block):
     n = len(a)
     return pl.pallas_call(
         functools.partial(backward_kernel, block),
@@ -469,7 +516,8 @@
         in_specs=[SMEM_SPEC] * 2 + [ANY_SPEC] * (2 * n + 2) + [VMEM_SPEC] * 2,
         out_specs=[ANY_SPEC] * n,
         scratch_shapes=[
-            pltpu.VMEM((3, n * block, HEAD_DIM), BF16),
+            pltpu.VMEM((2, n * block, HEAD_DIM), BF16),
+            pltpu.VMEM((n * block, HEAD_DIM), BF16),
             pltpu.VMEM((n, block, HEAD_DIM), BF16),
             pltpu.VMEM((HEAD_DIM, n * block), BF16),
             pltpu.VMEM((n, 4 * block, block), BF16),
@@ -478,69 +526,51 @@
             pltpu.VMEM((n * block, HEAD_DIM), F32),
             pltpu.VMEM((n * block, HEAD_DIM), F32),
             pltpu.VMEM((HEAD_DIM, block), F32),
-            pltpu.SemaphoreType.DMA((3, n)),
-            pltpu.SemaphoreType.DMA((n,)),
-            pltpu.SemaphoreType.DMA((n, len(OFFSETS))),
+            pltpu.SemaphoreType.DMA((2, n)),
+            pltpu.SemaphoreType.DMA((2, n)),
+            pltpu.SemaphoreType.DMA((n, 4)),
             pltpu.SemaphoreType.DMA((n,)),
             pltpu.SemaphoreType.DMA((n,)),
         ],
-        compiler_params=pltpu.CompilerParams(vmem_limit_bytes=VMEM_BYTES),
+        compiler_params=params(),
         name="backward",
-    )(rank, bounds, *a, *g, probs, out_t, inv_total, stats_by_block)
-
-
-def core_test(rank, a, g, stats):
-    block, n = 512, 8
-    a = [a[m] for m in ORDER]
-    g = [g[m] for m in ORDER]
-    probs, out_t, out, inv_total, square, bounds = run_forward(rank, a, block)
-    s = run_project(rank, g, out, square, block)
-    by = stats.reshape(2, n, block).transpose(1, 0, 2)
-    grads = run_backward(rank, bounds, a, g, probs, out_t, inv_total, by, block)
-    grads = [grads[ORDER.index(m)] for m in range(n)]
-    return [out, s, *grads]
+    )(rank, bounds, *a, *vg, probs, out_t, inv_total, stats)
 
 
 def by_head(queries, keys, values, grad_normed, docs):
     block, width_dev = queries.shape
     n = width_dev // HEAD_DIM
     rank = lax.axis_index("seq").reshape(1).astype(jnp.int32)
-    rows = 3 * block + 16
-    params = pltpu.CompilerParams(vmem_limit_bytes=VMEM_BYTES)
     packed = pl.pallas_call(
         functools.partial(pack_kernel, block),
-        out_shape=[shape_of((rows, HEAD_DIM), BF16)] * n + [shape_of((block, HEAD_DIM), BF16)] * n,
+        out_shape=[shape_of((2 * block + 16, HEAD_DIM), BF16)] * n
+        + [shape_of((2 * block, HEAD_DIM), BF16)] * n,
         in_specs=[SMEM_SPEC] + [ANY_SPEC] * 4 + [VMEM_SPEC],
         out_specs=[VMEM_SPEC] * (2 * n),
         scratch_shapes=[pltpu.SemaphoreType.DMA((4 * n,))],
-        compiler_params=params,
+        compiler_params=params(),
         name="pack",
     )(rank, queries, keys, values, grad_normed, docs.reshape(1, block))
     a = swap_all(packed[:n])
-    first, packed_g = lax.optimization_barrier((a[2], list(packed[n:])))
-    a[2] = first
-    g = swap_all(packed_g)
-
-    probs, out_t, out, inv_total, square, bounds = run_forward(rank, a, block)
-    stats = run_project(rank, g, out, square, block)
-    stats = sum_everywhere(stats)
-
-    home = swap_all(
-        [lax.dynamic_index_in_dim(out, rank[0] ^ m, 0, keepdims=False) for m in ORDER]
-    )
-    home, stats = lax.optimization_barrier((home, stats))
-    stats_by_block = stats.reshape(2, n, block).transpose(1, 0, 2)
-    own_stats = lax.dynamic_slice_in_dim(stats_by_block, rank[0], 1, axis=0)
+    a[1:TIE], vg = lax.optimization_barrier((a[1:TIE], list(packed[n:])))
+    vg = swap_all(vg)
+
+    probs, inv_total, bounds = run_score(rank, a, block)
+    out_t, out, stats = run_attend(rank, bounds, vg, probs, inv_total, block)
+    stats = sum_everywhere(stats.reshape(2, n * block)).reshape(2, n, 1, block)
+
+    home = all_to_all(out)
+    grads = run_backward(rank, bounds, a, vg, probs, out_t, inv_total, stats, block)
+    home, grads = lax.optimization_barrier((home, grads))
+    own_stats = lax.dynamic_index_in_dim(stats[0], rank[0], 0, keepdims=False)
     normed = pl.pallas_call(
         functools.partial(normed_kernel, block),
         out_shape=shape_of((block, width_dev), BF16),
-        in_specs=[SMEM_SPEC] + [VMEM_SPEC] * (n + 1),
+        in_specs=[VMEM_SPEC] * 2,
         out_specs=VMEM_SPEC,
-        compiler_params=params,
+        compiler_params=params(),
         name="normed",
-    )(rank, own_stats, *home)
-
-    grads = run_backward(rank, bounds, a, g, probs, out_t, inv_total, stats_by_block, block)
+    )(own_stats, home)
     back = swap_all(grads)
     grad_outs = pl.pallas_call(
         functools.partial(unpack_kernel, block),
@@ -548,7 +578,7 @@
         in_specs=[SMEM_SPEC] + [ANY_SPEC] * n,
         out_specs=[VMEM_SPEC] * 3,
         scratch_shapes=[pltpu.SemaphoreType.DMA((3 * n,))],
-        compiler_params=params,
+        compiler_params=params(),
         name="unpack",
     )(rank, *back)
     return (normed, *grad_outs)

time: 164 us -> 155 us (0.945)
  waiting for transfers between devices: 66.9 us -> 52.2 us
  Pallas kernels: 54.3 us -> 59.4 us
  starting transfers between devices: 34.6 us -> 38.5 us
  local copies, waits for them, and re-layouts: 4.85 us -> 2.26 us
    ppermute x32 -> x25, waiting for transfers between devices: 64.1 us -> 51.2 us  [swap(): return lax.ppermute(value, 'seq', [(s, s ^ m) for s in range(n)])]
    pallas_call x2, Pallas kernels: 21.3 us -> 25.1 us  [the longest x1 13.9 us: run_score(): pl.pallas_call(functools.partial(score_kernel, block), out_shape=[shape_o...]
    all_to_all x0 -> x1, starting transfers between devices: none -> 3.74 us  [all_to_all(): return lax.all_to_all(value, 'seq', split_axis=0, concat_axis=0, tiled=True)]
    ppermute x3, waiting for transfers between devices: 2.76 us -> 0.94 us  [sum_everywhere(): lax.ppermute(stats, 'head', [(s, (s + d) % heads) for s in range(heads)])]
    ppermute x32 -> x25, starting transfers between devices: 29.7 us -> 30.1 us  [swap(): return lax.ppermute(value, 'seq', [(s, s ^ m) for s in range(n)])]
  transfers between devices with their start and end apart: 35 -> 29, of which waited for: 13 -> 17; matrix products, arithmetic and copies ran while one was open for 2% -> 1% of each run, Pallas kernels for 12% -> 25%
where the time goes in v1:
time: 155 us; the launch traced here: 154 us
  Pallas kernels  59.4 us (38%)
  waiting for transfers between devices  52.2 us (34%)
  starting transfers between devices  38.5 us (25%)
  local copies, waits for them, and re-layouts  2.26 us (1%)
    ppermute x25, waiting for transfers between devices, swap(): return lax.ppermute(value, 'seq', [(s, s ^ m) for s in range(n)])  51.2 us
    ppermute x25, starting transfers between devices, swap(): return lax.ppermute(value, 'seq', [(s, s ^ m) for s in range(n)])  30.1 us
    pallas_call x1, Pallas kernels, run_backward(): pl.pallas_call(functools.partial(backward_kernel, block), out_shape=[shap...  22.7 us
    pallas_call x1, Pallas kernels, run_score(): pl.pallas_call(functools.partial(score_kernel, block), out_shape=[shape_o...  13.9 us
    pallas_call x1, Pallas kernels, run_attend(): pl.pallas_call(functools.partial(attend_kernel, block), out_shape=[shape_...  11.2 us
    pallas_call x1, Pallas kernels, by_head(): pl.pallas_call(functools.partial(pack_kernel, block), out_shape=[shape_of...  5.34 us
    ppermute x3, starting transfers between devices, sum_everywhere(): lax.ppermute(stats, 'head', [(s, (s + d) % heads) for s in range(heads)])  4.67 us
    pallas_call x1, Pallas kernels, by_head(): pl.pallas_call(functools.partial(unpack_kernel, block), out_shape=[shape_...  3.78 us
  transfers between devices with their start and end apart: 29, of which 17 were waited for; matrix products, arithmetic and copies ran while one was open for 1% of the time, Pallas kernels for 25%

profile of v1, /device:TPU:0, one launch (start us, length us, event | category | flops | bytes accessed | tf_op | source)
XLA Modules:
  0.0 154.3 jit_solution(7969540383428083295)
XLA Ops:
  0.6 5.3 %pack.1 = (bf16[1040,128]{1,0:T(8,128)(2,1)}, bf16[1040,128]{1,0:T(8,128)(2,1)}, bf16[1040,128]{1,0:T(8,128)(2,1)}, bf16[1040,128]{1,0:T(8,128)(2,1)}, bf16[1040...) custom-call(s32[1]{0:T(128)} %bitcast.rank_ref, ...), custom_call_target="tpu_custom_call" | custom-call | tf_op jit(solution)/shard_map/pack/pallas_call | solution.py:544
  6.0 0.5 collective-permute-start
  6.5 2.6 %collective-permute-start.1 = (bf16[1040,128]{1,0:T(8,128)(2,1)}, bf16[1040,128]{1,0:T(8,128)(2,1)S(1)}, u32[]{:S(2)}, u32[]{:S(2)}) collective-permute-start(bf16[1040,128]{1,0:T(8,128)(2,1)} %get-tuple-element.58), channel_id=1, source_target_pairs={{0,8},{4,12},{8,0},{12,4},{16,24},{20,28},{24,16},{28,20},{1,9},{5... | collective-permute-start | bytes 798728 | tf_op jit(solution)/shard_map/ppermute | solution.py:433
  9.1 1.5 collective-permute-start.2
  10.6 1.1 collective-permute-start.4
  11.8 2.0 %collective-permute-start.5 = (bf16[1040,128]{1,0:T(8,128)(2,1)}, bf16[1040,128]{1,0:T(8,128)(2,1)S(1)}, u32[]{:S(2)}, u32[]{:S(2)}) collective-permute-start(bf16[1040,128]{1,0:T(8,128)(2,1)} %get-tuple-element.72), channel_id=1, source_target_pairs={{0,20},{4,16},{8,28},{12,24},{16,4},{20,0},{24,12},{28,8},{1,21},{... | collective-permute-start | bytes 798728 | tf_op jit(solution)/shard_map/ppermute | solution.py:433
  13.8 2.7 %collective-permute-done.1.refs_2_ = bf16[1040,128]{1,0:T(8,128)(2,1)S(1)} collective-permute-done((bf16[1040,128]{1,0:T(8,128)(2,1)}, bf16[1040,128]{1,0:T(8,128)(2,1)S(1)}, u32[]{:S(2)}, u32[]{:S(2)}) %collective-permute-start.1) | collective-permute-done | bytes 266272 | tf_op jit(solution)/shard_map/ppermute | solution.py:433
  16.5 1.7 %collective-permute-start.6 = (bf16[1040,128]{1,0:T(8,128)(2,1)}, bf16[1040,128]{1,0:T(8,128)(2,1)S(1)}, u32[]{:S(2)}, u32[]{:S(2)}) collective-permute-start(bf16[1040,128]{1,0:T(8,128)(2,1)} %get-tuple-element.73), channel_id=1, source_target_pairs={{0,28},{4,24},{8,20},{12,16},{16,12},{20,8},{24,4},{28,0},{1,29},{... | collective-permute-start | bytes 798728 | tf_op jit(solution)/shard_map/ppermute | solution.py:433
  18.2 6.0 %collective-permute-done.2.refs_3_ = bf16[1040,128]{1,0:T(8,128)(2,1)S(1)} collective-permute-done((bf16[1040,128]{1,0:T(8,128)(2,1)}, bf16[1040,128]{1,0:T(8,128)(2,1)S(1)}, u32[]{:S(2)}, u32[]{:S(2)}) %collective-permute-start.2) | collective-permute-done | bytes 266272 | tf_op jit(solution)/shard_map/ppermute | solution.py:433
  24.2 0.9 collective-permute-start.8
  25.2 2.4 %collective-permute-done.4.refs_5_ = bf16[1040,128]{1,0:T(8,128)(2,1)S(1)} collective-permute-done((bf16[1040,128]{1,0:T(8,128)(2,1)}, bf16[1040,128]{1,0:T(8,128)(2,1)S(1)}, u32[]{:S(2)}, u32[]{:S(2)}) %collective-permute-start.4) | collective-permute-done | bytes 266272 | tf_op jit(solution)/shard_map/ppermute | solution.py:433
  27.6 1.5 collective-permute-start.9
  29.1 5.7 %collective-permute-done.5.refs_6_ = bf16[1040,128]{1,0:T(8,128)(2,1)S(1)} collective-permute-done((bf16[1040,128]{1,0:T(8,128)(2,1)}, bf16[1040,128]{1,0:T(8,128)(2,1)S(1)}, u32[]{:S(2)}, u32[]{:S(2)}) %collective-permute-start.5) | collective-permute-done | bytes 266272 | tf_op jit(solution)/shard_map/ppermute | solution.py:433
  34.8 3.3 %collective-permute-start.11 = (bf16[1024,128]{1,0:T(8,128)(2,1)}, bf16[1024,128]{1,0:T(8,128)(2,1)S(1)}, u32[]{:S(2)}, u32[]{:S(2)}) collective-permute-start(bf16[1024,128]{1,0:T(8,128)(2,1)} %get-tuple-element.80), channel_id=1, source_target_pairs={{0,12},{4,8},{8,4},{12,0},{16,28},{20,24},{24,20},{28,16},{1,13},{... | collective-permute-start | bytes 786440 | tf_op jit(solution)/shard_map/ppermute | solution.py:433
  38.1 1.0 collective-permute-done.8.refs_2_.refs_10_
  39.1 2.0 %collective-permute-start.13 = (bf16[1024,128]{1,0:T(8,128)(2,1)}, bf16[1024,128]{1,0:T(8,128)(2,1)S(1)}, u32[]{:S(2)}, u32[]{:S(2)}) collective-permute-start(bf16[1024,128]{1,0:T(8,128)(2,1)} %get-tuple-element.82), channel_id=1, source_target_pairs={{0,28},{4,24},{8,20},{12,16},{16,12},{20,8},{24,4},{28,0},{1,29},{... | collective-permute-start | bytes 786440 | tf_op jit(solution)/shard_map/ppermute | solution.py:433
  41.1 13.9 %score.1 = (bf16[8,2048,512]{2,1,0:T(8,128)(2,1)}, f32[8,1,512]{2,1,0:T(1,128)}, s32[3]{0:T(128)}) custom-call(s32[1]{0:T(128)} %bitcast.rank_ref, bf16[1040,128]{1,0:T(8,128)(2,1)} %get-tuple-element.56.refs_0_, bf16[1040,128]{1,0:T(8,128)(2,1)} %copy-done.1, bf16[1040,128]{1,0:T(8,128)(2,1)} %copy-done.2, bf16[1040,128]{1,0:T(8,128)(2,1)} %copy-done.3, ...), custom_call_target="tpu_custom_call" | custom-call | tf_op jit(solution)/shard_map/score/pallas_call | solution.py:461
  55.1 1.4 collective-permute-done.12.refs_6_.refs_14_
  57.2 0.4 copy-done.14
  57.6 11.2 %attend.1 = (f32[8,128,512]{2,1,0:T(8,128)}, bf16[8,512,128]{2,1,0:T(8,128)(2,1)}, f32[2,8,1,512]{3,2,1,0:T(1,128)}) custom-call(s32[1]{0:T(128)} %bitcast.rank_ref, s32[3]{0:T(128)} %get-tuple-element.74.bounds, bf16[1024,128]{1,0:T(8,128)(2,1)} %get-tuple-element.75.refs_0_.refs_8_, bf16[1024,128]{1,0:T(8,128)(2,1)} %copy-done.8, ...), custom_call_target="tpu_custom_call" | custom-call | tf_op jit(solution)/shard_map/attend/pallas_call | solution.py:485
  68.8 0.8 reduce
  69.7 1.2 collective-permute-start.14
  70.9 0.9 collective-permute-done.14
  71.8 3.4 %collective-permute-start.17 = (f32[2,4096]{1,0:T(2,128)S(1)}, f32[2,4096]{1,0:T(2,128)S(1)}, u32[]{:S(2)}, u32[]{:S(2)}) collective-permute-start(f32[2,4096]{1,0:T(2,128)S(1)} %add.25), channel_id=1, source_target_pairs={{0,24},{4,28},{8,16},{12,20},{16,8},{20,12},{24,0},{28,4},{1,25},{... | collective-permute-start | bytes 98312 | tf_op jit(solution)/shard_map/ppermute | solution.py:433
  75.2 0.6 collective-permute-start.16
  75.8 0.7 collective-permute-start.15
  76.5 0.6 collective-permute-done.17
  77.1 2.0 %collective-permute-done.16 = f32[2,4096]{1,0:T(2,128)S(1)} collective-permute-done((f32[2,4096]{1,0:T(2,128)S(1)}, f32[2,4096]{1,0:T(2,128)S(1)}, u32[]{:S(2)}, u32[]{:S(2)}) %collective-permute-start.16) | collective-permute-done | bytes 32800 | tf_op jit(solution)/shard_map/ppermute | solution.py:433
  79.1 0.6 collective-permute-done.15
  79.8 3.7 %collective-permute-start.20 = (f32[2,4096]{1,0:T(2,128)S(1)}, f32[2,4096]{1,0:T(2,128)S(1)}, u32[]{:S(2)}, u32[]{:S(2)}) collective-permute-start(f32[2,4096]{1,0:T(2,128)S(1)} %add_add_fusion.1), channel_id=1, source_target_pairs={{0,3},{1,0},{2,1},{3,2},{4,7},{5,4},{6,5},{7,6},{8,11},{9,8},{10,9... | collective-permute-start | bytes 98312 | tf_op jit(solution)/shard_map/ppermute | solution.py:449
  83.4 1.0 collective-permute-start.18
  84.4 3.7 %all-to-all-start = ((bf16[8,512,128]{2,1,0:T(8,128)(2,1)}), bf16[8,512,128]{2,1,0:T(8,128)(2,1)S(1)}, u32[]{:S(2)}, u32[]{:S(2)}) async-start(bf16[8,512,128]{2,1,0:T(8,128)(2,1)} %get-tuple-element.86), calls=%async_computation | async-start | bytes 2097152 | tf_op jit(solution)/shard_map/all_to_all | solution.py:441
  88.2 0.9 collective-permute-done.18
  89.2 0.7 reshape.25.refs_19_
  89.8 22.7 %backward.1 = (bf16[1536,128]{1,0:T(8,128)(2,1)}, bf16[1536,128]{1,0:T(8,128)(2,1)}, bf16[1536,128]{1,0:T(8,128)(2,1)}, bf16[1536,128]{1,0:T(8,128)(2,1)}, bf16[...) custom-call(s32[1]{0:T(128)} %bitcast.rank_ref, ...), custom_call_target="tpu_custom_call" | custom-call | tf_op jit(solution)/shard_map/backward/pallas_call | solution.py:513
  112.6 0.9 collective-permute-start.22
  113.6 1.8 %collective-permute-start.23 = (bf16[1536,128]{1,0:T(8,128)(2,1)}, bf16[1536,128]{1,0:T(8,128)(2,1)S(1)}, u32[]{:S(2)}, u32[]{:S(2)}) collective-permute-start(bf16[1536,128]{1,0:T(8,128)(2,1)} %get-tuple-element.100), channel_id=1, source_target_pairs={{0,16},{4,20},{8,24},{12,28},{16,0},{20,4},{24,8},{28,12},{1,17},{... | collective-permute-start | bytes 1179656 | tf_op jit(solution)/shard_map/ppermute | solution.py:433
  115.4 0.8 collective-permute-start.24
  116.3 2.3 %collective-permute-start.26 = (bf16[1536,128]{1,0:T(8,128)(2,1)}, bf16[1536,128]{1,0:T(8,128)(2,1)S(1)}, u32[]{:S(2)}, u32[]{:S(2)}) collective-permute-start(bf16[1536,128]{1,0:T(8,128)(2,1)} %get-tuple-element.103), channel_id=1, source_target_pairs={{0,20},{4,16},{8,28},{12,24},{16,4},{20,0},{24,12},{28,8},{1,21},{... | collective-permute-start | bytes 1179656 | tf_op jit(solution)/shard_map/ppermute | solution.py:433
  118.6 6.2 %collective-permute-done.22.refs_2_ = bf16[1536,128]{1,0:T(8,128)(2,1)S(1)} collective-permute-done((bf16[1536,128]{1,0:T(8,128)(2,1)}, bf16[1536,128]{1,0:T(8,128)(2,1)S(1)}, u32[]{:S(2)}, u32[]{:S(2)}) %collective-permute-start.22) | collective-permute-done | bytes 393248 | tf_op jit(solution)/shard_map/ppermute | solution.py:433
  124.8 0.9 collective-permute-start.27
  125.8 0.6 dynamic-slice_bitcast_fusion.stats_ref
  126.4 2.5 %normed.1 = bf16[512,1024]{1,0:T(8,128)(2,1)} custom-call(f32[1,512]{1,0:T(1,128)} %dynamic-slice_bitcast_fusion.stats_ref, bf16[8,512,128]{2,1,0:T(8,128)(2,1)} %copy-done), custom_call_target="tpu_custom_call" | custom-call | tf_op jit(solution)/shard_map/normed/pallas_call | solution.py:566
  128.9 5.3 %collective-permute-done.23.refs_3_ = bf16[1536,128]{1,0:T(8,128)(2,1)S(1)} collective-permute-done((bf16[1536,128]{1,0:T(8,128)(2,1)}, bf16[1536,128]{1,0:T(8,128)(2,1)S(1)}, u32[]{:S(2)}, u32[]{:S(2)}) %collective-permute-start.23) | collective-permute-done | bytes 393248 | tf_op jit(solution)/shard_map/ppermute | solution.py:433
  134.2 6.6 %collective-permute-done.25.refs_5_ = bf16[1536,128]{1,0:T(8,128)(2,1)S(1)} collective-permute-done((bf16[1536,128]{1,0:T(8,128)(2,1)}, bf16[1536,128]{1,0:T(8,128)(2,1)S(1)}, u32[]{:S(2)}, u32[]{:S(2)}) %collective-permute-start.25) | collective-permute-done | bytes 393248 | tf_op jit(solution)/shard_map/ppermute | solution.py:433
  140.8 8.9 %collective-permute-done.26.refs_6_ = bf16[1536,128]{1,0:T(8,128)(2,1)S(1)} collective-permute-done((bf16[1536,128]{1,0:T(8,128)(2,1)}, bf16[1536,128]{1,0:T(8,128)(2,1)S(1)}, u32[]{:S(2)}, u32[]{:S(2)}) %collective-permute-start.26) | collective-permute-done | bytes 393248 | tf_op jit(solution)/shard_map/ppermute | solution.py:433
  149.7 0.5 collective-permute-done.27.refs_7_
  150.4 3.8 %unpack.1 = (bf16[512,1024]{1,0:T(8,128)(2,1)}, bf16[512,1024]{1,0:T(8,128)(2,1)}, bf16[512,1024]{1,0:T(8,128)(2,1)}) custom-call(s32[1]{0:T(128)} %bitcast.rank_ref, bf16[1536,128]{1,0:T(8,128)(2,1)} %get-tuple-element.97.refs_0_, bf16[1536,128]{1,0:T(8,128)(2,1)} %copy-done.15, bf16[1536,128]{1,0:T(8,128)(2,1)} %copy-done.16, ...), custom_call_target="tpu_custom_call" | custom-call | tf_op jit(solution)/shard_map/unpack/pallas_call | solution.py:575
  (67 shorter events, 1.4 us)
Async XLA Ops:
  6.0 5.8 %collective-permute-start = (bf16[1040,128]{1,0:T(8,128)(2,1)}, bf16[1040,128]{1,0:T(8,128)(2,1)S(1)}, u32[]{:S(2)}, u32[]{:S(2)}) collective-permute-start(bf16[1040,128]{1,0:T(8,128)(2,1)} %get-tuple-element.57), channel_id=1, source_target_pairs={{0,4},{4,0},{8,12},{12,8},{16,20},{20,16},{24,28},{28,24},{1,5},{5... | collective-permute-start | bytes 798728 | tf_op jit(solution)/shard_map/ppermute | solution.py:433
  6.5 10.0 %collective-permute-start.1 = (bf16[1040,128]{1,0:T(8,128)(2,1)}, bf16[1040,128]{1,0:T(8,128)(2,1)S(1)}, u32[]{:S(2)}, u32[]{:S(2)}) collective-permute-start(bf16[1040,128]{1,0:T(8,128)(2,1)} %get-tuple-element.58), channel_id=1, source_target_pairs={{0,8},{4,12},{8,0},{12,4},{16,24},{20,28},{24,16},{28,20},{1,9},{5... | collective-permute-start | bytes 798728 | tf_op jit(solution)/shard_map/ppermute | solution.py:433
  9.1 15.2 %collective-permute-start.2 = (bf16[1040,128]{1,0:T(8,128)(2,1)}, bf16[1040,128]{1,0:T(8,128)(2,1)S(1)}, u32[]{:S(2)}, u32[]{:S(2)}) collective-permute-start(bf16[1040,128]{1,0:T(8,128)(2,1)} %get-tuple-element.69), channel_id=1, source_target_pairs={{0,16},{4,20},{8,24},{12,28},{16,0},{20,4},{24,8},{28,12},{1,17},{... | collective-permute-start | bytes 798728 | tf_op jit(solution)/shard_map/ppermute | solution.py:433
  10.6 13.6 %collective-permute-start.3 = (bf16[1040,128]{1,0:T(8,128)(2,1)}, bf16[1040,128]{1,0:T(8,128)(2,1)S(1)}, u32[]{:S(2)}, u32[]{:S(2)}) collective-permute-start(bf16[1040,128]{1,0:T(8,128)(2,1)} %get-tuple-element.70), channel_id=1, source_target_pairs={{0,24},{4,28},{8,16},{12,20},{16,8},{20,12},{24,0},{28,4},{1,25},{... | collective-permute-start | bytes 798728 | tf_op jit(solution)/shard_map/ppermute | solution.py:433
  10.6 16.9 %collective-permute-start.4 = (bf16[1040,128]{1,0:T(8,128)(2,1)}, bf16[1040,128]{1,0:T(8,128)(2,1)S(1)}, u32[]{:S(2)}, u32[]{:S(2)}) collective-permute-start(bf16[1040,128]{1,0:T(8,128)(2,1)} %get-tuple-element.71), channel_id=1, source_target_pairs={{0,12},{4,8},{8,4},{12,0},{16,28},{20,24},{24,20},{28,16},{1,13},{... | collective-permute-start | bytes 798728 | tf_op jit(solution)/shard_map/ppermute | solution.py:433
  11.8 29.3 %copy-start.1 = (bf16[1040,128]{1,0:T(8,128)(2,1)}, bf16[1040,128]{1,0:T(8,128)(2,1)S(1)}, u32[]{:S(2)}) copy-start(bf16[1040,128]{1,0:T(8,128)(2,1)S(1)} %collective-permute-done.refs_1_) | copy-start | bytes 798724
  11.8 23.0 %collective-permute-start.5 = (bf16[1040,128]{1,0:T(8,128)(2,1)}, bf16[1040,128]{1,0:T(8,128)(2,1)S(1)}, u32[]{:S(2)}, u32[]{:S(2)}) collective-permute-start(bf16[1040,128]{1,0:T(8,128)(2,1)} %get-tuple-element.72), channel_id=1, source_target_pairs={{0,20},{4,16},{8,28},{12,24},{16,4},{20,0},{24,12},{28,8},{1,21},{... | collective-permute-start | bytes 798728 | tf_op jit(solution)/shard_map/ppermute | solution.py:433
  16.5 24.6 %copy-start.2 = (bf16[1040,128]{1,0:T(8,128)(2,1)}, bf16[1040,128]{1,0:T(8,128)(2,1)S(1)}, u32[]{:S(2)}) copy-start(bf16[1040,128]{1,0:T(8,128)(2,1)S(1)} %collective-permute-done.1.refs_2_) | copy-start | bytes 798724
  16.5 18.3 %collective-permute-start.6 = (bf16[1040,128]{1,0:T(8,128)(2,1)}, bf16[1040,128]{1,0:T(8,128)(2,1)S(1)}, u32[]{:S(2)}, u32[]{:S(2)}) collective-permute-start(bf16[1040,128]{1,0:T(8,128)(2,1)} %get-tuple-element.73), channel_id=1, source_target_pairs={{0,28},{4,24},{8,20},{12,16},{16,12},{20,8},{24,4},{28,0},{1,29},{... | collective-permute-start | bytes 798728 | tf_op jit(solution)/shard_map/ppermute | solution.py:433
  24.2 16.9 %copy-start.3 = (bf16[1040,128]{1,0:T(8,128)(2,1)}, bf16[1040,128]{1,0:T(8,128)(2,1)S(1)}, u32[]{:S(2)}) copy-start(bf16[1040,128]{1,0:T(8,128)(2,1)S(1)} %collective-permute-done.2.refs_3_) | copy-start | bytes 798724
  24.2 13.8 %collective-permute-start.7 = (bf16[1024,128]{1,0:T(8,128)(2,1)}, bf16[1024,128]{1,0:T(8,128)(2,1)S(1)}, u32[]{:S(2)}, u32[]{:S(2)}) collective-permute-start(bf16[1024,128]{1,0:T(8,128)(2,1)} %get-tuple-element.76), channel_id=1, source_target_pairs={{0,4},{4,0},{8,12},{12,8},{16,20},{20,16},{24,28},{28,24},{1,5},{5... | collective-permute-start | bytes 786440 | tf_op jit(solution)/shard_map/ppermute | solution.py:433
  24.2 16.8 %copy-start.4 = (bf16[1040,128]{1,0:T(8,128)(2,1)}, bf16[1040,128]{1,0:T(8,128)(2,1)S(1)}, u32[]{:S(2)}) copy-start(bf16[1040,128]{1,0:T(8,128)(2,1)S(1)} %collective-permute-done.3.refs_4_) | copy-start | bytes 798724
  24.2 14.8 %collective-permute-start.8 = (bf16[1024,128]{1,0:T(8,128)(2,1)}, bf16[1024,128]{1,0:T(8,128)(2,1)S(1)}, u32[]{:S(2)}, u32[]{:S(2)}) collective-permute-start(bf16[1024,128]{1,0:T(8,128)(2,1)} %get-tuple-element.77), channel_id=1, source_target_pairs={{0,8},{4,12},{8,0},{12,4},{16,24},{20,28},{24,16},{28,20},{1,9},{5... | collective-permute-start | bytes 786440 | tf_op jit(solution)/shard_map/ppermute | solution.py:433
  27.6 13.5 %copy-start.5 = (bf16[1040,128]{1,0:T(8,128)(2,1)}, bf16[1040,128]{1,0:T(8,128)(2,1)S(1)}, u32[]{:S(2)}) copy-start(bf16[1040,128]{1,0:T(8,128)(2,1)S(1)} %collective-permute-done.4.refs_5_) | copy-start | bytes 798724
  27.6 27.4 %collective-permute-start.9 = (bf16[1024,128]{1,0:T(8,128)(2,1)}, bf16[1024,128]{1,0:T(8,128)(2,1)S(1)}, u32[]{:S(2)}, u32[]{:S(2)}) collective-permute-start(bf16[1024,128]{1,0:T(8,128)(2,1)} %get-tuple-element.78), channel_id=1, source_target_pairs={{0,16},{4,20},{8,24},{12,28},{16,0},{20,4},{24,8},{28,12},{1,17},{... | collective-permute-start | bytes 786440 | tf_op jit(solution)/shard_map/ppermute | solution.py:433
  34.8 6.3 %copy-start.6 = (bf16[1040,128]{1,0:T(8,128)(2,1)}, bf16[1040,128]{1,0:T(8,128)(2,1)S(1)}, u32[]{:S(2)}) copy-start(bf16[1040,128]{1,0:T(8,128)(2,1)S(1)} %collective-permute-done.5.refs_6_) | copy-start | bytes 798724
  34.8 20.2 %collective-permute-start.10 = (bf16[1024,128]{1,0:T(8,128)(2,1)}, bf16[1024,128]{1,0:T(8,128)(2,1)S(1)}, u32[]{:S(2)}, u32[]{:S(2)}) collective-permute-start(bf16[1024,128]{1,0:T(8,128)(2,1)} %get-tuple-element.79), channel_id=1, source_target_pairs={{0,24},{4,28},{8,16},{12,20},{16,8},{20,12},{24,0},{28,4},{1,25},{... | collective-permute-start | bytes 786440 | tf_op jit(solution)/shard_map/ppermute | solution.py:433
  34.8 6.3 %copy-start.7 = (bf16[1040,128]{1,0:T(8,128)(2,1)}, bf16[1040,128]{1,0:T(8,128)(2,1)S(1)}, u32[]{:S(2)}) copy-start(bf16[1040,128]{1,0:T(8,128)(2,1)S(1)} %collective-permute-done.6.refs_7_) | copy-start | bytes 798724
  34.8 20.3 %collective-permute-start.11 = (bf16[1024,128]{1,0:T(8,128)(2,1)}, bf16[1024,128]{1,0:T(8,128)(2,1)S(1)}, u32[]{:S(2)}, u32[]{:S(2)}) collective-permute-start(bf16[1024,128]{1,0:T(8,128)(2,1)} %get-tuple-element.80), channel_id=1, source_target_pairs={{0,12},{4,8},{8,4},{12,0},{16,28},{20,24},{24,20},{28,16},{1,13},{... | collective-permute-start | bytes 786440 | tf_op jit(solution)/shard_map/ppermute | solution.py:433
  38.1 18.8 %copy-start.8 = (bf16[1024,128]{1,0:T(8,128)(2,1)}, bf16[1024,128]{1,0:T(8,128)(2,1)S(1)}, u32[]{:S(2)}) copy-start(bf16[1024,128]{1,0:T(8,128)(2,1)S(1)} %collective-permute-done.7.refs_1_.refs_9_) | copy-start | bytes 786436
  38.1 18.4 %collective-permute-start.12 = (bf16[1024,128]{1,0:T(8,128)(2,1)}, bf16[1024,128]{1,0:T(8,128)(2,1)S(1)}, u32[]{:S(2)}, u32[]{:S(2)}) collective-permute-start(bf16[1024,128]{1,0:T(8,128)(2,1)} %get-tuple-element.81), channel_id=1, source_target_pairs={{0,20},{4,16},{8,28},{12,24},{16,4},{20,0},{24,12},{28,8},{1,21},{... | collective-permute-start | bytes 786440 | tf_op jit(solution)/shard_map/ppermute | solution.py:433
  39.1 17.8 %copy-start.9 = (bf16[1024,128]{1,0:T(8,128)(2,1)}, bf16[1024,128]{1,0:T(8,128)(2,1)S(1)}, u32[]{:S(2)}) copy-start(bf16[1024,128]{1,0:T(8,128)(2,1)S(1)} %collective-permute-done.8.refs_2_.refs_10_) | copy-start | bytes 786436
  39.1 17.8 %collective-permute-start.13 = (bf16[1024,128]{1,0:T(8,128)(2,1)}, bf16[1024,128]{1,0:T(8,128)(2,1)S(1)}, u32[]{:S(2)}, u32[]{:S(2)}) collective-permute-start(bf16[1024,128]{1,0:T(8,128)(2,1)} %get-tuple-element.82), channel_id=1, source_target_pairs={{0,28},{4,24},{8,20},{12,16},{16,12},{20,8},{24,4},{28,0},{1,29},{... | collective-permute-start | bytes 786440 | tf_op jit(solution)/shard_map/ppermute | solution.py:433
  55.0 1.8 %copy-start.10 = (bf16[1024,128]{1,0:T(8,128)(2,1)}, bf16[1024,128]{1,0:T(8,128)(2,1)S(1)}, u32[]{:S(2)}) copy-start(bf16[1024,128]{1,0:T(8,128)(2,1)S(1)} %collective-permute-done.9.refs_3_.refs_11_) | copy-start | bytes 786436
  55.0 1.8 %copy-start.11 = (bf16[1024,128]{1,0:T(8,128)(2,1)}, bf16[1024,128]{1,0:T(8,128)(2,1)S(1)}, u32[]{:S(2)}) copy-start(bf16[1024,128]{1,0:T(8,128)(2,1)S(1)} %collective-permute-done.10.refs_4_.refs_12_) | copy-start | bytes 786436
  55.1 1.8 %copy-start.12 = (bf16[1024,128]{1,0:T(8,128)(2,1)}, bf16[1024,128]{1,0:T(8,128)(2,1)S(1)}, u32[]{:S(2)}) copy-start(bf16[1024,128]{1,0:T(8,128)(2,1)S(1)} %collective-permute-done.11.refs_5_.refs_13_) | copy-start | bytes 786436
  69.7 2.0 %collective-permute-start.14 = (f32[2,4096]{1,0:T(2,128)S(1)}, f32[2,4096]{1,0:T(2,128)S(1)}, u32[]{:S(2)}, u32[]{:S(2)}) collective-permute-start(f32[2,4096]{1,0:T(2,128)S(1)} %bitcast.6), channel_id=1, source_target_pairs={{0,4},{4,0},{8,12},{12,8},{16,20},{20,16},{24,28},{28,24},{1,5},{5... | collective-permute-start | bytes 98312 | tf_op jit(solution)/shard_map/ppermute | solution.py:433
  71.8 5.3 %collective-permute-start.17 = (f32[2,4096]{1,0:T(2,128)S(1)}, f32[2,4096]{1,0:T(2,128)S(1)}, u32[]{:S(2)}, u32[]{:S(2)}) collective-permute-start(f32[2,4096]{1,0:T(2,128)S(1)} %add.25), channel_id=1, source_target_pairs={{0,24},{4,28},{8,16},{12,20},{16,8},{20,12},{24,0},{28,4},{1,25},{... | collective-permute-start | bytes 98312 | tf_op jit(solution)/shard_map/ppermute | solution.py:433
  75.2 3.9 %collective-permute-start.16 = (f32[2,4096]{1,0:T(2,128)S(1)}, f32[2,4096]{1,0:T(2,128)S(1)}, u32[]{:S(2)}, u32[]{:S(2)}) collective-permute-start(f32[2,4096]{1,0:T(2,128)S(1)} %add.25), channel_id=1, source_target_pairs={{0,16},{4,20},{8,24},{12,28},{16,0},{20,4},{24,8},{28,12},{1,17},{... | collective-permute-start | bytes 98312 | tf_op jit(solution)/shard_map/ppermute | solution.py:433
  75.8 3.9 %collective-permute-start.15 = (f32[2,4096]{1,0:T(2,128)S(1)}, f32[2,4096]{1,0:T(2,128)S(1)}, u32[]{:S(2)}, u32[]{:S(2)}) collective-permute-start(f32[2,4096]{1,0:T(2,128)S(1)} %add.25), channel_id=1, source_target_pairs={{0,8},{4,12},{8,0},{12,4},{16,24},{20,28},{24,16},{28,20},{1,9},{5... | collective-permute-start | bytes 98312 | tf_op jit(solution)/shard_map/ppermute | solution.py:433
  79.8 8.4 %collective-permute-start.20 = (f32[2,4096]{1,0:T(2,128)S(1)}, f32[2,4096]{1,0:T(2,128)S(1)}, u32[]{:S(2)}, u32[]{:S(2)}) collective-permute-start(f32[2,4096]{1,0:T(2,128)S(1)} %add_add_fusion.1), channel_id=1, source_target_pairs={{0,3},{1,0},{2,1},{3,2},{4,7},{5,4},{6,5},{7,6},{8,11},{9,8},{10,9... | collective-permute-start | bytes 98312 | tf_op jit(solution)/shard_map/ppermute | solution.py:449
  83.4 4.8 %collective-permute-start.19 = (f32[2,4096]{1,0:T(2,128)S(1)}, f32[2,4096]{1,0:T(2,128)S(1)}, u32[]{:S(2)}, u32[]{:S(2)}) collective-permute-start(f32[2,4096]{1,0:T(2,128)S(1)} %add_add_fusion.1), channel_id=1, source_target_pairs={{0,2},{1,3},{2,0},{3,1},{4,6},{5,7},{6,4},{7,5},{8,10},{9,11},{10,... | collective-permute-start | bytes 98312 | tf_op jit(solution)/shard_map/ppermute | solution.py:449
  83.4 5.7 %collective-permute-start.18 = (f32[2,4096]{1,0:T(2,128)S(1)}, f32[2,4096]{1,0:T(2,128)S(1)}, u32[]{:S(2)}, u32[]{:S(2)}) collective-permute-start(f32[2,4096]{1,0:T(2,128)S(1)} %add_add_fusion.1), channel_id=1, source_target_pairs={{0,1},{1,2},{2,3},{3,0},{4,5},{5,6},{6,7},{7,4},{8,9},{9,10},{10,1... | collective-permute-start | bytes 98312 | tf_op jit(solution)/shard_map/ppermute | solution.py:449
  84.4 28.1 %all-to-all-start = ((bf16[8,512,128]{2,1,0:T(8,128)(2,1)}), bf16[8,512,128]{2,1,0:T(8,128)(2,1)S(1)}, u32[]{:S(2)}, u32[]{:S(2)}) async-start(bf16[8,512,128]{2,1,0:T(8,128)(2,1)} %get-tuple-element.86), calls=%async_computation | async-start | bytes 2097152 | tf_op jit(solution)/shard_map/all_to_all | solution.py:441
  112.5 13.9 %copy-start = (bf16[8,512,128]{2,1,0:T(8,128)(2,1)}, bf16[8,512,128]{2,1,0:T(8,128)(2,1)S(1)}, u32[]{:S(2)}) copy-start(bf16[8,512,128]{2,1,0:T(8,128)(2,1)S(1)} %all-to-all-done.home_ref) | copy-start | bytes 3145732
  112.5 3.8 %collective-permute-start.21 = (bf16[1536,128]{1,0:T(8,128)(2,1)}, bf16[1536,128]{1,0:T(8,128)(2,1)S(1)}, u32[]{:S(2)}, u32[]{:S(2)}) collective-permute-start(bf16[1536,128]{1,0:T(8,128)(2,1)} %get-tuple-element.98), channel_id=1, source_target_pairs={{0,4},{4,0},{8,12},{12,8},{16,20},{20,16},{24,28},{28,24},{1,5},{5... | collective-permute-start | bytes 1179656 | tf_op jit(solution)/shard_map/ppermute | solution.py:433
  112.6 12.2 %collective-permute-start.22 = (bf16[1536,128]{1,0:T(8,128)(2,1)}, bf16[1536,128]{1,0:T(8,128)(2,1)S(1)}, u32[]{:S(2)}, u32[]{:S(2)}) collective-permute-start(bf16[1536,128]{1,0:T(8,128)(2,1)} %get-tuple-element.99), channel_id=1, source_target_pairs={{0,8},{4,12},{8,0},{12,4},{16,24},{20,28},{24,16},{28,20},{1,9},{5... | collective-permute-start | bytes 1179656 | tf_op jit(solution)/shard_map/ppermute | solution.py:433
  113.6 20.6 %collective-permute-start.23 = (bf16[1536,128]{1,0:T(8,128)(2,1)}, bf16[1536,128]{1,0:T(8,128)(2,1)S(1)}, u32[]{:S(2)}, u32[]{:S(2)}) collective-permute-start(bf16[1536,128]{1,0:T(8,128)(2,1)} %get-tuple-element.100), channel_id=1, source_target_pairs={{0,16},{4,20},{8,24},{12,28},{16,0},{20,4},{24,8},{28,12},{1,17},{... | collective-permute-start | bytes 1179656 | tf_op jit(solution)/shard_map/ppermute | solution.py:433
  115.4 18.8 %collective-permute-start.24 = (bf16[1536,128]{1,0:T(8,128)(2,1)}, bf16[1536,128]{1,0:T(8,128)(2,1)S(1)}, u32[]{:S(2)}, u32[]{:S(2)}) collective-permute-start(bf16[1536,128]{1,0:T(8,128)(2,1)} %get-tuple-element.101), channel_id=1, source_target_pairs={{0,24},{4,28},{8,16},{12,20},{16,8},{20,12},{24,0},{28,4},{1,25},{... | collective-permute-start | bytes 1179656 | tf_op jit(solution)/shard_map/ppermute | solution.py:433
  116.2 24.6 %collective-permute-start.25 = (bf16[1536,128]{1,0:T(8,128)(2,1)}, bf16[1536,128]{1,0:T(8,128)(2,1)S(1)}, u32[]{:S(2)}, u32[]{:S(2)}) collective-permute-start(bf16[1536,128]{1,0:T(8,128)(2,1)} %get-tuple-element.102), channel_id=1, source_target_pairs={{0,12},{4,8},{8,4},{12,0},{16,28},{20,24},{24,20},{28,16},{1,13},{... | collective-permute-start | bytes 1179656 | tf_op jit(solution)/shard_map/ppermute | solution.py:433
  116.3 33.9 %copy-start.15 = (bf16[1536,128]{1,0:T(8,128)(2,1)}, bf16[1536,128]{1,0:T(8,128)(2,1)S(1)}, u32[]{:S(2)}) copy-start(bf16[1536,128]{1,0:T(8,128)(2,1)S(1)} %collective-permute-done.21.refs_1_) | copy-start | bytes 1179652
  116.3 33.3 %collective-permute-start.26 = (bf16[1536,128]{1,0:T(8,128)(2,1)}, bf16[1536,128]{1,0:T(8,128)(2,1)S(1)}, u32[]{:S(2)}, u32[]{:S(2)}) collective-permute-start(bf16[1536,128]{1,0:T(8,128)(2,1)} %get-tuple-element.103), channel_id=1, source_target_pairs={{0,20},{4,16},{8,28},{12,24},{16,4},{20,0},{24,12},{28,8},{1,21},{... | collective-permute-start | bytes 1179656 | tf_op jit(solution)/shard_map/ppermute | solution.py:433
  124.8 25.4 %copy-start.16 = (bf16[1536,128]{1,0:T(8,128)(2,1)}, bf16[1536,128]{1,0:T(8,128)(2,1)S(1)}, u32[]{:S(2)}) copy-start(bf16[1536,128]{1,0:T(8,128)(2,1)S(1)} %collective-permute-done.22.refs_2_) | copy-start | bytes 1179652
  124.8 25.4 %collective-permute-start.27 = (bf16[1536,128]{1,0:T(8,128)(2,1)}, bf16[1536,128]{1,0:T(8,128)(2,1)}, u32[]{:S(2)}, u32[]{:S(2)}) collective-permute-start(bf16[1536,128]{1,0:T(8,128)(2,1)} %get-tuple-element.104), channel_id=1, source_target_pairs={{0,28},{4,24},{8,20},{12,16},{16,12},{20,8},{24,4},{28,0},{1,29},{... | collective-permute-start | bytes 1179656 | tf_op jit(solution)/shard_map/ppermute | solution.py:433
  134.2 16.1 %copy-start.17 = (bf16[1536,128]{1,0:T(8,128)(2,1)}, bf16[1536,128]{1,0:T(8,128)(2,1)S(1)}, u32[]{:S(2)}) copy-start(bf16[1536,128]{1,0:T(8,128)(2,1)S(1)} %collective-permute-done.23.refs_3_) | copy-start | bytes 1179652
  134.2 16.1 %copy-start.18 = (bf16[1536,128]{1,0:T(8,128)(2,1)}, bf16[1536,128]{1,0:T(8,128)(2,1)S(1)}, u32[]{:S(2)}) copy-start(bf16[1536,128]{1,0:T(8,128)(2,1)S(1)} %collective-permute-done.24.refs_4_) | copy-start | bytes 1179652
  140.8 9.4 %copy-start.19 = (bf16[1536,128]{1,0:T(8,128)(2,1)}, bf16[1536,128]{1,0:T(8,128)(2,1)S(1)}, u32[]{:S(2)}) copy-start(bf16[1536,128]{1,0:T(8,128)(2,1)S(1)} %collective-permute-done.25.refs_5_) | copy-start | bytes 1179652
  149.7 0.7 copy-start.20
  (2 other events, 1.4 us)

commit v2 on v1

--- a/solution.py
+++ b/solution.py
@@ -90,6 +90,21 @@
     pl.when(far)(lambda: act(0))
 
 
+def by_rows(i, act):
+    if isinstance(i, int):
+        act(0 if i >= 4 else max(1, 3 - i))
+        return
+    pl.when(i == 0)(lambda: act(3))
+    pl.when(i == 1)(lambda: act(2))
+    pl.when((i == 2) | (i == 3))(lambda: act(1))
+    pl.when(i >= 4)(lambda: act(0))
+
+
+def move_probs(source, target, sems, block, i, slot):
+    rows = slice(slot * block, 4 * block)
+    return pltpu.make_async_copy(source.at[i, rows, :], target.at[i, rows, :], sems.at[i])
+
+
 def doc_starts(i, block, bounds):
     pos = i * block + lax.broadcasted_iota(jnp.int32, (1, block), 1)
     start = jnp.zeros((1, block), jnp.int32)
@@ -138,11 +153,7 @@
 
     gain = math.log2(math.e) / math.sqrt(HEAD_DIM)
 
-    def prob_out(i, slot):
-        rows = slice(slot * block, (slot + 1) * block)
-        return pltpu.make_async_copy(
-            prob.at[i, rows, :], prob_ref.at[i, rows, :], prob_sems.at[i, slot]
-        )
+    prob_out = functools.partial(move_probs, prob, prob_ref, prob_sems, block)
 
     def one_block(i, carry):
         own_rows = pl.ds(pl.multiple_of(i * block, block), block)
@@ -175,19 +186,15 @@
                 prob[i, row : row + size, :] = p.astype(BF16)
                 total = line if total is None else total + line
             inv_ref[i] = 1.0 / total
-            for slot in slots_of(near, far):
-                prob_out(i, slot).start()
 
         for_each_reach(i, block, bounds, body, True)
+        by_rows(i, lambda slot: prob_out(i, slot).start())
         return carry
 
     lax.fori_loop(0, n, one_block, 0)
 
-    def finish(i, carry):
-        each_slot(i, block, bounds, lambda slot: prob_out(i, slot).wait())
-        return carry
-
-    lax.fori_loop(0, n, finish, 0)
+    for i in range(n):
+        by_rows(i, lambda slot: prob_out(i, slot).wait())
 
 
 def value_in(vg_ref, t, block, values, sems):
@@ -202,21 +209,13 @@
     return pltpu.make_async_copy(vg_ref.at[block:, :], cot.at[t], sems.at[1, t])
 
 
-def fetch_probs(n, block, bounds, prob_ref, prob, sems):
-    def prob_in(i, slot):
-        rows = slice(slot * block, (slot + 1) * block)
-        return pltpu.make_async_copy(prob_ref.at[i, rows, :], prob.at[i, rows, :], sems.at[i, slot])
-
-    return prob_in
-
-
 def attend_kernel(block, rank_ref, bounds, *refs):
     n = 8
     vg_refs = refs[:n]
     prob_ref, inv_ref, out_t_ref, out_ref, stats_ref = refs[n : n + 5]
     values, cot, val_t, prob, out_t_keep, out_keep, acc, vg_sems, prob_sems, out_sems = refs[n + 5 :]
     vg_ref = vg_refs[0]
-    prob_in = fetch_probs(n, block, bounds, prob_ref, prob, prob_sems)
+    prob_in = functools.partial(move_probs, prob_ref, prob, prob_sems, block)
 
     def rows_out(i):
         return (
@@ -228,7 +227,7 @@
         value_in(ref, rank_ref[0] ^ m, block, values, vg_sems).start()
         cot_in(ref, rank_ref[0] ^ m, block, cot, vg_sems).start()
     for t in range(n):
-        each_slot(t, block, bounds, lambda slot: prob_in(t, slot).start())
+        by_rows(t, lambda slot: prob_in(t, slot).start())
     ones = jnp.ones((16, HEAD_DIM), BF16)
 
     def one_block(i, carry):
@@ -237,31 +236,33 @@
         val_t[:, own_rows] = values[own_rows, :].T
 
         def body(near, far, masked):
-            for slot in slots_of(near, far):
-                prob_in(i, slot).wait()
             out = None
             for row, key, size, own in pieces(i, near, far, block):
                 term = nn_dot(val_t[:, pl.ds(key, size)], prob[i, row : row + size, :])
                 out = term if out is None else out + term
             acc[...] = out
 
+        by_rows(i, lambda slot: prob_in(i, slot).wait())
         for_each_reach(i, block, bounds, body, False)
 
         out_t = acc[...] * inv_ref[i]
         out_t_keep[i] = out_t
-        out = out_t.T
+        rows_out(i)[0].start()
+        stats_ref[0:1, own_rows] = jnp.sum(out_t * out_t, axis=0, keepdims=True)
+        return carry
+
+    lax.fori_loop(0, n, one_block, 0)
+
+    for i in range(n):
+        cols = slice(i * block, (i + 1) * block)
+        out = out_t_keep[i].T
         out_keep[i] = out.astype(BF16)
-        for copy in rows_out(i):
-            copy.start()
-        stats_ref[0, i] = jnp.sum(out_t * out_t, axis=0, keepdims=True)
+        rows_out(i)[1].start()
         cot_in(vg_ref, i, block, cot, vg_sems).wait()
         x = cot[i].astype(F32) * out
         high = x.astype(BF16)
         low = (x - high.astype(F32)).astype(BF16)
-        stats_ref[1, i] = (nt_dot(ones, high) + nt_dot(ones, low))[0:1]
-        return carry
-
-    lax.fori_loop(0, n, one_block, 0)
+        stats_ref[1:2, cols] = (nt_dot(ones, high) + nt_dot(ones, low))[0:1]
 
     def finish(i, carry):
         for copy in rows_out(i):
@@ -281,7 +282,8 @@
     held, values, cot, key_t, prob, out_t_keep, stage, grad_k, grad_v, acc = refs[
         2 * n + 5 : 2 * n + 15
     ]
-    sems, vg_sems, prob_sems, out_sems, d_sems = refs[2 * n + 15 :]
+    dattn_t, dattn_keep, deltas = refs[2 * n + 15 : 2 * n + 18]
+    sems, vg_sems, prob_sems, out_sems, d_sems = refs[2 * n + 18 :]
     rank = rank_ref[0]
     scale = 1.0 / math.sqrt(HEAD_DIM)
     width = HEADS * HEAD_DIM
@@ -289,9 +291,17 @@
     def out_in(i):
         return pltpu.make_async_copy(out_t_ref.at[i], out_t_keep.at[i], out_sems.at[i])
 
-    prob_in = fetch_probs(n, block, bounds, prob_ref, prob, prob_sems)
+    def prob_in(i, slot):
+        rows = slice(slot * block, (slot + 1) * block)
+        return pltpu.make_async_copy(
+            prob_ref.at[i, rows, :], prob.at[i, rows, :], prob_sems.at[i, slot]
+        )
+
     for m, ref in zip(ORDER, vg_refs):
         cot_in(ref, rank ^ m, block, cot, vg_sems).start()
+    for i in reversed(range(n)):
+        out_in(i).start()
+    for m, ref in zip(ORDER, vg_refs):
         value_in(ref, rank ^ m, block, values, vg_sems).start()
     for m, ref in zip(ORDER, a_refs):
         for copy in parts_in(ref, rank ^ m, block, held, sems):
@@ -299,7 +309,6 @@
 
     def fetch(step, carry):
         i = n - 1 - step
-        out_in(i).start()
         each_slot(i, block, bounds, lambda slot: prob_in(i, slot).start())
         return carry
 
@@ -307,18 +316,26 @@
     grad_k[...] = jnp.zeros_like(grad_k)
     grad_v[...] = jnp.zeros_like(grad_v)
 
+    for i in reversed(range(n)):
+        cols = slice(i * block, (i + 1) * block)
+        cot_in(vg_ref, i, block, cot, vg_sems).wait()
+        out_in(i).wait()
+        inv_rms = lax.rsqrt(stats_ref[0:1, cols] / width + norm_eps)
+        coef = inv_rms * inv_rms * inv_rms * stats_ref[1:2, cols] / width
+        out_t = out_t_keep[i]
+        rows_t = (inv_rms * cot[i].astype(F32).T - out_t * coef) * inv_ref[i]
+        rounded = rows_t.astype(BF16)
+        dattn_t[:, cols] = rounded
+        rows_f = rounded.astype(F32)
+        deltas[0:1, cols] = jnp.sum(rows_f * out_t, axis=0, keepdims=True)
+        dattn_keep[cols, :] = rows_f.T.astype(BF16)
+
     def one_block(step, carry):
         i = n - 1 - step
-        cot_in(vg_ref, i, block, cot, vg_sems).wait()
-        out_in(i).wait()
-        inv_rms = lax.rsqrt(stats_ref[0, i] / width + norm_eps)
-        coef = inv_rms * inv_rms * inv_rms * stats_ref[1, i] / width
-        out_t = out_t_keep[i]
-        dattn_t = (inv_rms * cot[i].astype(F32).T - out_t * coef) * inv_ref[i]
-        dattn_tb = dattn_t.astype(BF16)
-        dattn_f = dattn_tb.astype(F32)
-        delta = jnp.sum(dattn_f * out_t, axis=0, keepdims=True)
-        dattn = dattn_f.T.astype(BF16)
+        own_rows = pl.ds(pl.multiple_of(i * block, block), block)
+        dattn_tb = dattn_t[:, own_rows]
+        dattn = dattn_keep[own_rows, :]
+        delta = deltas[0:1, own_rows]
         for first in sorted(set(FIRST_USE)):
 
             @pl.when(i == first)
@@ -331,7 +348,6 @@
                         cols = slice(t * block, (t + 1) * block)
                         key_t[:, cols] = held[1, cols, :].T
 
-        own_rows = pl.ds(pl.multiple_of(i * block, block), block)
         query = held[0, own_rows, :]
 
         def body(near, far, masked):
@@ -365,52 +381,87 @@
         pltpu.make_async_copy(stage.at[0], ref, d_sems.at[m]).wait()
 
 
-def pack_kernel(block, rank_ref, q_ref, k_ref, v_ref, g_ref, doc_ref, *refs):
-    n = 8
-    a_refs, vg_refs, sems = refs[:n], refs[n : 2 * n], refs[2 * n]
-    parts = []
-    for m, ref, other in zip(ORDER, a_refs, vg_refs):
-        cols = pl.ds(pl.multiple_of((rank_ref[0] ^ m) * HEAD_DIM, HEAD_DIM), HEAD_DIM)
-        parts.append((q_ref.at[:, cols], ref.at[0:block, :]))
-        parts.append((k_ref.at[:, cols], ref.at[block : 2 * block, :]))
-        parts.append((v_ref.at[:, cols], other.at[0:block, :]))
-        parts.append((g_ref.at[:, cols], other.at[block:, :]))
+def own_cols(rank_ref, m):
+    return pl.ds(pl.multiple_of((rank_ref[0] ^ m) * HEAD_DIM, HEAD_DIM), HEAD_DIM)
+
+
+def start_all(pairs, sems):
     copies = [
         pltpu.make_async_copy(source, target, sems.at[number])
-        for number, (source, target) in enumerate(parts)
+        for number, (source, target) in enumerate(pairs)
     ]
     for copy in copies:
         copy.start()
+    return copies
+
+
+def pass_on(arrivals, keep, refs, sems):
+    copies = []
+    for index, ref in enumerate(refs):
+        for copy in arrivals[index]:
+            copy.wait()
+        copies.append(pltpu.make_async_copy(keep.at[index], ref, sems.at[index]))
+        copies[-1].start()
+    for copy in copies:
+        copy.wait()
+
+
+def gather_columns(block, rank_ref, top_ref, low_ref, keep, sems):
+    arrivals = []
+    for index, m in enumerate(ORDER):
+        cols = own_cols(rank_ref, m)
+        pairs = [
+            (top_ref.at[:, cols], keep.at[index, 0:block, :]),
+            (low_ref.at[:, cols], keep.at[index, block : 2 * block, :]),
+        ]
+        arrivals.append(start_all(pairs, sems.at[index]))
+    return arrivals
+
+
+def pack_scores_kernel(block, rank_ref, q_ref, k_ref, doc_ref, *refs):
+    n = 8
+    a_refs, keep, sems, out_sems = refs[:n], *refs[n:]
+    arrivals = gather_columns(block, rank_ref, q_ref, k_ref, keep, sems)
     row = lax.broadcasted_iota(jnp.int32, (16, HEAD_DIM), 0)
     ids = jnp.full((16, HEAD_DIM), 4.0, F32)
     for k in range(block // HEAD_DIM):
         part = doc_ref[0:1, k * HEAD_DIM : (k + 1) * HEAD_DIM].astype(F32)
         ids = jnp.where(row == k, part, ids)
-    for ref in a_refs:
-        ref[2 * block :, :] = ids.astype(BF16)
+    for index in range(n):
+        keep[index, 2 * block :, :] = ids.astype(BF16)
+    pass_on(arrivals, keep, a_refs, out_sems)
+
+
+def pack_values_kernel(block, rank_ref, v_ref, g_ref, *refs):
+    n = 8
+    vg_refs, keep, sems, out_sems = refs[:n], *refs[n:]
+    pass_on(gather_columns(block, rank_ref, v_ref, g_ref, keep, sems), keep, vg_refs, out_sems)
+
+
+def unpack_kernel(block, rank_ref, *refs):
+    n = 8
+    d_refs, outs, keep, sems, out_sems = refs[:n], refs[n : n + 3], *refs[n + 3 :]
+    arrivals = []
+    for part in range(3):
+        rows = slice(part * block, (part + 1) * block)
+        pairs = [
+            (ref.at[rows, :], keep.at[part, :, own_cols(rank_ref, m)])
+            for m, ref in zip(ORDER, d_refs)
+        ]
+        arrivals.append(start_all(pairs, sems.at[part]))
+    copies = []
+    for part, out in enumerate(outs):
+        for copy in arrivals[part]:
+            copy.wait()
+        copies.append(pltpu.make_async_copy(keep.at[part], out, out_sems.at[part]))
+        copies[-1].start()
     for copy in copies:
         copy.wait()
 
 
-def unpack_kernel(block, rank_ref, *refs):
-    n = 8
-    d_refs, outs, sems = refs[:n], refs[n : n + 3], refs[n + 3]
-    copies = []
-    for m, ref in zip(ORDER, d_refs):
-        cols = pl.ds(pl.multiple_of((rank_ref[0] ^ m) * HEAD_DIM, HEAD_DIM), HEAD_DIM)
-        for part, out in enumerate(outs):
-            rows = slice(part * block, (part + 1) * block)
-            copies.append(
-                pltpu.make_async_copy(ref.at[rows, :], out.at[:, cols], sems.at[len(copies)])
-            )
-    for copy in copies:
-        copy.start()
-    for copy in copies:
-        copy.wait()
-
-
-def normed_kernel(block, stats_ref, home_ref, out_ref):
-    inv_rms = lax.rsqrt(stats_ref[...] / (HEADS * HEAD_DIM) + norm_eps)
+def normed_kernel(block, rank_ref, stats_ref, home_ref, out_ref):
+    own_rows = pl.ds(pl.multiple_of(rank_ref[0] * block, block), block)
+    inv_rms = lax.rsqrt(stats_ref[0:1, own_rows] / (HEADS * HEAD_DIM) + norm_eps)
     spread = jnp.broadcast_to(inv_rms, (HEAD_DIM, block)).T
     for h in range(home_ref.shape[0]):
         cols = slice(h * HEAD_DIM, (h + 1) * HEAD_DIM)
@@ -473,7 +524,7 @@
             pltpu.VMEM((n, 4 * block, block), BF16),
             pltpu.SemaphoreType.DMA((2, n)),
             pltpu.SemaphoreType.DMA((n,)),
-            pltpu.SemaphoreType.DMA((n, 4)),
+            pltpu.SemaphoreType.DMA((n,)),
         ],
         compiler_params=params(),
         name="score",
@@ -487,7 +538,7 @@
         out_shape=[
             shape_of((n, HEAD_DIM, block), F32),
             shape_of((n, block, HEAD_DIM), BF16),
-            shape_of((2, n, 1, block), F32),
+            shape_of((2, n * block), F32),
         ],
         in_specs=[SMEM_SPEC] * 2 + [ANY_SPEC] * (n + 1) + [VMEM_SPEC],
         out_specs=[ANY_SPEC] * 2 + [VMEM_SPEC],
@@ -500,7 +551,7 @@
             pltpu.VMEM((n, block, HEAD_DIM), BF16),
             pltpu.VMEM((HEAD_DIM, block), F32),
             pltpu.SemaphoreType.DMA((2, n)),
-            pltpu.SemaphoreType.DMA((n, 4)),
+            pltpu.SemaphoreType.DMA((n,)),
             pltpu.SemaphoreType.DMA((2, n)),
         ],
         compiler_params=params(),
@@ -526,6 +577,9 @@
             pltpu.VMEM((n * block, HEAD_DIM), F32),
             pltpu.VMEM((n * block, HEAD_DIM), F32),
             pltpu.VMEM((HEAD_DIM, block), F32),
+            pltpu.VMEM((HEAD_DIM, n * block), BF16),
+            pltpu.VMEM((n * block, HEAD_DIM), BF16),
+            pltpu.VMEM((1, n * block), F32),
             pltpu.SemaphoreType.DMA((2, n)),
             pltpu.SemaphoreType.DMA((2, n)),
             pltpu.SemaphoreType.DMA((n, 4)),
@@ -541,43 +595,62 @@
     block, width_dev = queries.shape
     n = width_dev // HEAD_DIM
     rank = lax.axis_index("seq").reshape(1).astype(jnp.int32)
-    packed = pl.pallas_call(
-        functools.partial(pack_kernel, block),
-        out_shape=[shape_of((2 * block + 16, HEAD_DIM), BF16)] * n
-        + [shape_of((2 * block, HEAD_DIM), BF16)] * n,
-        in_specs=[SMEM_SPEC] + [ANY_SPEC] * 4 + [VMEM_SPEC],
-        out_specs=[VMEM_SPEC] * (2 * n),
-        scratch_shapes=[pltpu.SemaphoreType.DMA((4 * n,))],
+    a = pl.pallas_call(
+        functools.partial(pack_scores_kernel, block),
+        out_shape=[shape_of((2 * block + 16, HEAD_DIM), BF16)] * n,
+        in_specs=[SMEM_SPEC] + [ANY_SPEC] * 2 + [VMEM_SPEC],
+        out_specs=[ANY_SPEC] * n,
+        scratch_shapes=[
+            pltpu.VMEM((n, 2 * block + 16, HEAD_DIM), BF16),
+            pltpu.SemaphoreType.DMA((n, 2)),
+            pltpu.SemaphoreType.DMA((n,)),
+        ],
         compiler_params=params(),
-        name="pack",
-    )(rank, queries, keys, values, grad_normed, docs.reshape(1, block))
-    a = swap_all(packed[:n])
-    a[1:TIE], vg = lax.optimization_barrier((a[1:TIE], list(packed[n:])))
+        name="pack_scores",
+    )(rank, queries, keys, docs.reshape(1, block))
+    a = swap_all(a)
+    a[1:TIE], values, grad_normed = lax.optimization_barrier((a[1:TIE], values, grad_normed))
+    vg = pl.pallas_call(
+        functools.partial(pack_values_kernel, block),
+        out_shape=[shape_of((2 * block, HEAD_DIM), BF16)] * n,
+        in_specs=[SMEM_SPEC] + [ANY_SPEC] * 2,
+        out_specs=[ANY_SPEC] * n,
+        scratch_shapes=[
+            pltpu.VMEM((n, 2 * block, HEAD_DIM), BF16),
+            pltpu.SemaphoreType.DMA((n, 2)),
+            pltpu.SemaphoreType.DMA((n,)),
+        ],
+        compiler_params=params(),
+        name="pack_values",
+    )(rank, values, grad_normed)
     vg = swap_all(vg)
 
     probs, inv_total, bounds = run_score(rank, a, block)
     out_t, out, stats = run_attend(rank, bounds, vg, probs, inv_total, block)
-    stats = sum_everywhere(stats.reshape(2, n * block)).reshape(2, n, 1, block)
+    stats = sum_everywhere(stats)
 
     home = all_to_all(out)
     grads = run_backward(rank, bounds, a, vg, probs, out_t, inv_total, stats, block)
     home, grads = lax.optimization_barrier((home, grads))
-    own_stats = lax.dynamic_index_in_dim(stats[0], rank[0], 0, keepdims=False)
     normed = pl.pallas_call(
         functools.partial(normed_kernel, block),
         out_shape=shape_of((block, width_dev), BF16),
-        in_specs=[VMEM_SPEC] * 2,
+        in_specs=[SMEM_SPEC] + [VMEM_SPEC] * 2,
         out_specs=VMEM_SPEC,
         compiler_params=params(),
         name="normed",
-    )(own_stats, home)
+    )(rank, stats, home)
     back = swap_all(grads)
     grad_outs = pl.pallas_call(
         functools.partial(unpack_kernel, block),
         out_shape=[shape_of((block, width_dev), BF16)] * 3,
         in_specs=[SMEM_SPEC] + [ANY_SPEC] * n,
-        out_specs=[VMEM_SPEC] * 3,
-        scratch_shapes=[pltpu.SemaphoreType.DMA((3 * n,))],
+        out_specs=[ANY_SPEC] * 3,
+        scratch_shapes=[
+            pltpu.VMEM((3, block, width_dev), BF16),
+            pltpu.SemaphoreType.DMA((3, n)),
+            pltpu.SemaphoreType.DMA((3,)),
+        ],
         compiler_params=params(),
         name="unpack",
     )(rank, *back)

time: 155 us -> 150 us (0.968)
  Pallas kernels: 59.4 us -> 57.5 us
    pallas_call x1 -> x2, Pallas kernels: 5.34 us -> 5.8 us  [the longest x1 3.25 us: by_head(): pl.pallas_call(functools.partial(pack_scores_kernel, block), out_shape=[s...]
  transfers between devices with their start and end apart: 29 -> 29, of which waited for: 17 -> 17; matrix products, arithmetic and copies ran while one was open for 1% -> 0% of each run, Pallas kernels for 25% -> 27%
where the time goes in v2:
time: 150 us
  Pallas kernels  57.5 us (38%)
  waiting for transfers between devices  51.2 us (34%)
  starting transfers between devices  37.1 us (25%)
  local copies, waits for them, and re-layouts  1.5 us (1%)
    ppermute x25, waiting for transfers between devices, swap(): return lax.ppermute(value, 'seq', [(s, s ^ m) for s in range(n)])  50.3 us
    ppermute x25, starting transfers between devices, swap(): return lax.ppermute(value, 'seq', [(s, s ^ m) for s in range(n)])  28.7 us
    pallas_call x1, Pallas kernels, run_backward(): pl.pallas_call(functools.partial(backward_kernel, block), out_shape=[shap...  22 us
    pallas_call x1, Pallas kernels, run_score(): pl.pallas_call(functools.partial(score_kernel, block), out_shape=[shape_o...  13.7 us
    pallas_call x1, Pallas kernels, run_attend(): pl.pallas_call(functools.partial(attend_kernel, block), out_shape=[shape_...  10.3 us
    ppermute x3, starting transfers between devices, sum_everywhere(): lax.ppermute(stats, 'head', [(s, (s + d) % heads) for s in range(heads)])  4.65 us
    all_to_all x1, starting transfers between devices, all_to_all(): return lax.all_to_all(value, 'seq', split_axis=0, concat_axis=0, tiled=True)  3.74 us
    pallas_call x1, Pallas kernels, by_head(): pl.pallas_call(functools.partial(pack_scores_kernel, block), out_shape=[s...  3.25 us
  transfers between devices with their start and end apart: 29, of which 17 were waited for; matrix products, arithmetic and copies ran while one was open for 0% of the time, Pallas kernels for 27%

profile of v2, /device:TPU:0, one launch (start us, length us, event | category | flops | bytes accessed | tf_op | source)
XLA Modules:
  0.0 149.9 jit_solution(16626300437819518661)
XLA Ops:
  0.6 3.2 %pack_scores.1 = (bf16[1040,128]{1,0:T(8,128)(2,1)}, bf16[1040,128]{1,0:T(8,128)(2,1)}, bf16[1040,128]{1,0:T(8,128)(2,1)}, bf16[1040,128]{1,0:T(8,128)(2,1)}, bf...) custom-call(s32[1]{0:T(128)} %bitcast.rank_ref, ...), custom_call_target="tpu_custom_call" | custom-call | tf_op jit(solution)/shard_map/pack_scores/pallas_call | solution.py:598
  3.9 0.5 collective-permute-start
  4.4 2.6 %collective-permute-start.1 = (bf16[1040,128]{1,0:T(8,128)(2,1)}, bf16[1040,128]{1,0:T(8,128)(2,1)S(1)}, u32[]{:S(2)}, u32[]{:S(2)}) collective-permute-start(bf16[1040,128]{1,0:T(8,128)(2,1)} %get-tuple-element.52), channel_id=1, source_target_pairs={{0,8},{4,12},{8,0},{12,4},{16,24},{20,28},{24,16},{28,20},{1,9},{5... | collective-permute-start | bytes 798728 | tf_op jit(solution)/shard_map/ppermute | solution.py:484
  7.0 1.5 %collective-permute-start.2 = (bf16[1040,128]{1,0:T(8,128)(2,1)}, bf16[1040,128]{1,0:T(8,128)(2,1)S(1)}, u32[]{:S(2)}, u32[]{:S(2)}) collective-permute-start(bf16[1040,128]{1,0:T(8,128)(2,1)} %get-tuple-element.55), channel_id=1, source_target_pairs={{0,16},{4,20},{8,24},{12,28},{16,0},{20,4},{24,8},{28,12},{1,17},{... | collective-permute-start | bytes 798728 | tf_op jit(solution)/shard_map/ppermute | solution.py:484
  8.5 1.1 collective-permute-start.4
  9.7 2.0 %collective-permute-start.5 = (bf16[1040,128]{1,0:T(8,128)(2,1)}, bf16[1040,128]{1,0:T(8,128)(2,1)S(1)}, u32[]{:S(2)}, u32[]{:S(2)}) collective-permute-start(bf16[1040,128]{1,0:T(8,128)(2,1)} %get-tuple-element.58), channel_id=1, source_target_pairs={{0,20},{4,16},{8,28},{12,24},{16,4},{20,0},{24,12},{28,8},{1,21},{... | collective-permute-start | bytes 798728 | tf_op jit(solution)/shard_map/ppermute | solution.py:484
  11.7 2.7 %collective-permute-done.1.refs_2_ = bf16[1040,128]{1,0:T(8,128)(2,1)S(1)} collective-permute-done((bf16[1040,128]{1,0:T(8,128)(2,1)}, bf16[1040,128]{1,0:T(8,128)(2,1)S(1)}, u32[]{:S(2)}, u32[]{:S(2)}) %collective-permute-start.1) | collective-permute-done | bytes 266272 | tf_op jit(solution)/shard_map/ppermute | solution.py:484
  14.4 1.7 %collective-permute-start.6 = (bf16[1040,128]{1,0:T(8,128)(2,1)}, bf16[1040,128]{1,0:T(8,128)(2,1)S(1)}, u32[]{:S(2)}, u32[]{:S(2)}) collective-permute-start(bf16[1040,128]{1,0:T(8,128)(2,1)} %get-tuple-element.59), channel_id=1, source_target_pairs={{0,28},{4,24},{8,20},{12,16},{16,12},{20,8},{24,4},{28,0},{1,29},{... | collective-permute-start | bytes 798728 | tf_op jit(solution)/shard_map/ppermute | solution.py:484
  16.2 2.6 %pack_values.1 = (bf16[1024,128]{1,0:T(8,128)(2,1)}, bf16[1024,128]{1,0:T(8,128)(2,1)}, bf16[1024,128]{1,0:T(8,128)(2,1)}, bf16[1024,128]{1,0:T(8,128)(2,1)}, bf...) custom-call(s32[1]{0:T(128)} %bitcast.rank_ref, ...), custom_call_target="tpu_custom_call" | custom-call | tf_op jit(solution)/shard_map/pack_values/pallas_call | solution.py:613
  18.7 3.4 %collective-permute-done.2.refs_3_ = bf16[1040,128]{1,0:T(8,128)(2,1)S(1)} collective-permute-done((bf16[1040,128]{1,0:T(8,128)(2,1)}, bf16[1040,128]{1,0:T(8,128)(2,1)S(1)}, u32[]{:S(2)}, u32[]{:S(2)}) %collective-permute-start.2) | collective-permute-done | bytes 266272 | tf_op jit(solution)/shard_map/ppermute | solution.py:484
  22.1 0.9 collective-permute-start.8
  23.1 2.4 %collective-permute-done.4.refs_5_ = bf16[1040,128]{1,0:T(8,128)(2,1)S(1)} collective-permute-done((bf16[1040,128]{1,0:T(8,128)(2,1)}, bf16[1040,128]{1,0:T(8,128)(2,1)S(1)}, u32[]{:S(2)}, u32[]{:S(2)}) %collective-permute-start.4) | collective-permute-done | bytes 266272 | tf_op jit(solution)/shard_map/ppermute | solution.py:484
  25.5 1.5 %collective-permute-start.9 = (bf16[1024,128]{1,0:T(8,128)(2,1)}, bf16[1024,128]{1,0:T(8,128)(2,1)S(1)}, u32[]{:S(2)}, u32[]{:S(2)}) collective-permute-start(bf16[1024,128]{1,0:T(8,128)(2,1)} %get-tuple-element.66), channel_id=1, source_target_pairs={{0,16},{4,20},{8,24},{12,28},{16,0},{20,4},{24,8},{28,12},{1,17},{... | collective-permute-start | bytes 786440 | tf_op jit(solution)/shard_map/ppermute | solution.py:484
  27.0 5.7 %collective-permute-done.5.refs_6_ = bf16[1040,128]{1,0:T(8,128)(2,1)S(1)} collective-permute-done((bf16[1040,128]{1,0:T(8,128)(2,1)}, bf16[1040,128]{1,0:T(8,128)(2,1)S(1)}, u32[]{:S(2)}, u32[]{:S(2)}) %collective-permute-start.5) | collective-permute-done | bytes 266272 | tf_op jit(solution)/shard_map/ppermute | solution.py:484
  32.7 3.3 %collective-permute-start.11 = (bf16[1024,128]{1,0:T(8,128)(2,1)}, bf16[1024,128]{1,0:T(8,128)(2,1)S(1)}, u32[]{:S(2)}, u32[]{:S(2)}) collective-permute-start(bf16[1024,128]{1,0:T(8,128)(2,1)} %get-tuple-element.68), channel_id=1, source_target_pairs={{0,12},{4,8},{8,4},{12,0},{16,28},{20,24},{24,20},{28,16},{1,13},{... | collective-permute-start | bytes 786440 | tf_op jit(solution)/shard_map/ppermute | solution.py:484
  36.0 1.0 collective-permute-done.8.refs_2_.refs_10_
  37.0 2.0 %collective-permute-start.13 = (bf16[1024,128]{1,0:T(8,128)(2,1)}, bf16[1024,128]{1,0:T(8,128)(2,1)S(1)}, u32[]{:S(2)}, u32[]{:S(2)}) collective-permute-start(bf16[1024,128]{1,0:T(8,128)(2,1)} %get-tuple-element.70), channel_id=1, source_target_pairs={{0,28},{4,24},{8,20},{12,16},{16,12},{20,8},{24,4},{28,0},{1,29},{... | collective-permute-start | bytes 786440 | tf_op jit(solution)/shard_map/ppermute | solution.py:484
  39.0 13.7 %score.1 = (bf16[8,2048,512]{2,1,0:T(8,128)(2,1)}, f32[8,1,512]{2,1,0:T(1,128)}, s32[3]{0:T(128)}) custom-call(s32[1]{0:T(128)} %bitcast.rank_ref, bf16[1040,128]{1,0:T(8,128)(2,1)} %get-tuple-element.50.refs_0_, bf16[1040,128]{1,0:T(8,128)(2,1)} %copy-done.1, bf16[1040,128]{1,0:T(8,128)(2,1)} %copy-done.2, bf16[1040,128]{1,0:T(8,128)(2,1)} %copy-done.3, ...), custom_call_target="tpu_custom_call" | custom-call | tf_op jit(solution)/shard_map/score/pallas_call | solution.py:512
  52.8 1.6 %collective-permute-done.12.refs_6_.refs_14_ = bf16[1024,128]{1,0:T(8,128)(2,1)S(1)} collective-permute-done((bf16[1024,128]{1,0:T(8,128)(2,1)}, bf16[1024,128]{1,0:T(8,128)(2,1)S(1)}, u32[]{:S(2)}, u32[]{:S(2)}) %collective-permute-start.12) | collective-permute-done | bytes 262176 | tf_op jit(solution)/shard_map/ppermute | solution.py:484
  55.1 0.4 copy-done.14
  55.5 10.3 %attend.1 = (f32[8,128,512]{2,1,0:T(8,128)}, bf16[8,512,128]{2,1,0:T(8,128)(2,1)}, f32[2,4096]{1,0:T(2,128)}) custom-call(s32[1]{0:T(128)} %bitcast.rank_ref, s32[3]{0:T(128)} %get-tuple-element.60.bounds, bf16[1024,128]{1,0:T(8,128)(2,1)} %get-tuple-element.63.refs_0_.refs_8_, bf16[1024,128]{1,0:T(8,128)(2,1)} %copy-done.8, bf16[1024,128]{1,0:T(8,128)(2,1)} %copy-done.9, ...), custom_call_target="tpu_custom_call" | custom-call | tf_op jit(solution)/shard_map/attend/pallas_call | solution.py:536
  65.8 0.5 collective-permute-start.14
  66.3 1.1 collective-permute-done.14
  67.4 0.8 add.21
  68.2 3.5 %collective-permute-start.17 = (f32[2,4096]{1,0:T(2,128)S(1)}, f32[2,4096]{1,0:T(2,128)S(1)}, u32[]{:S(2)}, u32[]{:S(2)}) collective-permute-start(f32[2,4096]{1,0:T(2,128)S(1)} %add.21), channel_id=1, source_target_pairs={{0,24},{4,28},{8,16},{12,20},{16,8},{20,12},{24,0},{28,4},{1,25},{... | collective-permute-start | bytes 98312 | tf_op jit(solution)/shard_map/ppermute | solution.py:484
  71.7 0.6 collective-permute-start.15
  72.3 1.3 collective-permute-done.17
  73.6 2.0 %collective-permute-done.16 = f32[2,4096]{1,0:T(2,128)S(1)} collective-permute-done((f32[2,4096]{1,0:T(2,128)S(1)}, f32[2,4096]{1,0:T(2,128)S(1)}, u32[]{:S(2)}, u32[]{:S(2)}) %collective-permute-start.16) | collective-permute-done | bytes 32800 | tf_op jit(solution)/shard_map/ppermute | solution.py:484
  75.6 3.6 %collective-permute-start.20 = (f32[2,4096]{1,0:T(2,128)S(1)}, f32[2,4096]{1,0:T(2,128)S(1)}, u32[]{:S(2)}, u32[]{:S(2)}) collective-permute-start(f32[2,4096]{1,0:T(2,128)S(1)} %add_add_fusion.1), channel_id=1, source_target_pairs={{0,3},{1,0},{2,1},{3,2},{4,7},{5,4},{6,5},{7,6},{8,11},{9,8},{10,9... | collective-permute-start | bytes 98312 | tf_op jit(solution)/shard_map/ppermute | solution.py:500
  79.2 1.0 collective-permute-start.18
  80.3 3.7 %all-to-all-start = ((bf16[8,512,128]{2,1,0:T(8,128)(2,1)}), bf16[8,512,128]{2,1,0:T(8,128)(2,1)S(1)}, u32[]{:S(2)}, u32[]{:S(2)}) async-start(bf16[8,512,128]{2,1,0:T(8,128)(2,1)} %get-tuple-element.74), calls=%async_computation | async-start | bytes 2097152 | tf_op jit(solution)/shard_map/all_to_all | solution.py:492
  84.1 0.9 collective-permute-done.18
  85.0 0.6 add_add_fusion.refs_19_.stats_ref
  85.6 22.0 %backward.1 = (bf16[1536,128]{1,0:T(8,128)(2,1)}, bf16[1536,128]{1,0:T(8,128)(2,1)}, bf16[1536,128]{1,0:T(8,128)(2,1)}, bf16[1536,128]{1,0:T(8,128)(2,1)}, bf16[...) custom-call(s32[1]{0:T(128)} %bitcast.rank_ref, ...), custom_call_target="tpu_custom_call" | custom-call | tf_op jit(solution)/shard_map/backward/pallas_call | solution.py:564
  107.7 0.9 collective-permute-start.22
  108.6 1.8 %collective-permute-start.23 = (bf16[1536,128]{1,0:T(8,128)(2,1)}, bf16[1536,128]{1,0:T(8,128)(2,1)S(1)}, u32[]{:S(2)}, u32[]{:S(2)}) collective-permute-start(bf16[1536,128]{1,0:T(8,128)(2,1)} %get-tuple-element.88), channel_id=1, source_target_pairs={{0,16},{4,20},{8,24},{12,28},{16,0},{20,4},{24,8},{28,12},{1,17},{... | collective-permute-start | bytes 1179656 | tf_op jit(solution)/shard_map/ppermute | solution.py:484
  110.4 0.9 collective-permute-start.24
  111.4 2.3 %collective-permute-start.26 = (bf16[1536,128]{1,0:T(8,128)(2,1)}, bf16[1536,128]{1,0:T(8,128)(2,1)S(1)}, u32[]{:S(2)}, u32[]{:S(2)}) collective-permute-start(bf16[1536,128]{1,0:T(8,128)(2,1)} %get-tuple-element.91), channel_id=1, source_target_pairs={{0,20},{4,16},{8,28},{12,24},{16,4},{20,0},{24,12},{28,8},{1,21},{... | collective-permute-start | bytes 1179656 | tf_op jit(solution)/shard_map/ppermute | solution.py:484
  113.6 6.3 %collective-permute-done.22.refs_2_ = bf16[1536,128]{1,0:T(8,128)(2,1)S(1)} collective-permute-done((bf16[1536,128]{1,0:T(8,128)(2,1)}, bf16[1536,128]{1,0:T(8,128)(2,1)S(1)}, u32[]{:S(2)}, u32[]{:S(2)}) %collective-permute-start.22) | collective-permute-done | bytes 393248 | tf_op jit(solution)/shard_map/ppermute | solution.py:484
  119.9 0.9 collective-permute-start.27
  120.8 2.5 %normed.1 = bf16[512,1024]{1,0:T(8,128)(2,1)} custom-call(s32[1]{0:T(128)} %bitcast.rank_ref, f32[2,4096]{1,0:T(2,128)} %add_add_fusion.refs_19_.stats_ref, bf16[8,512,128]{2,1,0:T(8,128)(2,1)} %copy-done), custom_call_target="tpu_custom_call" | custom-call | tf_op jit(solution)/shard_map/normed/pallas_call | solution.py:635
  123.3 5.3 %collective-permute-done.23.refs_3_ = bf16[1536,128]{1,0:T(8,128)(2,1)S(1)} collective-permute-done((bf16[1536,128]{1,0:T(8,128)(2,1)}, bf16[1536,128]{1,0:T(8,128)(2,1)S(1)}, u32[]{:S(2)}, u32[]{:S(2)}) %collective-permute-start.23) | collective-permute-done | bytes 393248 | tf_op jit(solution)/shard_map/ppermute | solution.py:484
  128.6 1.2 collective-permute-done.24.refs_4_
  129.8 6.1 %collective-permute-done.25.refs_5_ = bf16[1536,128]{1,0:T(8,128)(2,1)S(1)} collective-permute-done((bf16[1536,128]{1,0:T(8,128)(2,1)}, bf16[1536,128]{1,0:T(8,128)(2,1)S(1)}, u32[]{:S(2)}, u32[]{:S(2)}) %collective-permute-start.25) | collective-permute-done | bytes 393248 | tf_op jit(solution)/shard_map/ppermute | solution.py:484
  135.9 8.8 %collective-permute-done.26.refs_6_ = bf16[1536,128]{1,0:T(8,128)(2,1)S(1)} collective-permute-done((bf16[1536,128]{1,0:T(8,128)(2,1)}, bf16[1536,128]{1,0:T(8,128)(2,1)S(1)}, u32[]{:S(2)}, u32[]{:S(2)}) %collective-permute-start.26) | collective-permute-done | bytes 393248 | tf_op jit(solution)/shard_map/ppermute | solution.py:484
  144.7 1.1 collective-permute-done.27.refs_7_
  145.8 0.7 copy-done.21
  146.5 3.2 %unpack.1 = (bf16[512,1024]{1,0:T(8,128)(2,1)}, bf16[512,1024]{1,0:T(8,128)(2,1)}, bf16[512,1024]{1,0:T(8,128)(2,1)}) custom-call(s32[1]{0:T(128)} %bitcast.rank_ref, bf16[1536,128]{1,0:T(8,128)(2,1)} %get-tuple-element.85.refs_0_, bf16[1536,128]{1,0:T(8,128)(2,1)} %copy-done.15, bf16[1536,128]{1,0:T(8,128)(2,1)} %copy-done.16, ...), custom_call_target="tpu_custom_call" | custom-call | tf_op jit(solution)/shard_map/unpack/pallas_call | solution.py:644
  (64 shorter events, 1.1 us)
Async XLA Ops:
  3.9 5.8 %collective-permute-start = (bf16[1040,128]{1,0:T(8,128)(2,1)}, bf16[1040,128]{1,0:T(8,128)(2,1)S(1)}, u32[]{:S(2)}, u32[]{:S(2)}) collective-permute-start(bf16[1040,128]{1,0:T(8,128)(2,1)} %get-tuple-element.51), channel_id=1, source_target_pairs={{0,4},{4,0},{8,12},{12,8},{16,20},{20,16},{24,28},{28,24},{1,5},{5... | collective-permute-start | bytes 798728 | tf_op jit(solution)/shard_map/ppermute | solution.py:484
  4.4 10.0 %collective-permute-start.1 = (bf16[1040,128]{1,0:T(8,128)(2,1)}, bf16[1040,128]{1,0:T(8,128)(2,1)S(1)}, u32[]{:S(2)}, u32[]{:S(2)}) collective-permute-start(bf16[1040,128]{1,0:T(8,128)(2,1)} %get-tuple-element.52), channel_id=1, source_target_pairs={{0,8},{4,12},{8,0},{12,4},{16,24},{20,28},{24,16},{28,20},{1,9},{5... | collective-permute-start | bytes 798728 | tf_op jit(solution)/shard_map/ppermute | solution.py:484
  7.0 15.2 %collective-permute-start.2 = (bf16[1040,128]{1,0:T(8,128)(2,1)}, bf16[1040,128]{1,0:T(8,128)(2,1)S(1)}, u32[]{:S(2)}, u32[]{:S(2)}) collective-permute-start(bf16[1040,128]{1,0:T(8,128)(2,1)} %get-tuple-element.55), channel_id=1, source_target_pairs={{0,16},{4,20},{8,24},{12,28},{16,0},{20,4},{24,8},{28,12},{1,17},{... | collective-permute-start | bytes 798728 | tf_op jit(solution)/shard_map/ppermute | solution.py:484
  8.5 13.6 %collective-permute-start.3 = (bf16[1040,128]{1,0:T(8,128)(2,1)}, bf16[1040,128]{1,0:T(8,128)(2,1)S(1)}, u32[]{:S(2)}, u32[]{:S(2)}) collective-permute-start(bf16[1040,128]{1,0:T(8,128)(2,1)} %get-tuple-element.56), channel_id=1, source_target_pairs={{0,24},{4,28},{8,16},{12,20},{16,8},{20,12},{24,0},{28,4},{1,25},{... | collective-permute-start | bytes 798728 | tf_op jit(solution)/shard_map/ppermute | solution.py:484
  8.5 16.9 %collective-permute-start.4 = (bf16[1040,128]{1,0:T(8,128)(2,1)}, bf16[1040,128]{1,0:T(8,128)(2,1)S(1)}, u32[]{:S(2)}, u32[]{:S(2)}) collective-permute-start(bf16[1040,128]{1,0:T(8,128)(2,1)} %get-tuple-element.57), channel_id=1, source_target_pairs={{0,12},{4,8},{8,4},{12,0},{16,28},{20,24},{24,20},{28,16},{1,13},{... | collective-permute-start | bytes 798728 | tf_op jit(solution)/shard_map/ppermute | solution.py:484
  9.7 29.3 %copy-start.1 = (bf16[1040,128]{1,0:T(8,128)(2,1)}, bf16[1040,128]{1,0:T(8,128)(2,1)S(1)}, u32[]{:S(2)}) copy-start(bf16[1040,128]{1,0:T(8,128)(2,1)S(1)} %collective-permute-done.refs_1_) | copy-start | bytes 798724
  9.7 23.0 %collective-permute-start.5 = (bf16[1040,128]{1,0:T(8,128)(2,1)}, bf16[1040,128]{1,0:T(8,128)(2,1)S(1)}, u32[]{:S(2)}, u32[]{:S(2)}) collective-permute-start(bf16[1040,128]{1,0:T(8,128)(2,1)} %get-tuple-element.58), channel_id=1, source_target_pairs={{0,20},{4,16},{8,28},{12,24},{16,4},{20,0},{24,12},{28,8},{1,21},{... | collective-permute-start | bytes 798728 | tf_op jit(solution)/shard_map/ppermute | solution.py:484
  14.4 24.6 %copy-start.2 = (bf16[1040,128]{1,0:T(8,128)(2,1)}, bf16[1040,128]{1,0:T(8,128)(2,1)S(1)}, u32[]{:S(2)}) copy-start(bf16[1040,128]{1,0:T(8,128)(2,1)S(1)} %collective-permute-done.1.refs_2_) | copy-start | bytes 798724
  14.4 18.3 %collective-permute-start.6 = (bf16[1040,128]{1,0:T(8,128)(2,1)}, bf16[1040,128]{1,0:T(8,128)(2,1)S(1)}, u32[]{:S(2)}, u32[]{:S(2)}) collective-permute-start(bf16[1040,128]{1,0:T(8,128)(2,1)} %get-tuple-element.59), channel_id=1, source_target_pairs={{0,28},{4,24},{8,20},{12,16},{16,12},{20,8},{24,4},{28,0},{1,29},{... | collective-permute-start | bytes 798728 | tf_op jit(solution)/shard_map/ppermute | solution.py:484
  22.1 16.9 %copy-start.3 = (bf16[1040,128]{1,0:T(8,128)(2,1)}, bf16[1040,128]{1,0:T(8,128)(2,1)S(1)}, u32[]{:S(2)}) copy-start(bf16[1040,128]{1,0:T(8,128)(2,1)S(1)} %collective-permute-done.2.refs_3_) | copy-start | bytes 798724
  22.1 13.8 %collective-permute-start.7 = (bf16[1024,128]{1,0:T(8,128)(2,1)}, bf16[1024,128]{1,0:T(8,128)(2,1)S(1)}, u32[]{:S(2)}, u32[]{:S(2)}) collective-permute-start(bf16[1024,128]{1,0:T(8,128)(2,1)} %get-tuple-element.64), channel_id=1, source_target_pairs={{0,4},{4,0},{8,12},{12,8},{16,20},{20,16},{24,28},{28,24},{1,5},{5... | collective-permute-start | bytes 786440 | tf_op jit(solution)/shard_map/ppermute | solution.py:484
  22.1 16.8 %copy-start.4 = (bf16[1040,128]{1,0:T(8,128)(2,1)}, bf16[1040,128]{1,0:T(8,128)(2,1)S(1)}, u32[]{:S(2)}) copy-start(bf16[1040,128]{1,0:T(8,128)(2,1)S(1)} %collective-permute-done.3.refs_4_) | copy-start | bytes 798724
  22.1 14.8 %collective-permute-start.8 = (bf16[1024,128]{1,0:T(8,128)(2,1)}, bf16[1024,128]{1,0:T(8,128)(2,1)S(1)}, u32[]{:S(2)}, u32[]{:S(2)}) collective-permute-start(bf16[1024,128]{1,0:T(8,128)(2,1)} %get-tuple-element.65), channel_id=1, source_target_pairs={{0,8},{4,12},{8,0},{12,4},{16,24},{20,28},{24,16},{28,20},{1,9},{5... | collective-permute-start | bytes 786440 | tf_op jit(solution)/shard_map/ppermute | solution.py:484
  25.5 13.5 %copy-start.5 = (bf16[1040,128]{1,0:T(8,128)(2,1)}, bf16[1040,128]{1,0:T(8,128)(2,1)S(1)}, u32[]{:S(2)}) copy-start(bf16[1040,128]{1,0:T(8,128)(2,1)S(1)} %collective-permute-done.4.refs_5_) | copy-start | bytes 798724
  25.5 27.3 %collective-permute-start.9 = (bf16[1024,128]{1,0:T(8,128)(2,1)}, bf16[1024,128]{1,0:T(8,128)(2,1)S(1)}, u32[]{:S(2)}, u32[]{:S(2)}) collective-permute-start(bf16[1024,128]{1,0:T(8,128)(2,1)} %get-tuple-element.66), channel_id=1, source_target_pairs={{0,16},{4,20},{8,24},{12,28},{16,0},{20,4},{24,8},{28,12},{1,17},{... | collective-permute-start | bytes 786440 | tf_op jit(solution)/shard_map/ppermute | solution.py:484
  32.7 6.3 %copy-start.6 = (bf16[1040,128]{1,0:T(8,128)(2,1)}, bf16[1040,128]{1,0:T(8,128)(2,1)S(1)}, u32[]{:S(2)}) copy-start(bf16[1040,128]{1,0:T(8,128)(2,1)S(1)} %collective-permute-done.5.refs_6_) | copy-start | bytes 798724
  32.7 20.1 %collective-permute-start.10 = (bf16[1024,128]{1,0:T(8,128)(2,1)}, bf16[1024,128]{1,0:T(8,128)(2,1)S(1)}, u32[]{:S(2)}, u32[]{:S(2)}) collective-permute-start(bf16[1024,128]{1,0:T(8,128)(2,1)} %get-tuple-element.67), channel_id=1, source_target_pairs={{0,24},{4,28},{8,16},{12,20},{16,8},{20,12},{24,0},{28,4},{1,25},{... | collective-permute-start | bytes 786440 | tf_op jit(solution)/shard_map/ppermute | solution.py:484
  32.7 6.3 %copy-start.7 = (bf16[1040,128]{1,0:T(8,128)(2,1)}, bf16[1040,128]{1,0:T(8,128)(2,1)S(1)}, u32[]{:S(2)}) copy-start(bf16[1040,128]{1,0:T(8,128)(2,1)S(1)} %collective-permute-done.6.refs_7_) | copy-start | bytes 798724
  32.7 20.1 %collective-permute-start.11 = (bf16[1024,128]{1,0:T(8,128)(2,1)}, bf16[1024,128]{1,0:T(8,128)(2,1)S(1)}, u32[]{:S(2)}, u32[]{:S(2)}) collective-permute-start(bf16[1024,128]{1,0:T(8,128)(2,1)} %get-tuple-element.68), channel_id=1, source_target_pairs={{0,12},{4,8},{8,4},{12,0},{16,28},{20,24},{24,20},{28,16},{1,13},{... | collective-permute-start | bytes 786440 | tf_op jit(solution)/shard_map/ppermute | solution.py:484
  36.0 18.8 %copy-start.8 = (bf16[1024,128]{1,0:T(8,128)(2,1)}, bf16[1024,128]{1,0:T(8,128)(2,1)S(1)}, u32[]{:S(2)}) copy-start(bf16[1024,128]{1,0:T(8,128)(2,1)S(1)} %collective-permute-done.7.refs_1_.refs_9_) | copy-start | bytes 786436
  36.0 18.4 %collective-permute-start.12 = (bf16[1024,128]{1,0:T(8,128)(2,1)}, bf16[1024,128]{1,0:T(8,128)(2,1)S(1)}, u32[]{:S(2)}, u32[]{:S(2)}) collective-permute-start(bf16[1024,128]{1,0:T(8,128)(2,1)} %get-tuple-element.69), channel_id=1, source_target_pairs={{0,20},{4,16},{8,28},{12,24},{16,4},{20,0},{24,12},{28,8},{1,21},{... | collective-permute-start | bytes 786440 | tf_op jit(solution)/shard_map/ppermute | solution.py:484
  37.0 17.8 %copy-start.9 = (bf16[1024,128]{1,0:T(8,128)(2,1)}, bf16[1024,128]{1,0:T(8,128)(2,1)S(1)}, u32[]{:S(2)}) copy-start(bf16[1024,128]{1,0:T(8,128)(2,1)S(1)} %collective-permute-done.8.refs_2_.refs_10_) | copy-start | bytes 786436
  37.0 17.8 %collective-permute-start.13 = (bf16[1024,128]{1,0:T(8,128)(2,1)}, bf16[1024,128]{1,0:T(8,128)(2,1)S(1)}, u32[]{:S(2)}, u32[]{:S(2)}) collective-permute-start(bf16[1024,128]{1,0:T(8,128)(2,1)} %get-tuple-element.70), channel_id=1, source_target_pairs={{0,28},{4,24},{8,20},{12,16},{16,12},{20,8},{24,4},{28,0},{1,29},{... | collective-permute-start | bytes 786440 | tf_op jit(solution)/shard_map/ppermute | solution.py:484
  52.8 2.0 %copy-start.10 = (bf16[1024,128]{1,0:T(8,128)(2,1)}, bf16[1024,128]{1,0:T(8,128)(2,1)S(1)}, u32[]{:S(2)}) copy-start(bf16[1024,128]{1,0:T(8,128)(2,1)S(1)} %collective-permute-done.9.refs_3_.refs_11_) | copy-start | bytes 786436
  52.8 2.0 %copy-start.11 = (bf16[1024,128]{1,0:T(8,128)(2,1)}, bf16[1024,128]{1,0:T(8,128)(2,1)S(1)}, u32[]{:S(2)}) copy-start(bf16[1024,128]{1,0:T(8,128)(2,1)S(1)} %collective-permute-done.10.refs_4_.refs_12_) | copy-start | bytes 786436
  52.8 2.0 %copy-start.12 = (bf16[1024,128]{1,0:T(8,128)(2,1)}, bf16[1024,128]{1,0:T(8,128)(2,1)S(1)}, u32[]{:S(2)}) copy-start(bf16[1024,128]{1,0:T(8,128)(2,1)S(1)} %collective-permute-done.11.refs_5_.refs_13_) | copy-start | bytes 786436
  65.8 1.6 %collective-permute-start.14 = (f32[2,4096]{1,0:T(2,128)}, f32[2,4096]{1,0:T(2,128)S(1)}, u32[]{:S(2)}, u32[]{:S(2)}) collective-permute-start(f32[2,4096]{1,0:T(2,128)} %get-tuple-element.73), channel_id=1, source_target_pairs={{0,4},{4,0},{8,12},{12,8},{16,20},{20,16},{24,28},{28,24},{1,5},{5... | collective-permute-start | bytes 98312 | tf_op jit(solution)/shard_map/ppermute | solution.py:484
  68.2 5.4 %collective-permute-start.17 = (f32[2,4096]{1,0:T(2,128)S(1)}, f32[2,4096]{1,0:T(2,128)S(1)}, u32[]{:S(2)}, u32[]{:S(2)}) collective-permute-start(f32[2,4096]{1,0:T(2,128)S(1)} %add.21), channel_id=1, source_target_pairs={{0,24},{4,28},{8,16},{12,20},{16,8},{20,12},{24,0},{28,4},{1,25},{... | collective-permute-start | bytes 98312 | tf_op jit(solution)/shard_map/ppermute | solution.py:484
  71.6 3.9 %collective-permute-start.16 = (f32[2,4096]{1,0:T(2,128)S(1)}, f32[2,4096]{1,0:T(2,128)S(1)}, u32[]{:S(2)}, u32[]{:S(2)}) collective-permute-start(f32[2,4096]{1,0:T(2,128)S(1)} %add.21), channel_id=1, source_target_pairs={{0,16},{4,20},{8,24},{12,28},{16,0},{20,4},{24,8},{28,12},{1,17},{... | collective-permute-start | bytes 98312 | tf_op jit(solution)/shard_map/ppermute | solution.py:484
  71.7 3.9 %collective-permute-start.15 = (f32[2,4096]{1,0:T(2,128)S(1)}, f32[2,4096]{1,0:T(2,128)S(1)}, u32[]{:S(2)}, u32[]{:S(2)}) collective-permute-start(f32[2,4096]{1,0:T(2,128)S(1)} %add.21), channel_id=1, source_target_pairs={{0,8},{4,12},{8,0},{12,4},{16,24},{20,28},{24,16},{28,20},{1,9},{5... | collective-permute-start | bytes 98312 | tf_op jit(solution)/shard_map/ppermute | solution.py:484
  75.6 8.4 %collective-permute-start.20 = (f32[2,4096]{1,0:T(2,128)S(1)}, f32[2,4096]{1,0:T(2,128)S(1)}, u32[]{:S(2)}, u32[]{:S(2)}) collective-permute-start(f32[2,4096]{1,0:T(2,128)S(1)} %add_add_fusion.1), channel_id=1, source_target_pairs={{0,3},{1,0},{2,1},{3,2},{4,7},{5,4},{6,5},{7,6},{8,11},{9,8},{10,9... | collective-permute-start | bytes 98312 | tf_op jit(solution)/shard_map/ppermute | solution.py:500
  79.2 4.8 %collective-permute-start.19 = (f32[2,4096]{1,0:T(2,128)S(1)}, f32[2,4096]{1,0:T(2,128)S(1)}, u32[]{:S(2)}, u32[]{:S(2)}) collective-permute-start(f32[2,4096]{1,0:T(2,128)S(1)} %add_add_fusion.1), channel_id=1, source_target_pairs={{0,2},{1,3},{2,0},{3,1},{4,6},{5,7},{6,4},{7,5},{8,10},{9,11},{10,... | collective-permute-start | bytes 98312 | tf_op jit(solution)/shard_map/ppermute | solution.py:500
  79.2 5.7 %collective-permute-start.18 = (f32[2,4096]{1,0:T(2,128)S(1)}, f32[2,4096]{1,0:T(2,128)S(1)}, u32[]{:S(2)}, u32[]{:S(2)}) collective-permute-start(f32[2,4096]{1,0:T(2,128)S(1)} %add_add_fusion.1), channel_id=1, source_target_pairs={{0,1},{1,2},{2,3},{3,0},{4,5},{5,6},{6,7},{7,4},{8,9},{9,10},{10,1... | collective-permute-start | bytes 98312 | tf_op jit(solution)/shard_map/ppermute | solution.py:500
  80.3 27.4 %all-to-all-start = ((bf16[8,512,128]{2,1,0:T(8,128)(2,1)}), bf16[8,512,128]{2,1,0:T(8,128)(2,1)S(1)}, u32[]{:S(2)}, u32[]{:S(2)}) async-start(bf16[8,512,128]{2,1,0:T(8,128)(2,1)} %get-tuple-element.74), calls=%async_computation | async-start | bytes 2097152 | tf_op jit(solution)/shard_map/all_to_all | solution.py:492
  107.6 13.2 %copy-start = (bf16[8,512,128]{2,1,0:T(8,128)(2,1)}, bf16[8,512,128]{2,1,0:T(8,128)(2,1)S(1)}, u32[]{:S(2)}) copy-start(bf16[8,512,128]{2,1,0:T(8,128)(2,1)S(1)} %all-to-all-done.home_ref) | copy-start | bytes 3145732
  107.6 3.7 %collective-permute-start.21 = (bf16[1536,128]{1,0:T(8,128)(2,1)}, bf16[1536,128]{1,0:T(8,128)(2,1)S(1)}, u32[]{:S(2)}, u32[]{:S(2)}) collective-permute-start(bf16[1536,128]{1,0:T(8,128)(2,1)} %get-tuple-element.86), channel_id=1, source_target_pairs={{0,4},{4,0},{8,12},{12,8},{16,20},{20,16},{24,28},{28,24},{1,5},{5... | collective-permute-start | bytes 1179656 | tf_op jit(solution)/shard_map/ppermute | solution.py:484
  107.7 12.2 %collective-permute-start.22 = (bf16[1536,128]{1,0:T(8,128)(2,1)}, bf16[1536,128]{1,0:T(8,128)(2,1)S(1)}, u32[]{:S(2)}, u32[]{:S(2)}) collective-permute-start(bf16[1536,128]{1,0:T(8,128)(2,1)} %get-tuple-element.87), channel_id=1, source_target_pairs={{0,8},{4,12},{8,0},{12,4},{16,24},{20,28},{24,16},{28,20},{1,9},{5... | collective-permute-start | bytes 1179656 | tf_op jit(solution)/shard_map/ppermute | solution.py:484
  108.6 20.0 %collective-permute-start.23 = (bf16[1536,128]{1,0:T(8,128)(2,1)}, bf16[1536,128]{1,0:T(8,128)(2,1)S(1)}, u32[]{:S(2)}, u32[]{:S(2)}) collective-permute-start(bf16[1536,128]{1,0:T(8,128)(2,1)} %get-tuple-element.88), channel_id=1, source_target_pairs={{0,16},{4,20},{8,24},{12,28},{16,0},{20,4},{24,8},{28,12},{1,17},{... | collective-permute-start | bytes 1179656 | tf_op jit(solution)/shard_map/ppermute | solution.py:484
  110.4 19.4 %collective-permute-start.24 = (bf16[1536,128]{1,0:T(8,128)(2,1)}, bf16[1536,128]{1,0:T(8,128)(2,1)S(1)}, u32[]{:S(2)}, u32[]{:S(2)}) collective-permute-start(bf16[1536,128]{1,0:T(8,128)(2,1)} %get-tuple-element.89), channel_id=1, source_target_pairs={{0,24},{4,28},{8,16},{12,20},{16,8},{20,12},{24,0},{28,4},{1,25},{... | collective-permute-start | bytes 1179656 | tf_op jit(solution)/shard_map/ppermute | solution.py:484
  111.3 24.6 %collective-permute-start.25 = (bf16[1536,128]{1,0:T(8,128)(2,1)}, bf16[1536,128]{1,0:T(8,128)(2,1)S(1)}, u32[]{:S(2)}, u32[]{:S(2)}) collective-permute-start(bf16[1536,128]{1,0:T(8,128)(2,1)} %get-tuple-element.90), channel_id=1, source_target_pairs={{0,12},{4,8},{8,4},{12,0},{16,28},{20,24},{24,20},{28,16},{1,13},{... | collective-permute-start | bytes 1179656 | tf_op jit(solution)/shard_map/ppermute | solution.py:484
  111.4 34.4 %copy-start.15 = (bf16[1536,128]{1,0:T(8,128)(2,1)}, bf16[1536,128]{1,0:T(8,128)(2,1)S(1)}, u32[]{:S(2)}) copy-start(bf16[1536,128]{1,0:T(8,128)(2,1)S(1)} %collective-permute-done.21.refs_1_) | copy-start | bytes 1179652
  111.4 33.3 %collective-permute-start.26 = (bf16[1536,128]{1,0:T(8,128)(2,1)}, bf16[1536,128]{1,0:T(8,128)(2,1)S(1)}, u32[]{:S(2)}, u32[]{:S(2)}) collective-permute-start(bf16[1536,128]{1,0:T(8,128)(2,1)} %get-tuple-element.91), channel_id=1, source_target_pairs={{0,20},{4,16},{8,28},{12,24},{16,4},{20,0},{24,12},{28,8},{1,21},{... | collective-permute-start | bytes 1179656 | tf_op jit(solution)/shard_map/ppermute | solution.py:484
  119.9 25.9 %copy-start.16 = (bf16[1536,128]{1,0:T(8,128)(2,1)}, bf16[1536,128]{1,0:T(8,128)(2,1)S(1)}, u32[]{:S(2)}) copy-start(bf16[1536,128]{1,0:T(8,128)(2,1)S(1)} %collective-permute-done.22.refs_2_) | copy-start | bytes 1179652
  119.9 25.9 %collective-permute-start.27 = (bf16[1536,128]{1,0:T(8,128)(2,1)}, bf16[1536,128]{1,0:T(8,128)(2,1)S(1)}, u32[]{:S(2)}, u32[]{:S(2)}) collective-permute-start(bf16[1536,128]{1,0:T(8,128)(2,1)} %get-tuple-element.92), channel_id=1, source_target_pairs={{0,28},{4,24},{8,20},{12,16},{16,12},{20,8},{24,4},{28,0},{1,29},{... | collective-permute-start | bytes 1179656 | tf_op jit(solution)/shard_map/ppermute | solution.py:484
  128.6 17.1 %copy-start.17 = (bf16[1536,128]{1,0:T(8,128)(2,1)}, bf16[1536,128]{1,0:T(8,128)(2,1)S(1)}, u32[]{:S(2)}) copy-start(bf16[1536,128]{1,0:T(8,128)(2,1)S(1)} %collective-permute-done.23.refs_3_) | copy-start | bytes 1179652
  129.8 16.0 %copy-start.18 = (bf16[1536,128]{1,0:T(8,128)(2,1)}, bf16[1536,128]{1,0:T(8,128)(2,1)S(1)}, u32[]{:S(2)}) copy-start(bf16[1536,128]{1,0:T(8,128)(2,1)S(1)} %collective-permute-done.24.refs_4_) | copy-start | bytes 1179652
  135.9 9.9 %copy-start.19 = (bf16[1536,128]{1,0:T(8,128)(2,1)}, bf16[1536,128]{1,0:T(8,128)(2,1)S(1)}, u32[]{:S(2)}) copy-start(bf16[1536,128]{1,0:T(8,128)(2,1)S(1)} %collective-permute-done.25.refs_5_) | copy-start | bytes 1179652
  144.7 1.1 copy-start.20
  (3 other events, 2.2 us)

commit v3 on v2

--- a/solution.py
+++ b/solution.py
@@ -213,9 +213,12 @@
     n = 8
     vg_refs = refs[:n]
     prob_ref, inv_ref, out_t_ref, out_ref, stats_ref = refs[n : n + 5]
-    values, cot, val_t, prob, out_t_keep, out_keep, acc, vg_sems, prob_sems, out_sems = refs[n + 5 :]
+    both, val_t, prob, out_t_keep, out_keep, acc, vg_sems, prob_sems, out_sems = refs[n + 5 :]
     vg_ref = vg_refs[0]
     prob_in = functools.partial(move_probs, prob_ref, prob, prob_sems, block)
+
+    def both_in(ref, t):
+        return pltpu.make_async_copy(ref, both.at[t], vg_sems.at[t])
 
     def rows_out(i):
         return (
@@ -224,16 +227,15 @@
         )
 
     for m, ref in zip(ORDER, vg_refs):
-        value_in(ref, rank_ref[0] ^ m, block, values, vg_sems).start()
-        cot_in(ref, rank_ref[0] ^ m, block, cot, vg_sems).start()
+        both_in(ref, rank_ref[0] ^ m).start()
     for t in range(n):
         by_rows(t, lambda slot: prob_in(t, slot).start())
     ones = jnp.ones((16, HEAD_DIM), BF16)
 
     def one_block(i, carry):
         own_rows = pl.ds(pl.multiple_of(i * block, block), block)
-        value_in(vg_ref, i, block, values, vg_sems).wait()
-        val_t[:, own_rows] = values[own_rows, :].T
+        both_in(vg_ref, i).wait()
+        val_t[:, own_rows] = both[i, 0:block, :].T
 
         def body(near, far, masked):
             out = None
@@ -258,8 +260,7 @@
         out = out_t_keep[i].T
         out_keep[i] = out.astype(BF16)
         rows_out(i)[1].start()
-        cot_in(vg_ref, i, block, cot, vg_sems).wait()
-        x = cot[i].astype(F32) * out
+        x = both[i, block:, :].astype(F32) * out
         high = x.astype(BF16)
         low = (x - high.astype(F32)).astype(BF16)
         stats_ref[1:2, cols] = (nt_dot(ones, high) + nt_dot(ones, low))[0:1]
@@ -543,14 +544,13 @@
         in_specs=[SMEM_SPEC] * 2 + [ANY_SPEC] * (n + 1) + [VMEM_SPEC],
         out_specs=[ANY_SPEC] * 2 + [VMEM_SPEC],
         scratch_shapes=[
-            pltpu.VMEM((n * block, HEAD_DIM), BF16),
-            pltpu.VMEM((n, block, HEAD_DIM), BF16),
+            pltpu.VMEM((n, 2 * block, HEAD_DIM), BF16),
             pltpu.VMEM((HEAD_DIM, n * block), BF16),
             pltpu.VMEM((n, 4 * block, block), BF16),
             pltpu.VMEM((n, HEAD_DIM, block), F32),
             pltpu.VMEM((n, block, HEAD_DIM), BF16),
             pltpu.VMEM((HEAD_DIM, block), F32),
-            pltpu.SemaphoreType.DMA((2, n)),
+            pltpu.SemaphoreType.DMA((n,)),
             pltpu.SemaphoreType.DMA((n,)),
             pltpu.SemaphoreType.DMA((2, n)),
         ],

time: 150 us -> 148 us (0.987)
  Pallas kernels: 57.5 us -> 53.8 us
    pallas_call x1, Pallas kernels: 22 us -> 20.4 us  [run_backward(): pl.pallas_call(functools.partial(backward_kernel, block), out_shape=[shap...]
  transfers between devices with their start and end apart: 29 -> 29, of which waited for: 17 -> 17; matrix products, arithmetic and copies ran while one was open for 0% -> 0% of each run, Pallas kernels for 27% -> 26%
where the time goes in v3:
time: 148 us
  Pallas kernels  53.8 us (36%)
  waiting for transfers between devices  51.7 us (35%)
  starting transfers between devices  38.1 us (26%)
  local copies, waits for them, and re-layouts  1.5 us (1%)
    ppermute x25, waiting for transfers between devices, swap(): return lax.ppermute(value, 'seq', [(s, s ^ m) for s in range(n)])  50.8 us
    ppermute x25, starting transfers between devices, swap(): return lax.ppermute(value, 'seq', [(s, s ^ m) for s in range(n)])  29.7 us
    pallas_call x1, Pallas kernels, run_backward(): pl.pallas_call(functools.partial(backward_kernel, block), out_shape=[shap...  20.4 us
    pallas_call x1, Pallas kernels, run_score(): pl.pallas_call(functools.partial(score_kernel, block), out_shape=[shape_o...  12.7 us
    pallas_call x1, Pallas kernels, run_attend(): pl.pallas_call(functools.partial(attend_kernel, block), out_shape=[shape_...  9.29 us
    ppermute x3, starting transfers between devices, sum_everywhere(): lax.ppermute(stats, 'head', [(s, (s + d) % heads) for s in range(heads)])  4.67 us
    all_to_all x1, starting transfers between devices, all_to_all(): return lax.all_to_all(value, 'seq', split_axis=0, concat_axis=0, tiled=True)  3.74 us
    pallas_call x1, Pallas kernels, by_head(): pl.pallas_call(functools.partial(pack_scores_kernel, block), out_shape=[s...  3.25 us
  transfers between devices with their start and end apart: 29, of which 17 were waited for; matrix products, arithmetic and copies ran while one was open for 0% of the time, Pallas kernels for 26%

profile of v3, /device:TPU:0, one launch (start us, length us, event | category | flops | bytes accessed | tf_op | source)
XLA Modules:
  0.0 147.6 jit_solution(3871237138391182886)
XLA Ops:
  0.6 3.2 %pack_scores.1 = (bf16[1040,128]{1,0:T(8,128)(2,1)}, bf16[1040,128]{1,0:T(8,128)(2,1)}, bf16[1040,128]{1,0:T(8,128)(2,1)}, bf16[1040,128]{1,0:T(8,128)(2,1)}, bf...) custom-call(s32[1]{0:T(128)} %bitcast.rank_ref, ...), custom_call_target="tpu_custom_call" | custom-call | tf_op jit(solution)/shard_map/pack_scores/pallas_call | solution.py:598
  3.9 0.5 collective-permute-start
  4.4 2.6 %collective-permute-start.1 = (bf16[1040,128]{1,0:T(8,128)(2,1)}, bf16[1040,128]{1,0:T(8,128)(2,1)S(1)}, u32[]{:S(2)}, u32[]{:S(2)}) collective-permute-start(bf16[1040,128]{1,0:T(8,128)(2,1)} %get-tuple-element.52), channel_id=1, source_target_pairs={{0,8},{4,12},{8,0},{12,4},{16,24},{20,28},{24,16},{28,20},{1,9},{5... | collective-permute-start | bytes 798728 | tf_op jit(solution)/shard_map/ppermute | solution.py:485
  7.0 1.5 %collective-permute-start.2 = (bf16[1040,128]{1,0:T(8,128)(2,1)}, bf16[1040,128]{1,0:T(8,128)(2,1)S(1)}, u32[]{:S(2)}, u32[]{:S(2)}) collective-permute-start(bf16[1040,128]{1,0:T(8,128)(2,1)} %get-tuple-element.55), channel_id=1, source_target_pairs={{0,16},{4,20},{8,24},{12,28},{16,0},{20,4},{24,8},{28,12},{1,17},{... | collective-permute-start | bytes 798728 | tf_op jit(solution)/shard_map/ppermute | solution.py:485
  8.5 1.1 collective-permute-start.4
  9.7 2.0 %collective-permute-start.5 = (bf16[1040,128]{1,0:T(8,128)(2,1)}, bf16[1040,128]{1,0:T(8,128)(2,1)S(1)}, u32[]{:S(2)}, u32[]{:S(2)}) collective-permute-start(bf16[1040,128]{1,0:T(8,128)(2,1)} %get-tuple-element.58), channel_id=1, source_target_pairs={{0,20},{4,16},{8,28},{12,24},{16,4},{20,0},{24,12},{28,8},{1,21},{... | collective-permute-start | bytes 798728 | tf_op jit(solution)/shard_map/ppermute | solution.py:485
  11.7 2.7 %collective-permute-done.1.refs_2_ = bf16[1040,128]{1,0:T(8,128)(2,1)S(1)} collective-permute-done((bf16[1040,128]{1,0:T(8,128)(2,1)}, bf16[1040,128]{1,0:T(8,128)(2,1)S(1)}, u32[]{:S(2)}, u32[]{:S(2)}) %collective-permute-start.1) | collective-permute-done | bytes 266272 | tf_op jit(solution)/shard_map/ppermute | solution.py:485
  14.4 1.7 %collective-permute-start.6 = (bf16[1040,128]{1,0:T(8,128)(2,1)}, bf16[1040,128]{1,0:T(8,128)(2,1)S(1)}, u32[]{:S(2)}, u32[]{:S(2)}) collective-permute-start(bf16[1040,128]{1,0:T(8,128)(2,1)} %get-tuple-element.59), channel_id=1, source_target_pairs={{0,28},{4,24},{8,20},{12,16},{16,12},{20,8},{24,4},{28,0},{1,29},{... | collective-permute-start | bytes 798728 | tf_op jit(solution)/shard_map/ppermute | solution.py:485
  16.2 2.6 %pack_values.1 = (bf16[1024,128]{1,0:T(8,128)(2,1)}, bf16[1024,128]{1,0:T(8,128)(2,1)}, bf16[1024,128]{1,0:T(8,128)(2,1)}, bf16[1024,128]{1,0:T(8,128)(2,1)}, bf...) custom-call(s32[1]{0:T(128)} %bitcast.rank_ref, ...), custom_call_target="tpu_custom_call" | custom-call | tf_op jit(solution)/shard_map/pack_values/pallas_call | solution.py:613
  18.7 3.4 %collective-permute-done.2.refs_3_ = bf16[1040,128]{1,0:T(8,128)(2,1)S(1)} collective-permute-done((bf16[1040,128]{1,0:T(8,128)(2,1)}, bf16[1040,128]{1,0:T(8,128)(2,1)S(1)}, u32[]{:S(2)}, u32[]{:S(2)}) %collective-permute-start.2) | collective-permute-done | bytes 266272 | tf_op jit(solution)/shard_map/ppermute | solution.py:485
  22.1 0.9 collective-permute-start.8
  23.1 2.4 %collective-permute-done.4.refs_5_ = bf16[1040,128]{1,0:T(8,128)(2,1)S(1)} collective-permute-done((bf16[1040,128]{1,0:T(8,128)(2,1)}, bf16[1040,128]{1,0:T(8,128)(2,1)S(1)}, u32[]{:S(2)}, u32[]{:S(2)}) %collective-permute-start.4) | collective-permute-done | bytes 266272 | tf_op jit(solution)/shard_map/ppermute | solution.py:485
  25.5 1.5 %collective-permute-start.9 = (bf16[1024,128]{1,0:T(8,128)(2,1)}, bf16[1024,128]{1,0:T(8,128)(2,1)S(1)}, u32[]{:S(2)}, u32[]{:S(2)}) collective-permute-start(bf16[1024,128]{1,0:T(8,128)(2,1)} %get-tuple-element.66), channel_id=1, source_target_pairs={{0,16},{4,20},{8,24},{12,28},{16,0},{20,4},{24,8},{28,12},{1,17},{... | collective-permute-start | bytes 786440 | tf_op jit(solution)/shard_map/ppermute | solution.py:485
  27.0 5.7 %collective-permute-done.5.refs_6_ = bf16[1040,128]{1,0:T(8,128)(2,1)S(1)} collective-permute-done((bf16[1040,128]{1,0:T(8,128)(2,1)}, bf16[1040,128]{1,0:T(8,128)(2,1)S(1)}, u32[]{:S(2)}, u32[]{:S(2)}) %collective-permute-start.5) | collective-permute-done | bytes 266272 | tf_op jit(solution)/shard_map/ppermute | solution.py:485
  32.7 3.3 %collective-permute-start.11 = (bf16[1024,128]{1,0:T(8,128)(2,1)}, bf16[1024,128]{1,0:T(8,128)(2,1)S(1)}, u32[]{:S(2)}, u32[]{:S(2)}) collective-permute-start(bf16[1024,128]{1,0:T(8,128)(2,1)} %get-tuple-element.68), channel_id=1, source_target_pairs={{0,12},{4,8},{8,4},{12,0},{16,28},{20,24},{24,20},{28,16},{1,13},{... | collective-permute-start | bytes 786440 | tf_op jit(solution)/shard_map/ppermute | solution.py:485
  36.0 1.0 collective-permute-done.8.refs_2_.refs_10_
  37.0 2.0 %collective-permute-start.13 = (bf16[1024,128]{1,0:T(8,128)(2,1)}, bf16[1024,128]{1,0:T(8,128)(2,1)S(1)}, u32[]{:S(2)}, u32[]{:S(2)}) collective-permute-start(bf16[1024,128]{1,0:T(8,128)(2,1)} %get-tuple-element.70), channel_id=1, source_target_pairs={{0,28},{4,24},{8,20},{12,16},{16,12},{20,8},{24,4},{28,0},{1,29},{... | collective-permute-start | bytes 786440 | tf_op jit(solution)/shard_map/ppermute | solution.py:485
  39.0 12.7 %score.1 = (bf16[8,2048,512]{2,1,0:T(8,128)(2,1)}, f32[8,1,512]{2,1,0:T(1,128)}, s32[3]{0:T(128)}) custom-call(s32[1]{0:T(128)} %bitcast.rank_ref, bf16[1040,128]{1,0:T(8,128)(2,1)} %get-tuple-element.50.refs_0_, bf16[1040,128]{1,0:T(8,128)(2,1)} %copy-done.1, bf16[1040,128]{1,0:T(8,128)(2,1)} %copy-done.2, bf16[1040,128]{1,0:T(8,128)(2,1)} %copy-done.3, ...), custom_call_target="tpu_custom_call" | custom-call | tf_op jit(solution)/shard_map/score/pallas_call | solution.py:513
  51.8 2.6 %collective-permute-done.12.refs_6_.refs_14_ = bf16[1024,128]{1,0:T(8,128)(2,1)S(1)} collective-permute-done((bf16[1024,128]{1,0:T(8,128)(2,1)}, bf16[1024,128]{1,0:T(8,128)(2,1)S(1)}, u32[]{:S(2)}, u32[]{:S(2)}) %collective-permute-start.12) | collective-permute-done | bytes 262176 | tf_op jit(solution)/shard_map/ppermute | solution.py:485
  55.1 0.4 copy-done.14
  55.5 9.3 %attend.1 = (f32[8,128,512]{2,1,0:T(8,128)}, bf16[8,512,128]{2,1,0:T(8,128)(2,1)}, f32[2,4096]{1,0:T(2,128)}) custom-call(s32[1]{0:T(128)} %bitcast.rank_ref, s32[3]{0:T(128)} %get-tuple-element.60.bounds, bf16[1024,128]{1,0:T(8,128)(2,1)} %get-tuple-element.63.refs_0_.refs_8_, bf16[1024,128]{1,0:T(8,128)(2,1)} %copy-done.8, bf16[1024,128]{1,0:T(8,128)(2,1)} %copy-done.9, ...), custom_call_target="tpu_custom_call" | custom-call | tf_op jit(solution)/shard_map/attend/pallas_call | solution.py:537
  64.8 0.8 collective-permute-start.14
  65.6 1.1 collective-permute-done.14
  66.7 0.8 add.21
  67.4 3.6 %collective-permute-start.17 = (f32[2,4096]{1,0:T(2,128)S(1)}, f32[2,4096]{1,0:T(2,128)S(1)}, u32[]{:S(2)}, u32[]{:S(2)}) collective-permute-start(f32[2,4096]{1,0:T(2,128)S(1)} %add.21), channel_id=1, source_target_pairs={{0,24},{4,28},{8,16},{12,20},{16,8},{20,12},{24,0},{28,4},{1,25},{... | collective-permute-start | bytes 98312 | tf_op jit(solution)/shard_map/ppermute | solution.py:485
  71.0 0.8 collective-permute-start.15
  71.8 1.1 collective-permute-done.17
  72.9 2.0 %collective-permute-done.16 = f32[2,4096]{1,0:T(2,128)S(1)} collective-permute-done((f32[2,4096]{1,0:T(2,128)S(1)}, f32[2,4096]{1,0:T(2,128)S(1)}, u32[]{:S(2)}, u32[]{:S(2)}) %collective-permute-start.16) | collective-permute-done | bytes 32800 | tf_op jit(solution)/shard_map/ppermute | solution.py:485
  74.9 3.7 %collective-permute-start.20 = (f32[2,4096]{1,0:T(2,128)S(1)}, f32[2,4096]{1,0:T(2,128)S(1)}, u32[]{:S(2)}, u32[]{:S(2)}) collective-permute-start(f32[2,4096]{1,0:T(2,128)S(1)} %add_add_fusion.1), channel_id=1, source_target_pairs={{0,3},{1,0},{2,1},{3,2},{4,7},{5,4},{6,5},{7,6},{8,11},{9,8},{10,9... | collective-permute-start | bytes 98312 | tf_op jit(solution)/shard_map/ppermute | solution.py:501
  78.6 1.0 collective-permute-start.18
  79.6 3.7 %all-to-all-start = ((bf16[8,512,128]{2,1,0:T(8,128)(2,1)}), bf16[8,512,128]{2,1,0:T(8,128)(2,1)S(1)}, u32[]{:S(2)}, u32[]{:S(2)}) async-start(bf16[8,512,128]{2,1,0:T(8,128)(2,1)} %get-tuple-element.74), calls=%async_computation | async-start | bytes 2097152 | tf_op jit(solution)/shard_map/all_to_all | solution.py:493
  83.4 0.9 collective-permute-done.18
  84.3 0.6 add_add_fusion.refs_19_.stats_ref
  85.0 20.4 %backward.1 = (bf16[1536,128]{1,0:T(8,128)(2,1)}, bf16[1536,128]{1,0:T(8,128)(2,1)}, bf16[1536,128]{1,0:T(8,128)(2,1)}, bf16[1536,128]{1,0:T(8,128)(2,1)}, bf16[...) custom-call(s32[1]{0:T(128)} %bitcast.rank_ref, ...), custom_call_target="tpu_custom_call" | custom-call | tf_op jit(solution)/shard_map/backward/pallas_call | solution.py:564
  105.4 1.0 collective-permute-start.22
  106.5 1.9 %collective-permute-start.23 = (bf16[1536,128]{1,0:T(8,128)(2,1)}, bf16[1536,128]{1,0:T(8,128)(2,1)S(1)}, u32[]{:S(2)}, u32[]{:S(2)}) collective-permute-start(bf16[1536,128]{1,0:T(8,128)(2,1)} %get-tuple-element.88), channel_id=1, source_target_pairs={{0,16},{4,20},{8,24},{12,28},{16,0},{20,4},{24,8},{28,12},{1,17},{... | collective-permute-start | bytes 1179656 | tf_op jit(solution)/shard_map/ppermute | solution.py:485
  108.3 0.7 collective-permute-start.24
  109.3 2.3 %collective-permute-start.26 = (bf16[1536,128]{1,0:T(8,128)(2,1)}, bf16[1536,128]{1,0:T(8,128)(2,1)S(1)}, u32[]{:S(2)}, u32[]{:S(2)}) collective-permute-start(bf16[1536,128]{1,0:T(8,128)(2,1)} %get-tuple-element.91), channel_id=1, source_target_pairs={{0,20},{4,16},{8,28},{12,24},{16,4},{20,0},{24,12},{28,8},{1,21},{... | collective-permute-start | bytes 1179656 | tf_op jit(solution)/shard_map/ppermute | solution.py:485
  111.5 6.1 %collective-permute-done.22.refs_2_ = bf16[1536,128]{1,0:T(8,128)(2,1)S(1)} collective-permute-done((bf16[1536,128]{1,0:T(8,128)(2,1)}, bf16[1536,128]{1,0:T(8,128)(2,1)S(1)}, u32[]{:S(2)}, u32[]{:S(2)}) %collective-permute-start.22) | collective-permute-done | bytes 393248 | tf_op jit(solution)/shard_map/ppermute | solution.py:485
  117.6 1.1 collective-permute-start.27
  118.7 2.5 %normed.1 = bf16[512,1024]{1,0:T(8,128)(2,1)} custom-call(s32[1]{0:T(128)} %bitcast.rank_ref, f32[2,4096]{1,0:T(2,128)} %add_add_fusion.refs_19_.stats_ref, bf16[8,512,128]{2,1,0:T(8,128)(2,1)} %copy-done), custom_call_target="tpu_custom_call" | custom-call | tf_op jit(solution)/shard_map/normed/pallas_call | solution.py:635
  121.2 5.3 %collective-permute-done.23.refs_3_ = bf16[1536,128]{1,0:T(8,128)(2,1)S(1)} collective-permute-done((bf16[1536,128]{1,0:T(8,128)(2,1)}, bf16[1536,128]{1,0:T(8,128)(2,1)S(1)}, u32[]{:S(2)}, u32[]{:S(2)}) %collective-permute-start.23) | collective-permute-done | bytes 393248 | tf_op jit(solution)/shard_map/ppermute | solution.py:485
  126.5 1.0 collective-permute-done.24.refs_4_
  127.5 6.1 %collective-permute-done.25.refs_5_ = bf16[1536,128]{1,0:T(8,128)(2,1)S(1)} collective-permute-done((bf16[1536,128]{1,0:T(8,128)(2,1)}, bf16[1536,128]{1,0:T(8,128)(2,1)S(1)}, u32[]{:S(2)}, u32[]{:S(2)}) %collective-permute-start.25) | collective-permute-done | bytes 393248 | tf_op jit(solution)/shard_map/ppermute | solution.py:485
  133.6 9.0 %collective-permute-done.26.refs_6_ = bf16[1536,128]{1,0:T(8,128)(2,1)S(1)} collective-permute-done((bf16[1536,128]{1,0:T(8,128)(2,1)}, bf16[1536,128]{1,0:T(8,128)(2,1)S(1)}, u32[]{:S(2)}, u32[]{:S(2)}) %collective-permute-start.26) | collective-permute-done | bytes 393248 | tf_op jit(solution)/shard_map/ppermute | solution.py:485
  142.6 0.9 collective-permute-done.27.refs_7_
  143.5 0.7 copy-done.21
  144.3 3.2 %unpack.1 = (bf16[512,1024]{1,0:T(8,128)(2,1)}, bf16[512,1024]{1,0:T(8,128)(2,1)}, bf16[512,1024]{1,0:T(8,128)(2,1)}) custom-call(s32[1]{0:T(128)} %bitcast.rank_ref, bf16[1536,128]{1,0:T(8,128)(2,1)} %get-tuple-element.85.refs_0_, bf16[1536,128]{1,0:T(8,128)(2,1)} %copy-done.15, bf16[1536,128]{1,0:T(8,128)(2,1)} %copy-done.16, ...), custom_call_target="tpu_custom_call" | custom-call | tf_op jit(solution)/shard_map/unpack/pallas_call | solution.py:644
  (64 shorter events, 1.3 us)
Async XLA Ops:
  3.9 5.8 %collective-permute-start = (bf16[1040,128]{1,0:T(8,128)(2,1)}, bf16[1040,128]{1,0:T(8,128)(2,1)S(1)}, u32[]{:S(2)}, u32[]{:S(2)}) collective-permute-start(bf16[1040,128]{1,0:T(8,128)(2,1)} %get-tuple-element.51), channel_id=1, source_target_pairs={{0,4},{4,0},{8,12},{12,8},{16,20},{20,16},{24,28},{28,24},{1,5},{5... | collective-permute-start | bytes 798728 | tf_op jit(solution)/shard_map/ppermute | solution.py:485
  4.4 10.0 %collective-permute-start.1 = (bf16[1040,128]{1,0:T(8,128)(2,1)}, bf16[1040,128]{1,0:T(8,128)(2,1)S(1)}, u32[]{:S(2)}, u32[]{:S(2)}) collective-permute-start(bf16[1040,128]{1,0:T(8,128)(2,1)} %get-tuple-element.52), channel_id=1, source_target_pairs={{0,8},{4,12},{8,0},{12,4},{16,24},{20,28},{24,16},{28,20},{1,9},{5... | collective-permute-start | bytes 798728 | tf_op jit(solution)/shard_map/ppermute | solution.py:485
  7.0 15.2 %collective-permute-start.2 = (bf16[1040,128]{1,0:T(8,128)(2,1)}, bf16[1040,128]{1,0:T(8,128)(2,1)S(1)}, u32[]{:S(2)}, u32[]{:S(2)}) collective-permute-start(bf16[1040,128]{1,0:T(8,128)(2,1)} %get-tuple-element.55), channel_id=1, source_target_pairs={{0,16},{4,20},{8,24},{12,28},{16,0},{20,4},{24,8},{28,12},{1,17},{... | collective-permute-start | bytes 798728 | tf_op jit(solution)/shard_map/ppermute | solution.py:485
  8.5 13.6 %collective-permute-start.3 = (bf16[1040,128]{1,0:T(8,128)(2,1)}, bf16[1040,128]{1,0:T(8,128)(2,1)S(1)}, u32[]{:S(2)}, u32[]{:S(2)}) collective-permute-start(bf16[1040,128]{1,0:T(8,128)(2,1)} %get-tuple-element.56), channel_id=1, source_target_pairs={{0,24},{4,28},{8,16},{12,20},{16,8},{20,12},{24,0},{28,4},{1,25},{... | collective-permute-start | bytes 798728 | tf_op jit(solution)/shard_map/ppermute | solution.py:485
  8.5 16.9 %collective-permute-start.4 = (bf16[1040,128]{1,0:T(8,128)(2,1)}, bf16[1040,128]{1,0:T(8,128)(2,1)S(1)}, u32[]{:S(2)}, u32[]{:S(2)}) collective-permute-start(bf16[1040,128]{1,0:T(8,128)(2,1)} %get-tuple-element.57), channel_id=1, source_target_pairs={{0,12},{4,8},{8,4},{12,0},{16,28},{20,24},{24,20},{28,16},{1,13},{... | collective-permute-start | bytes 798728 | tf_op jit(solution)/shard_map/ppermute | solution.py:485
  9.7 29.3 %copy-start.1 = (bf16[1040,128]{1,0:T(8,128)(2,1)}, bf16[1040,128]{1,0:T(8,128)(2,1)S(1)}, u32[]{:S(2)}) copy-start(bf16[1040,128]{1,0:T(8,128)(2,1)S(1)} %collective-permute-done.refs_1_) | copy-start | bytes 798724
  9.7 23.0 %collective-permute-start.5 = (bf16[1040,128]{1,0:T(8,128)(2,1)}, bf16[1040,128]{1,0:T(8,128)(2,1)S(1)}, u32[]{:S(2)}, u32[]{:S(2)}) collective-permute-start(bf16[1040,128]{1,0:T(8,128)(2,1)} %get-tuple-element.58), channel_id=1, source_target_pairs={{0,20},{4,16},{8,28},{12,24},{16,4},{20,0},{24,12},{28,8},{1,21},{... | collective-permute-start | bytes 798728 | tf_op jit(solution)/shard_map/ppermute | solution.py:485
  14.4 24.6 %copy-start.2 = (bf16[1040,128]{1,0:T(8,128)(2,1)}, bf16[1040,128]{1,0:T(8,128)(2,1)S(1)}, u32[]{:S(2)}) copy-start(bf16[1040,128]{1,0:T(8,128)(2,1)S(1)} %collective-permute-done.1.refs_2_) | copy-start | bytes 798724
  14.4 18.3 %collective-permute-start.6 = (bf16[1040,128]{1,0:T(8,128)(2,1)}, bf16[1040,128]{1,0:T(8,128)(2,1)S(1)}, u32[]{:S(2)}, u32[]{:S(2)}) collective-permute-start(bf16[1040,128]{1,0:T(8,128)(2,1)} %get-tuple-element.59), channel_id=1, source_target_pairs={{0,28},{4,24},{8,20},{12,16},{16,12},{20,8},{24,4},{28,0},{1,29},{... | collective-permute-start | bytes 798728 | tf_op jit(solution)/shard_map/ppermute | solution.py:485
  22.1 16.9 %copy-start.3 = (bf16[1040,128]{1,0:T(8,128)(2,1)}, bf16[1040,128]{1,0:T(8,128)(2,1)S(1)}, u32[]{:S(2)}) copy-start(bf16[1040,128]{1,0:T(8,128)(2,1)S(1)} %collective-permute-done.2.refs_3_) | copy-start | bytes 798724
  22.1 13.8 %collective-permute-start.7 = (bf16[1024,128]{1,0:T(8,128)(2,1)}, bf16[1024,128]{1,0:T(8,128)(2,1)S(1)}, u32[]{:S(2)}, u32[]{:S(2)}) collective-permute-start(bf16[1024,128]{1,0:T(8,128)(2,1)} %get-tuple-element.64), channel_id=1, source_target_pairs={{0,4},{4,0},{8,12},{12,8},{16,20},{20,16},{24,28},{28,24},{1,5},{5... | collective-permute-start | bytes 786440 | tf_op jit(solution)/shard_map/ppermute | solution.py:485
  22.1 16.8 %copy-start.4 = (bf16[1040,128]{1,0:T(8,128)(2,1)}, bf16[1040,128]{1,0:T(8,128)(2,1)S(1)}, u32[]{:S(2)}) copy-start(bf16[1040,128]{1,0:T(8,128)(2,1)S(1)} %collective-permute-done.3.refs_4_) | copy-start | bytes 798724
  22.1 14.8 %collective-permute-start.8 = (bf16[1024,128]{1,0:T(8,128)(2,1)}, bf16[1024,128]{1,0:T(8,128)(2,1)S(1)}, u32[]{:S(2)}, u32[]{:S(2)}) collective-permute-start(bf16[1024,128]{1,0:T(8,128)(2,1)} %get-tuple-element.65), channel_id=1, source_target_pairs={{0,8},{4,12},{8,0},{12,4},{16,24},{20,28},{24,16},{28,20},{1,9},{5... | collective-permute-start | bytes 786440 | tf_op jit(solution)/shard_map/ppermute | solution.py:485
  25.5 13.5 %copy-start.5 = (bf16[1040,128]{1,0:T(8,128)(2,1)}, bf16[1040,128]{1,0:T(8,128)(2,1)S(1)}, u32[]{:S(2)}) copy-start(bf16[1040,128]{1,0:T(8,128)(2,1)S(1)} %collective-permute-done.4.refs_5_) | copy-start | bytes 798724
  25.5 26.2 %collective-permute-start.9 = (bf16[1024,128]{1,0:T(8,128)(2,1)}, bf16[1024,128]{1,0:T(8,128)(2,1)S(1)}, u32[]{:S(2)}, u32[]{:S(2)}) collective-permute-start(bf16[1024,128]{1,0:T(8,128)(2,1)} %get-tuple-element.66), channel_id=1, source_target_pairs={{0,16},{4,20},{8,24},{12,28},{16,0},{20,4},{24,8},{28,12},{1,17},{... | collective-permute-start | bytes 786440 | tf_op jit(solution)/shard_map/ppermute | solution.py:485
  32.7 6.3 %copy-start.6 = (bf16[1040,128]{1,0:T(8,128)(2,1)}, bf16[1040,128]{1,0:T(8,128)(2,1)S(1)}, u32[]{:S(2)}) copy-start(bf16[1040,128]{1,0:T(8,128)(2,1)S(1)} %collective-permute-done.5.refs_6_) | copy-start | bytes 798724
  32.7 19.0 %collective-permute-start.10 = (bf16[1024,128]{1,0:T(8,128)(2,1)}, bf16[1024,128]{1,0:T(8,128)(2,1)S(1)}, u32[]{:S(2)}, u32[]{:S(2)}) collective-permute-start(bf16[1024,128]{1,0:T(8,128)(2,1)} %get-tuple-element.67), channel_id=1, source_target_pairs={{0,24},{4,28},{8,16},{12,20},{16,8},{20,12},{24,0},{28,4},{1,25},{... | collective-permute-start | bytes 786440 | tf_op jit(solution)/shard_map/ppermute | solution.py:485
  32.7 6.3 %copy-start.7 = (bf16[1040,128]{1,0:T(8,128)(2,1)}, bf16[1040,128]{1,0:T(8,128)(2,1)S(1)}, u32[]{:S(2)}) copy-start(bf16[1040,128]{1,0:T(8,128)(2,1)S(1)} %collective-permute-done.6.refs_7_) | copy-start | bytes 798724
  32.7 19.0 %collective-permute-start.11 = (bf16[1024,128]{1,0:T(8,128)(2,1)}, bf16[1024,128]{1,0:T(8,128)(2,1)S(1)}, u32[]{:S(2)}, u32[]{:S(2)}) collective-permute-start(bf16[1024,128]{1,0:T(8,128)(2,1)} %get-tuple-element.68), channel_id=1, source_target_pairs={{0,12},{4,8},{8,4},{12,0},{16,28},{20,24},{24,20},{28,16},{1,13},{... | collective-permute-start | bytes 786440 | tf_op jit(solution)/shard_map/ppermute | solution.py:485
  36.0 18.8 %copy-start.8 = (bf16[1024,128]{1,0:T(8,128)(2,1)}, bf16[1024,128]{1,0:T(8,128)(2,1)S(1)}, u32[]{:S(2)}) copy-start(bf16[1024,128]{1,0:T(8,128)(2,1)S(1)} %collective-permute-done.7.refs_1_.refs_9_) | copy-start | bytes 786436
  36.0 18.4 %collective-permute-start.12 = (bf16[1024,128]{1,0:T(8,128)(2,1)}, bf16[1024,128]{1,0:T(8,128)(2,1)S(1)}, u32[]{:S(2)}, u32[]{:S(2)}) collective-permute-start(bf16[1024,128]{1,0:T(8,128)(2,1)} %get-tuple-element.69), channel_id=1, source_target_pairs={{0,20},{4,16},{8,28},{12,24},{16,4},{20,0},{24,12},{28,8},{1,21},{... | collective-permute-start | bytes 786440 | tf_op jit(solution)/shard_map/ppermute | solution.py:485
  37.0 17.8 %copy-start.9 = (bf16[1024,128]{1,0:T(8,128)(2,1)}, bf16[1024,128]{1,0:T(8,128)(2,1)S(1)}, u32[]{:S(2)}) copy-start(bf16[1024,128]{1,0:T(8,128)(2,1)S(1)} %collective-permute-done.8.refs_2_.refs_10_) | copy-start | bytes 786436
  37.0 17.8 %collective-permute-start.13 = (bf16[1024,128]{1,0:T(8,128)(2,1)}, bf16[1024,128]{1,0:T(8,128)(2,1)S(1)}, u32[]{:S(2)}, u32[]{:S(2)}) collective-permute-start(bf16[1024,128]{1,0:T(8,128)(2,1)} %get-tuple-element.70), channel_id=1, source_target_pairs={{0,28},{4,24},{8,20},{12,16},{16,12},{20,8},{24,4},{28,0},{1,29},{... | collective-permute-start | bytes 786440 | tf_op jit(solution)/shard_map/ppermute | solution.py:485
  51.7 3.1 %copy-start.10 = (bf16[1024,128]{1,0:T(8,128)(2,1)}, bf16[1024,128]{1,0:T(8,128)(2,1)S(1)}, u32[]{:S(2)}) copy-start(bf16[1024,128]{1,0:T(8,128)(2,1)S(1)} %collective-permute-done.9.refs_3_.refs_11_) | copy-start | bytes 786436
  51.7 3.0 %copy-start.11 = (bf16[1024,128]{1,0:T(8,128)(2,1)}, bf16[1024,128]{1,0:T(8,128)(2,1)S(1)}, u32[]{:S(2)}) copy-start(bf16[1024,128]{1,0:T(8,128)(2,1)S(1)} %collective-permute-done.10.refs_4_.refs_12_) | copy-start | bytes 786436
  51.7 3.0 %copy-start.12 = (bf16[1024,128]{1,0:T(8,128)(2,1)}, bf16[1024,128]{1,0:T(8,128)(2,1)S(1)}, u32[]{:S(2)}) copy-start(bf16[1024,128]{1,0:T(8,128)(2,1)S(1)} %collective-permute-done.11.refs_5_.refs_13_) | copy-start | bytes 786436
  64.8 1.9 %collective-permute-start.14 = (f32[2,4096]{1,0:T(2,128)}, f32[2,4096]{1,0:T(2,128)S(1)}, u32[]{:S(2)}, u32[]{:S(2)}) collective-permute-start(f32[2,4096]{1,0:T(2,128)} %get-tuple-element.73), channel_id=1, source_target_pairs={{0,4},{4,0},{8,12},{12,8},{16,20},{20,16},{24,28},{28,24},{1,5},{5... | collective-permute-start | bytes 98312 | tf_op jit(solution)/shard_map/ppermute | solution.py:485
  67.4 5.5 %collective-permute-start.17 = (f32[2,4096]{1,0:T(2,128)S(1)}, f32[2,4096]{1,0:T(2,128)S(1)}, u32[]{:S(2)}, u32[]{:S(2)}) collective-permute-start(f32[2,4096]{1,0:T(2,128)S(1)} %add.21), channel_id=1, source_target_pairs={{0,24},{4,28},{8,16},{12,20},{16,8},{20,12},{24,0},{28,4},{1,25},{... | collective-permute-start | bytes 98312 | tf_op jit(solution)/shard_map/ppermute | solution.py:485
  71.0 3.9 %collective-permute-start.16 = (f32[2,4096]{1,0:T(2,128)S(1)}, f32[2,4096]{1,0:T(2,128)S(1)}, u32[]{:S(2)}, u32[]{:S(2)}) collective-permute-start(f32[2,4096]{1,0:T(2,128)S(1)} %add.21), channel_id=1, source_target_pairs={{0,16},{4,20},{8,24},{12,28},{16,0},{20,4},{24,8},{28,12},{1,17},{... | collective-permute-start | bytes 98312 | tf_op jit(solution)/shard_map/ppermute | solution.py:485
  71.0 3.9 %collective-permute-start.15 = (f32[2,4096]{1,0:T(2,128)S(1)}, f32[2,4096]{1,0:T(2,128)S(1)}, u32[]{:S(2)}, u32[]{:S(2)}) collective-permute-start(f32[2,4096]{1,0:T(2,128)S(1)} %add.21), channel_id=1, source_target_pairs={{0,8},{4,12},{8,0},{12,4},{16,24},{20,28},{24,16},{28,20},{1,9},{5... | collective-permute-start | bytes 98312 | tf_op jit(solution)/shard_map/ppermute | solution.py:485
  74.9 8.4 %collective-permute-start.20 = (f32[2,4096]{1,0:T(2,128)S(1)}, f32[2,4096]{1,0:T(2,128)S(1)}, u32[]{:S(2)}, u32[]{:S(2)}) collective-permute-start(f32[2,4096]{1,0:T(2,128)S(1)} %add_add_fusion.1), channel_id=1, source_target_pairs={{0,3},{1,0},{2,1},{3,2},{4,7},{5,4},{6,5},{7,6},{8,11},{9,8},{10,9... | collective-permute-start | bytes 98312 | tf_op jit(solution)/shard_map/ppermute | solution.py:501
  78.6 4.8 %collective-permute-start.19 = (f32[2,4096]{1,0:T(2,128)S(1)}, f32[2,4096]{1,0:T(2,128)S(1)}, u32[]{:S(2)}, u32[]{:S(2)}) collective-permute-start(f32[2,4096]{1,0:T(2,128)S(1)} %add_add_fusion.1), channel_id=1, source_target_pairs={{0,2},{1,3},{2,0},{3,1},{4,6},{5,7},{6,4},{7,5},{8,10},{9,11},{10,... | collective-permute-start | bytes 98312 | tf_op jit(solution)/shard_map/ppermute | solution.py:501
  78.6 5.7 %collective-permute-start.18 = (f32[2,4096]{1,0:T(2,128)S(1)}, f32[2,4096]{1,0:T(2,128)S(1)}, u32[]{:S(2)}, u32[]{:S(2)}) collective-permute-start(f32[2,4096]{1,0:T(2,128)S(1)} %add_add_fusion.1), channel_id=1, source_target_pairs={{0,1},{1,2},{2,3},{3,0},{4,5},{5,6},{6,7},{7,4},{8,9},{9,10},{10,1... | collective-permute-start | bytes 98312 | tf_op jit(solution)/shard_map/ppermute | solution.py:501
  79.6 25.7 %all-to-all-start = ((bf16[8,512,128]{2,1,0:T(8,128)(2,1)}), bf16[8,512,128]{2,1,0:T(8,128)(2,1)S(1)}, u32[]{:S(2)}, u32[]{:S(2)}) async-start(bf16[8,512,128]{2,1,0:T(8,128)(2,1)} %get-tuple-element.74), calls=%async_computation | async-start | bytes 2097152 | tf_op jit(solution)/shard_map/all_to_all | solution.py:493
  105.4 13.3 %copy-start = (bf16[8,512,128]{2,1,0:T(8,128)(2,1)}, bf16[8,512,128]{2,1,0:T(8,128)(2,1)S(1)}, u32[]{:S(2)}) copy-start(bf16[8,512,128]{2,1,0:T(8,128)(2,1)S(1)} %all-to-all-done.home_ref) | copy-start | bytes 3145732
  105.4 3.9 %collective-permute-start.21 = (bf16[1536,128]{1,0:T(8,128)(2,1)}, bf16[1536,128]{1,0:T(8,128)(2,1)S(1)}, u32[]{:S(2)}, u32[]{:S(2)}) collective-permute-start(bf16[1536,128]{1,0:T(8,128)(2,1)} %get-tuple-element.86), channel_id=1, source_target_pairs={{0,4},{4,0},{8,12},{12,8},{16,20},{20,16},{24,28},{28,24},{1,5},{5... | collective-permute-start | bytes 1179656 | tf_op jit(solution)/shard_map/ppermute | solution.py:485
  105.4 12.2 %collective-permute-start.22 = (bf16[1536,128]{1,0:T(8,128)(2,1)}, bf16[1536,128]{1,0:T(8,128)(2,1)S(1)}, u32[]{:S(2)}, u32[]{:S(2)}) collective-permute-start(bf16[1536,128]{1,0:T(8,128)(2,1)} %get-tuple-element.87), channel_id=1, source_target_pairs={{0,8},{4,12},{8,0},{12,4},{16,24},{20,28},{24,16},{28,20},{1,9},{5... | collective-permute-start | bytes 1179656 | tf_op jit(solution)/shard_map/ppermute | solution.py:485
  106.5 20.1 %collective-permute-start.23 = (bf16[1536,128]{1,0:T(8,128)(2,1)}, bf16[1536,128]{1,0:T(8,128)(2,1)S(1)}, u32[]{:S(2)}, u32[]{:S(2)}) collective-permute-start(bf16[1536,128]{1,0:T(8,128)(2,1)} %get-tuple-element.88), channel_id=1, source_target_pairs={{0,16},{4,20},{8,24},{12,28},{16,0},{20,4},{24,8},{28,12},{1,17},{... | collective-permute-start | bytes 1179656 | tf_op jit(solution)/shard_map/ppermute | solution.py:485
  108.3 19.2 %collective-permute-start.24 = (bf16[1536,128]{1,0:T(8,128)(2,1)}, bf16[1536,128]{1,0:T(8,128)(2,1)S(1)}, u32[]{:S(2)}, u32[]{:S(2)}) collective-permute-start(bf16[1536,128]{1,0:T(8,128)(2,1)} %get-tuple-element.89), channel_id=1, source_target_pairs={{0,24},{4,28},{8,16},{12,20},{16,8},{20,12},{24,0},{28,4},{1,25},{... | collective-permute-start | bytes 1179656 | tf_op jit(solution)/shard_map/ppermute | solution.py:485
  109.0 24.6 %collective-permute-start.25 = (bf16[1536,128]{1,0:T(8,128)(2,1)}, bf16[1536,128]{1,0:T(8,128)(2,1)S(1)}, u32[]{:S(2)}, u32[]{:S(2)}) collective-permute-start(bf16[1536,128]{1,0:T(8,128)(2,1)} %get-tuple-element.90), channel_id=1, source_target_pairs={{0,12},{4,8},{8,4},{12,0},{16,28},{20,24},{24,20},{28,16},{1,13},{... | collective-permute-start | bytes 1179656 | tf_op jit(solution)/shard_map/ppermute | solution.py:485
  109.3 34.2 %copy-start.15 = (bf16[1536,128]{1,0:T(8,128)(2,1)}, bf16[1536,128]{1,0:T(8,128)(2,1)S(1)}, u32[]{:S(2)}) copy-start(bf16[1536,128]{1,0:T(8,128)(2,1)S(1)} %collective-permute-done.21.refs_1_) | copy-start | bytes 1179652
  109.3 33.3 %collective-permute-start.26 = (bf16[1536,128]{1,0:T(8,128)(2,1)}, bf16[1536,128]{1,0:T(8,128)(2,1)S(1)}, u32[]{:S(2)}, u32[]{:S(2)}) collective-permute-start(bf16[1536,128]{1,0:T(8,128)(2,1)} %get-tuple-element.91), channel_id=1, source_target_pairs={{0,20},{4,16},{8,28},{12,24},{16,4},{20,0},{24,12},{28,8},{1,21},{... | collective-permute-start | bytes 1179656 | tf_op jit(solution)/shard_map/ppermute | solution.py:485
  117.6 25.9 %copy-start.16 = (bf16[1536,128]{1,0:T(8,128)(2,1)}, bf16[1536,128]{1,0:T(8,128)(2,1)S(1)}, u32[]{:S(2)}) copy-start(bf16[1536,128]{1,0:T(8,128)(2,1)S(1)} %collective-permute-done.22.refs_2_) | copy-start | bytes 1179652
  117.6 25.8 %collective-permute-start.27 = (bf16[1536,128]{1,0:T(8,128)(2,1)}, bf16[1536,128]{1,0:T(8,128)(2,1)S(1)}, u32[]{:S(2)}, u32[]{:S(2)}) collective-permute-start(bf16[1536,128]{1,0:T(8,128)(2,1)} %get-tuple-element.92), channel_id=1, source_target_pairs={{0,28},{4,24},{8,20},{12,16},{16,12},{20,8},{24,4},{28,0},{1,29},{... | collective-permute-start | bytes 1179656 | tf_op jit(solution)/shard_map/ppermute | solution.py:485
  126.5 16.9 %copy-start.17 = (bf16[1536,128]{1,0:T(8,128)(2,1)}, bf16[1536,128]{1,0:T(8,128)(2,1)S(1)}, u32[]{:S(2)}) copy-start(bf16[1536,128]{1,0:T(8,128)(2,1)S(1)} %collective-permute-done.23.refs_3_) | copy-start | bytes 1179652
  127.5 16.0 %copy-start.18 = (bf16[1536,128]{1,0:T(8,128)(2,1)}, bf16[1536,128]{1,0:T(8,128)(2,1)S(1)}, u32[]{:S(2)}) copy-start(bf16[1536,128]{1,0:T(8,128)(2,1)S(1)} %collective-permute-done.24.refs_4_) | copy-start | bytes 1179652
  133.6 9.9 %copy-start.19 = (bf16[1536,128]{1,0:T(8,128)(2,1)}, bf16[1536,128]{1,0:T(8,128)(2,1)S(1)}, u32[]{:S(2)}) copy-start(bf16[1536,128]{1,0:T(8,128)(2,1)S(1)} %collective-permute-done.25.refs_5_) | copy-start | bytes 1179652
  142.6 0.9 copy-start.20
  (3 other events, 2.2 us)
